TPU v7x, 32 devices: a whole 2x2x4 slice. The times are simulated.
32 devices in a mesh: clip: 2 (over core), row: 4 (over y, x), col: 4 (over z).
Axes of the slice: x: 2, y: 2, z: 4, core: 2. Of those that a mesh axis runs over, the one named last changes fastest.
Arguments:
- video: bfloat16 [2, 8, 64, 64, 128], P('clip', None, 'row', 'col'), may hold values from -6 to 6
- frame_counts: int32 [2], P('clip'), may hold values from 2 to 8, as said below
- kernel_main: bfloat16 [3, 3, 3, 128, 128], replicated, may hold values from -0.109375 to 0.109375
- kernel_down: bfloat16 [3, 3, 128, 128], replicated, may hold values from -0.1875 to 0.1875
- latent_grad: bfloat16 [2, 8, 32, 32, 128], P('clip', None, 'row', 'col'), may hold values from -6 to 6
Outputs:
- latent: bfloat16 [2, 8, 32, 32, 128], P('clip', None, 'row', 'col')
- video_grad: bfloat16 [2, 8, 64, 64, 128], P('clip', None, 'row', 'col')
- main_grad: float32 [3, 3, 3, 128, 128], replicated
- down_grad: float32 [3, 3, 128, 128], replicated
Inputs may be any that keep to these rules, and one draw needn't show every extreme that they name: `frame_counts`: some clip has all 8 frames in every draw.
All inputs are finite; a program needn't handle non-finite values.
Results may differ from a plain program's by a relative error of at most 0.005.
Values may be sent and summed in bfloat16 or wider, within the bound.
No kernel may reach another device: no remote copies, remote signals or barrier semaphores. Data moves between devices by JAX's collectives and lax.ppermute only.
A program may use at most 64 MiB of HBM per device.

v0:
```python
import jax
import jax.numpy as jnp
from jax import lax
from jax.experimental import pallas as pl
from jax.experimental.pallas import tpu as pltpu
from jax.sharding import PartitionSpec as P

BF = jnp.bfloat16
F32 = jnp.float32


def flip(axis, mask):
    return [(i, i ^ mask) for i in range(lax.axis_size(axis))]


def part(x, index, size):
    return lax.dynamic_slice_in_dim(x, index * size, size, axis=0)


def exchange(low_edge, high_edge, axis):
    count = lax.axis_size(axis)
    up = lax.ppermute(high_edge, axis, [(i, i + 1) for i in range(count - 1)])
    down = lax.ppermute(low_edge, axis, [(i + 1, i) for i in range(count - 1)])
    return up, down


def pack(a, b):
    return jnp.concatenate([a.reshape(-1, a.shape[-1]), b.reshape(-1, b.shape[-1])])


def unpack(buffer, a_shape, b_shape):
    rows = a_shape[0] * a_shape[1] * a_shape[2]
    return buffer[:rows].reshape(a_shape), buffer[rows:].reshape(b_shape)


def with_halo(video, grad):
    for axis, dim in (("row", 1), ("col", 2)):
        size, gsize = video.shape[dim], grad.shape[dim]
        v_low = lax.slice_in_dim(video, 0, 2, axis=dim)
        v_high = lax.slice_in_dim(video, size - 2, size, axis=dim)
        g_low = lax.slice_in_dim(grad, 0, 1, axis=dim)
        g_high = lax.slice_in_dim(grad, gsize - 1, gsize, axis=dim)
        before, after = exchange(pack(v_low, g_low), pack(v_high, g_high), axis)
        v_before, g_before = unpack(before, v_low.shape, g_low.shape)
        v_after, g_after = unpack(after, v_low.shape, g_low.shape)
        video = jnp.concatenate([v_before, video, v_after], axis=dim)
        grad = jnp.concatenate([g_before, grad, g_after], axis=dim)
    return video, grad


def direct_scatter(x, axis, beside):
    count, mine = lax.axis_size(axis), lax.axis_index(axis)
    share = x.shape[0] // count
    got = []
    for mask in range(1, count):
        sent = part(x, mine ^ mask, share).astype(BF)
        got.append(lax.ppermute(sent, axis, flip(axis, mask)))
    got, beside = lax.optimization_barrier((got, beside))
    total = part(x, mine, share)
    for term in got:
        total = total + term.astype(F32)
    return total, beside


def line_sum(x, axis):
    bits, mine = lax.axis_size(axis).bit_length() - 1, lax.axis_index(axis)
    for bit in range(bits - 1):
        side, half = (mine >> bit) & 1, x.shape[0] // 2
        sent = part(x, 1 - side, half).astype(BF)
        x = part(x, side, half) + lax.ppermute(sent, axis, flip(axis, 1 << bit)).astype(F32)
    x = lax.reduce_precision(x, 8, 7)
    got = lax.ppermute(x.astype(BF), axis, flip(axis, 1 << (bits - 1)))
    y = (x + got.astype(F32)).astype(BF)
    for bit in reversed(range(bits - 1)):
        got = lax.ppermute(y, axis, flip(axis, 1 << bit))
        low = ((mine >> bit) & 1) == 0
        y = jnp.where(low, jnp.stack([y, got]), jnp.stack([got, y])).reshape(-1, y.shape[-1])
    return y


def direct_gather(y, axis):
    count, mine = lax.axis_size(axis), lax.axis_index(axis)
    share = y.shape[0]
    whole = jnp.zeros((count * share,) + y.shape[1:], y.dtype)
    whole = lax.dynamic_update_slice_in_dim(whole, y, mine * share, 0)
    for mask in range(1, count):
        got = lax.ppermute(y, axis, flip(axis, mask))
        whole = lax.dynamic_update_slice_in_dim(whole, got, (mine ^ mask) * share, 0)
    return whole


def join_kernel(core, mine, other, main_grad, down_grad):
    split, end = mine.shape[0], main_grad.shape[0]
    for which, low, high in ((0, mine, other), (1, other, mine)):

        @pl.when(core[0] == which)
        def _():
            main_grad[0:split] = low[...].astype(F32)
            main_grad[split:end] = high[0 : end - split].astype(F32)
            down_grad[...] = high[end - split :].astype(F32)


def reduce_all(kept, sent, beside, main_rows):
    half, core = kept.shape[0], lax.axis_index("clip")
    swap = flip("clip", 1)
    x = kept + lax.ppermute(sent, "clip", swap)
    x, beside = direct_scatter(x, "row", beside)
    y = direct_gather(line_sum(x, "col"), "row")
    other = lax.ppermute(y, "clip", swap)
    vmem = pl.BlockSpec(memory_space=pltpu.VMEM)
    main_grad, down_grad = pl.pallas_call(
        join_kernel,
        out_shape=(
            jax.ShapeDtypeStruct((main_rows, x.shape[1]), F32),
            jax.ShapeDtypeStruct((2 * half - main_rows, x.shape[1]), F32),
        ),
        in_specs=[pl.BlockSpec(memory_space=pltpu.SMEM), vmem, vmem],
        out_specs=(vmem, vmem),
        compiler_params=pltpu.CompilerParams(vmem_limit_bytes=8 << 20),
    )(core[None], y, other)
    return main_grad, down_grad, beside


def dot(a, b):
    return lax.dot_general(a, b, (((1,), (0,)), ((), ())), preferred_element_type=F32)


LEFT = 8


def main_kernel(
    flags, wide, grad_wide, kernel_main, w_grad, w_down, latent_grad,
    kept, sent, grad_taps, latent,
    w_main, x32, side32, x_taps, pre, l32, act_grad, act_side, pre_grad, act, act_taps, grad_t,
    total, down_total,
):
    frames, in_rows, in_cols, channels = wide.shape
    rows, cols = in_rows - 4, in_cols - 4
    ext = rows + 2
    half_rows, half_cols = rows // 2, cols // 2
    own, side = ext * cols, ext * 8
    side32[...] = jnp.zeros_like(side32)
    pre[0:2] = jnp.zeros((2,) + pre.shape[1:], F32)
    grad_t[frames:] = jnp.zeros((2,) + grad_t.shape[1:], BF)
    l32[...] = jnp.zeros_like(l32)
    act_side[...] = jnp.zeros_like(act_side)
    for kt in range(3):
        for tap in range(9):
            rows_at, cols_at = tap * channels, kt * channels
            w_main[rows_at : rows_at + channels, cols_at : cols_at + channels] = kernel_main[9 * kt + tap]
    count = flags[0]
    low_row, high_row = flags[1].astype(F32), flags[2].astype(F32)
    low_col, high_col = flags[3].astype(F32), flags[4].astype(F32)

    def frame(t, carry):
        x32[:, 0:in_cols, :] = wide[t].astype(F32)
        for kw in range(3):
            shifted = x32[:, pl.ds(1 + kw, cols), :].astype(BF)
            x_taps[t, kw] = shifted.reshape(in_rows * cols, channels)
            side32[kw, :, 0:1, :] = x32[:, kw : kw + 1, :]
            side32[kw, :, 1:2, :] = x32[:, cols + 1 + kw : cols + 2 + kw, :]
        lhs = jnp.concatenate(
            [
                x_taps[t, kw, kh * cols : kh * cols + own]
                for kh in range(3)
                for kw in range(3)
            ],
            axis=1,
        )
        side_lhs = jnp.concatenate(
            [
                side32[kw, kh : kh + ext].reshape(side, channels).astype(BF)
                for kh in range(3)
                for kw in range(3)
            ],
            axis=1,
        )
        for start, size, left in ((0, own, lhs), (own, side, side_lhs)):
            out = dot(left, w_main[...])
            place = pl.ds(start, size)
            parts = [out[:, k * channels : (k + 1) * channels] for k in range(3)]
            pre[t + 2, place] = parts[0]
            pre[t + 1, place] += parts[1]
            pre[t, place] += parts[2]

            @pl.when(t == 0)
            def _():
                pre[0, place] += parts[0] + parts[1]
                pre[1, place] += parts[0]

        l32[:, 0 : half_cols + 2, :] = grad_wide[t].astype(F32)
        near = [l32[:, pl.ds(dq, 16), :].astype(BF) for dq in range(2)]
        grads = jnp.concatenate(
            [
                near[dq][dp : dp + half_rows + 1].reshape((half_rows + 1) * 16, channels)
                for dp in (1, 0)
                for dq in (1, 0)
            ],
            axis=1,
        )
        classes = dot(grads, w_grad[...])
        for p in range(half_rows + 1):
            for odd in range(2):
                line = classes[p * 16 : p * 16 + half_cols + 1]
                row = 2 * p + 1 - odd
                even_part = line[:, 2 * odd * channels : (2 * odd + 1) * channels]
                odd_part = line[:, (2 * odd + 1) * channels : (2 * odd + 2) * channels]
                act_grad[row, pl.ds(LEFT, half_cols + 1, stride=2), :] = even_part
                act_grad[row, pl.ds(LEFT - 1, half_cols + 1, stride=2), :] = odd_part
        act_side[:, 0:1, :] = act_grad[:, LEFT - 1 : LEFT, :]
        act_side[:, 1:2, :] = act_grad[:, LEFT + cols : LEFT + cols + 1, :]

        live = jnp.where(t < count, 1.0, 0.0).astype(F32)

        def row_mask(width):
            place = lax.broadcasted_iota(jnp.int32, (ext, width, channels), 0)
            edge = jnp.where(place == 0, low_row, jnp.where(place == ext - 1, high_row, 1.0))
            return edge * live

        def pointwise(v, grad, mask):
            logistic = 1.0 / (1.0 + jnp.exp(-v))
            out = (v * logistic * mask).astype(BF)
            back = (grad * logistic * (1.0 + v * (1.0 - logistic)) * mask).astype(BF)
            return out.astype(F32), back

        own_act, own_grad = pointwise(
            pre[t, 0:own],
            act_grad[:, LEFT : LEFT + cols, :].reshape(own, channels),
            row_mask(cols).reshape(own, channels),
        )
        act[:, LEFT : LEFT + cols, :] = own_act.reshape(ext, cols, channels)
        pre_grad[:, LEFT : LEFT + cols, :] = own_grad.astype(F32).reshape(ext, cols, channels)
        inner = own_grad[cols : cols + rows * cols].astype(F32)
        grad_t[t] = inner.T.astype(BF)
        place = lax.broadcasted_iota(jnp.int32, (ext, 8, channels), 1)
        col_mask = jnp.where(place == 0, low_col, jnp.where(place == 1, high_col, 0.0))
        rim_act, rim_grad = pointwise(
            pre[t, own : own + side],
            act_side[...].reshape(side, channels),
            (row_mask(8) * col_mask).reshape(side, channels),
        )
        rim_act = rim_act.reshape(ext, 8, channels)
        rim_grad = rim_grad.astype(F32).reshape(ext, 8, channels)
        act[:, LEFT + cols : LEFT + cols + 1, :] = rim_act[:, 1:2, :]
        pre_grad[:, LEFT - 1 : LEFT, :] = rim_grad[:, 0:1, :]
        pre_grad[:, LEFT + cols : LEFT + cols + 1, :] = rim_grad[:, 1:2, :]
        for kw in range(3):
            shifted = pre_grad[:, pl.ds(LEFT - 1 + kw, cols), :].astype(BF)
            grad_taps[t, kw] = shifted.reshape(own, channels)
        for a in range(3):
            for b in range(3):
                tap = jnp.concatenate(
                    [
                        act[2 * i + a + 1, pl.ds(LEFT + b, half_cols, stride=2), :]
                        for i in range(half_rows)
                    ],
                    axis=0,
                ).astype(BF)
                at = (3 * a + b) * channels
                act_taps[t, :, at : at + channels] = tap
        return carry

    lax.fori_loop(0, frames, frame, 0)

    flat = act_taps[...].reshape(frames * half_rows * half_cols, 9 * channels)
    latent[...] = dot(flat, w_down[...]).astype(BF)
    down = dot(latent_grad[...].astype(F32).T.astype(BF), flat)
    for tap in range(9):
        down_total[tap] = down[:, tap * channels : (tap + 1) * channels]

    total[...] = jnp.zeros_like(total)

    def weights(s, carry):
        right = jnp.concatenate(
            [
                x_taps[s, kw, (kh + 1) * cols : (kh + 1 + rows) * cols]
                for kh in range(3)
                for kw in range(3)
            ],
            axis=1,
        )
        left = grad_t[pl.ds(s, 3)].reshape(3 * channels, rows * cols)
        out = dot(left, right)
        for tap in range(9):
            block = out[:, tap * channels : (tap + 1) * channels]
            total[tap] += block

        @pl.when(s == 0)
        def _():
            for tap in range(9):
                block = out[:, tap * channels : (tap + 1) * channels]
                top, middle = block[:channels], block[channels : 2 * channels]
                total[tap, channels : 2 * channels] += top
                total[tap, 2 * channels :] += top + middle

        return carry

    lax.fori_loop(0, frames, weights, 0)

    def emit(low, high):
        def tap_out(tap, carry):
            at = pl.multiple_of(tap * channels, channels)
            after = pl.multiple_of((9 + tap) * channels, channels)
            low[pl.ds(at, channels), :] = total[tap, 2 * channels :].T
            low[pl.ds(after, channels), :] = total[tap, channels : 2 * channels].T
            high[pl.ds(at, channels), :] = total[tap, 0:channels].T
            high[pl.ds(after, channels), :] = down_total[tap].T
            return carry

        lax.fori_loop(0, 9, tap_out, 0)

    @pl.when(flags[5] == 0)
    def _():
        emit(kept, sent)

    @pl.when(flags[5] == 1)
    def _():
        emit(sent, kept)


def back_kernel(grad_taps, kernel_main, video_grad, w_back, total):
    frames, _, own, channels = grad_taps.shape
    inner = video_grad.shape[1]
    cols = (own - inner) // 2
    total[0:2] = jnp.zeros((2,) + total.shape[1:], F32)
    for kt in range(3):
        for tap in range(9):
            rows_at, cols_at = tap * channels, kt * channels
            block = kernel_main[9 * kt + 8 - tap].astype(F32).T.astype(BF)
            w_back[rows_at : rows_at + channels, cols_at : cols_at + channels] = block

    def frame(t, carry):
        lhs = jnp.concatenate(
            [
                grad_taps[t, kw, kh * cols : kh * cols + inner]
                for kh in range(3)
                for kw in range(3)
            ],
            axis=1,
        )
        out = dot(lhs, w_back[...])
        total[t + 2] = out[:, 2 * channels :]
        total[t + 1] += out[:, channels : 2 * channels]
        total[t] += out[:, :channels]
        return carry

    lax.fori_loop(0, frames, frame, 0)
    video_grad[0] = (total[0] + total[1] + total[2]).astype(BF)

    def store(t, carry):
        video_grad[t] = total[t + 2].astype(BF)
        return carry

    lax.fori_loop(1, frames, store, 0)


def grad_matrix(kernel_down):
    k = jnp.swapaxes(kernel_down, 2, 3)
    zero = jnp.zeros_like(k[0, 0])
    return jnp.concatenate(
        [
            jnp.concatenate([k[0, 0], zero, zero, zero], axis=1),
            jnp.concatenate([k[0, 2], k[0, 1], zero, zero], axis=1),
            jnp.concatenate([k[2, 0], zero, k[1, 0], zero], axis=1),
            jnp.concatenate([k[2, 2], k[2, 1], k[1, 2], k[1, 1]], axis=1),
        ]
    )


def on_device(video, frame_counts, kernel_main, kernel_down, latent_grad):
    _, frames, rows, cols, channels = video.shape
    wide, grad_wide = with_halo(video[0], latent_grad[0])
    row, col = lax.axis_index("row"), lax.axis_index("col")
    flags = jnp.stack(
        [
            frame_counts[0],
            (row > 0).astype(jnp.int32),
            (row < lax.axis_size("row") - 1).astype(jnp.int32),
            (col > 0).astype(jnp.int32),
            (col < lax.axis_size("col") - 1).astype(jnp.int32),
            lax.axis_index("clip"),
        ]
    )
    taps = kernel_main.reshape(27, channels, channels)
    w_down = kernel_down.reshape(9 * channels, channels)
    ext = rows + 2
    own, side, outs = ext * cols, ext * 8, frames * rows * cols // 4
    pixels = frames * rows * cols
    vmem = pl.BlockSpec(memory_space=pltpu.VMEM)
    kept, sent, grad_taps, latent = pl.pallas_call(
        main_kernel,
        out_shape=(
            jax.ShapeDtypeStruct((18 * channels, channels), F32),
            jax.ShapeDtypeStruct((18 * channels, channels), F32),
            jax.ShapeDtypeStruct((frames, 3, own, channels), BF),
            jax.ShapeDtypeStruct((outs, channels), BF),
        ),
        in_specs=[pl.BlockSpec(memory_space=pltpu.SMEM)] + [vmem] * 6,
        out_specs=(vmem,) * 4,
        scratch_shapes=[
            pltpu.VMEM((9 * channels, 3 * channels), BF),
            pltpu.VMEM((rows + 4, cols + 8, channels), F32),
            pltpu.VMEM((3, rows + 4, 8, channels), F32),
            pltpu.VMEM((frames, 3, (rows + 4) * cols, channels), BF),
            pltpu.VMEM((frames + 2, own + side, channels), F32),
            pltpu.VMEM((rows // 2 + 2, 24, channels), F32),
            pltpu.VMEM((ext, cols + 16, channels), F32),
            pltpu.VMEM((ext, 8, channels), F32),
            pltpu.VMEM((ext, cols + 16, channels), F32),
            pltpu.VMEM((ext, cols + 16, channels), F32),
            pltpu.VMEM((frames, rows * cols // 4, 9 * channels), BF),
            pltpu.VMEM((frames + 2, channels, rows * cols), BF),
            pltpu.VMEM((9, 3 * channels, channels), F32),
            pltpu.VMEM((9, channels, channels), F32),
        ],
        compiler_params=pltpu.CompilerParams(vmem_limit_bytes=24 << 20),
        cost_estimate=pl.CostEstimate(
            flops=2 * 60 * pixels * channels * channels,
            bytes_accessed=12 << 20,
            transcendentals=pixels * channels,
        ),
    )(
        flags,
        wide,
        grad_wide,
        taps,
        grad_matrix(kernel_down),
        w_down,
        latent_grad.reshape(outs, channels),
    )
    video_grad = pl.pallas_call(
        back_kernel,
        out_shape=jax.ShapeDtypeStruct((frames, rows * cols, channels), BF),
        in_specs=[vmem] * 2,
        out_specs=vmem,
        scratch_shapes=[
            pltpu.VMEM((9 * channels, 3 * channels), BF),
            pltpu.VMEM((frames + 2, rows * cols, channels), F32),
        ],
        compiler_params=pltpu.CompilerParams(vmem_limit_bytes=12 << 20),
        cost_estimate=pl.CostEstimate(
            flops=2 * 27 * pixels * channels * channels,
            bytes_accessed=4 << 20,
            transcendentals=0,
        ),
    )(grad_taps, taps)
    main_grad, down_grad, video_grad = reduce_all(kept, sent, video_grad, 27 * channels)
    main_grad = main_grad.reshape(kernel_main.shape)
    down_grad = down_grad.reshape(kernel_down.shape)
    return (latent.reshape(latent_grad.shape), video_grad.reshape(video.shape), main_grad, down_grad)


def solution(mesh):
    tiles = P("clip", None, "row", "col", None)
    return jax.shard_map(
        on_device,
        mesh=mesh,
        in_specs=(tiles, P("clip"), P(), P(), tiles),
        out_specs=(tiles, tiles, P(), P()),
        check_vma=False,
    )
```

profile of v0, /device:TPU:0, one launch (start us, length us, event | category | flops | bytes accessed | tf_op | source)
XLA Modules:
  0.0 87.3 jit_solution(14734879889845766537)
XLA Ops:
  0.6 0.0 copy-start.6
  0.6 0.0 copy-start
  0.7 1.0 %fusion.6 = (bf16[8,2,16,128]{3,2,1,0:T(8,128)(2,1)S(1)}, bf16[8,2,16,128]{3,2,1,0:T(8,128)(2,1)S(1)}) fusion(bf16[8,16,16,128]{3,2,1,0:T(8,128)(2,1)} %bitcast.59), kind=kLoop, calls=%fused_computation.44 | loop fusion | bytes 262144 | tf_op jit(solution)/shard_map/slice | solution.py:40
  1.6 0.7 slice_bitcast_fusion.12
  2.4 1.3 %collective-permute-start.1 = (bf16[320,128]{1,0:T(8,128)(2,1)S(1)}, bf16[320,128]{1,0:T(8,128)(2,1)S(1)}, u32[]{:S(2)}, u32[]{:S(2)}) collective-permute-start(bf16[320,128]{1,0:T(8,128)(2,1)S(1)} %pad_maximum_fusion.8), channel_id=1, source_target_pairs={{4,0},{8,4},{12,8},{5,1},{9,5},{13,9},{6,2},{10,6},{14,10},{7,3},{... | collective-permute-start | bytes 245768 | tf_op jit(solution)/shard_map/ppermute | solution.py:23
  3.7 5.5 %collective-permute-start = (bf16[320,128]{1,0:T(8,128)(2,1)S(1)}, bf16[320,128]{1,0:T(8,128)(2,1)S(1)}, u32[]{:S(2)}, u32[]{:S(2)}) collective-permute-start(bf16[320,128]{1,0:T(8,128)(2,1)S(1)} %pad_maximum_fusion.7), channel_id=1, source_target_pairs={{0,4},{4,8},{8,12},{1,5},{5,9},{9,13},{2,6},{6,10},{10,14},{3,7},{... | collective-permute-start | bytes 245768 | tf_op jit(solution)/shard_map/ppermute | solution.py:22
  9.2 1.2 %copy.12 = bf16[3,3,128,128]{2,3,1,0:T(8,128)(2,1)S(1)} copy(bf16[3,3,128,128]{3,2,1,0:T(8,128)(2,1)} %param.8) | data formatting | bytes 589824 | tf_op args[3]
  11.0 0.1 stack.53.flags
  11.1 0.1 collective-permute-done
  11.2 0.0 collective-permute-done.1
  11.2 0.0 copy-done
  11.2 0.2 maximum_reduce_fusion
  11.5 0.0 copy-done.6
  11.5 0.1 pad_maximum_fusion.6
  11.7 4.0 %collective-permute-start.2 = (bf16[400,128]{1,0:T(8,128)(2,1)S(1)}, bf16[400,128]{1,0:T(8,128)(2,1)S(1)}, u32[]{:S(2)}, u32[]{:S(2)}) collective-permute-start(bf16[400,128]{1,0:T(8,128)(2,1)S(1)} %pad_maximum_fusion.2), channel_id=1, source_target_pairs={{0,1},{1,2},{2,3},{4,5},{5,6},{6,7},{8,9},{9,10},{10,11},{12,13},{... | collective-permute-start | bytes 307208 | tf_op jit(solution)/shard_map/ppermute | solution.py:22
  15.7 1.3 %collective-permute-start.3 = (bf16[400,128]{1,0:T(8,128)(2,1)S(1)}, bf16[400,128]{1,0:T(8,128)(2,1)S(1)}, u32[]{:S(2)}, u32[]{:S(2)}) collective-permute-start(bf16[400,128]{1,0:T(8,128)(2,1)S(1)} %pad_maximum_fusion.3), channel_id=1, source_target_pairs={{1,0},{2,1},{3,2},{5,4},{6,5},{7,6},{9,8},{10,9},{11,10},{13,12},{... | collective-permute-start | bytes 307208 | tf_op jit(solution)/shard_map/ppermute | solution.py:23
  17.1 0.0 copy-start.1
  17.1 0.8 collective-permute-done.2
  17.9 4.3 %collective-permute-done.3 = bf16[400,128]{1,0:T(8,128)(2,1)S(1)} collective-permute-done((bf16[400,128]{1,0:T(8,128)(2,1)S(1)}, bf16[400,128]{1,0:T(8,128)(2,1)S(1)}, u32[]{:S(2)}, u32[]{:S(2)}) %collective-permute-start.3) | collective-permute-done | bytes 102432 | tf_op jit(solution)/shard_map/ppermute | solution.py:23
  22.3 0.2 pad_maximum_fusion.1.grad_wide
  22.5 0.6 pad_maximum_fusion.wide
  23.1 0.0 copy-done.1
  23.1 0.0 copy-start.2
  23.1 1.2 %copy-done.2 = bf16[3,3,3,128,128]{4,3,2,1,0:T(8,128)(2,1)S(1)} copy-done((bf16[3,3,3,128,128]{4,3,2,1,0:T(8,128)(2,1)S(1)}, bf16[3,3,3,128,128]{4,3,2,1,0:T(8,128)(2,1)}, u32[]{:S(2)}) %copy-start.2) | copy-done | bytes 884760
  24.3 17.9 %shard_map.84 = (f32[2304,128]{1,0:T(8,128)S(1)}, f32[2304,128]{1,0:T(8,128)S(1)}, bf16[8,3,288,128]{3,2,1,0:T(8,128)(2,1)S(1)}, bf16[512,128]{1,0:T(8,128)(2,1)}) custom-call(s32[6]{0:T(128)S(1)} %stack.53.flags, bf16[8,20,20,128]{3,2,1,0:T(8,128)(2,1)S(1)} %pad_maximum_fusion.wide, bf16[8,10,10,128]{3,2,1,0:T(8,128)(2,1)S(1)} %pad_maximum_fusion.1.grad_wide, ...), custom_call_target="tpu_custom_call" | custom-call | flops 4026531840 | bytes 12582912 | tf_op jit(solution)/shard_map/pallas_call | solution.py:390
  42.2 0.0 copy-start.4
  42.2 1.2 %copy-done.4 = bf16[8,3,288,128]{3,2,1,0:T(8,128)(2,1)} copy-done((bf16[8,3,288,128]{3,2,1,0:T(8,128)(2,1)}, bf16[8,3,288,128]{3,2,1,0:T(8,128)(2,1)S(1)}, u32[]{:S(2)}) %copy-start.4) | copy-done | bytes 1769496
  43.4 0.0 collective-permute-start.4
  43.4 3.0 %collective-permute-done.4 = f32[2304,128]{1,0:T(8,128)} collective-permute-done((f32[2304,128]{1,0:T(8,128)S(1)}, f32[2304,128]{1,0:T(8,128)}, u32[]{:S(2)}, u32[]{:S(2)}) %collective-permute-start.4) | collective-permute-done | bytes 1179680 | tf_op jit(solution)/shard_map/ppermute | solution.py:106
  46.4 0.0 copy-start.3
  46.4 0.0 copy-start.5
  46.4 1.5 %add.42 = f32[2304,128]{1,0:T(8,128)S(1)} add(f32[2304,128]{1,0:T(8,128)S(1)} %get-tuple-element.15, f32[2304,128]{1,0:T(8,128)} %collective-permute-done.4) | non-fusion elementwise | flops 294912 | bytes 3538944 | tf_op jit(solution)/shard_map/add | solution.py:106
  48.0 0.1 dynamic-slice_convert_fusion
  48.0 2.5 %collective-permute-start.5 = (bf16[576,128]{1,0:T(8,128)(2,1)S(1)}, bf16[576,128]{1,0:T(8,128)(2,1)S(1)}, u32[]{:S(2)}, u32[]{:S(2)}) collective-permute-start(bf16[576,128]{1,0:T(8,128)(2,1)S(1)} %get-tuple-element.28), channel_id=1, source_target_pairs={{0,4},{4,0},{8,12},{12,8},{1,5},{5,1},{9,13},{13,9},{2,6},{6,2},{1... | collective-permute-start | bytes 442376 | tf_op jit(solution)/shard_map/ppermute | solution.py:57
  50.5 1.9 %collective-permute-start.6 = (bf16[576,128]{1,0:T(8,128)(2,1)S(1)}, bf16[576,128]{1,0:T(8,128)(2,1)S(1)}, u32[]{:S(2)}, u32[]{:S(2)}) collective-permute-start(bf16[576,128]{1,0:T(8,128)(2,1)S(1)} %get-tuple-element.27), channel_id=1, source_target_pairs={{0,8},{4,12},{8,0},{12,4},{1,9},{5,13},{9,1},{13,5},{2,10},{6,14},... | collective-permute-start | bytes 442376 | tf_op jit(solution)/shard_map/ppermute | solution.py:57
  52.4 1.4 %collective-permute-start.7 = (bf16[576,128]{1,0:T(8,128)(2,1)S(1)}, bf16[576,128]{1,0:T(8,128)(2,1)S(1)}, u32[]{:S(2)}, u32[]{:S(2)}) collective-permute-start(bf16[576,128]{1,0:T(8,128)(2,1)S(1)} %get-tuple-element.26), channel_id=1, source_target_pairs={{0,12},{4,8},{8,4},{12,0},{1,13},{5,9},{9,5},{13,1},{2,14},{6,10},... | collective-permute-start | bytes 442376 | tf_op jit(solution)/shard_map/ppermute | solution.py:57
  53.8 0.0 copy-done.3
  53.8 0.0 copy-done.5
  53.8 5.0 %shard_map.85 = bf16[8,256,128]{2,1,0:T(8,128)(2,1)} custom-call(bf16[8,3,288,128]{3,2,1,0:T(8,128)(2,1)S(1)} %copy-done.5, bf16[27,128,128]{2,1,0:T(8,128)(2,1)S(1)} %bitcast.58), custom_call_target="tpu_custom_call" | custom-call | flops 1811939328 | bytes 4194304 | tf_op jit(solution)/shard_map/pallas_call | solution.py:431
  58.8 0.0 collective-permute-done.5
  58.8 0.1 collective-permute-done.6
  59.0 1.8 %collective-permute-done.7 = bf16[576,128]{1,0:T(8,128)(2,1)S(1)} collective-permute-done((bf16[576,128]{1,0:T(8,128)(2,1)S(1)}, bf16[576,128]{1,0:T(8,128)(2,1)S(1)}, u32[]{:S(2)}, u32[]{:S(2)}) %collective-permute-start.7) | collective-permute-done | bytes 147488 | tf_op jit(solution)/shard_map/ppermute | solution.py:57
  60.8 0.1 convert_add_fusion
  60.9 1.7 %collective-permute-start.8 = (bf16[288,128]{1,0:T(8,128)(2,1)S(1)}, bf16[288,128]{1,0:T(8,128)(2,1)S(1)}, u32[]{:S(2)}, u32[]{:S(2)}) collective-permute-start(bf16[288,128]{1,0:T(8,128)(2,1)S(1)} %dynamic-slice_convert_fusion.3), channel_id=1, source_target_pairs={{0,1},{1,0},{2,3},{3,2},{4,5},{5,4},{6,7},{7,6},{8,9},{9,8},{10,11... | collective-permute-start | bytes 221192 | tf_op jit(solution)/shard_map/ppermute | solution.py:70
  62.6 2.8 %collective-permute-done.8 = bf16[288,128]{1,0:T(8,128)(2,1)S(1)} collective-permute-done((bf16[288,128]{1,0:T(8,128)(2,1)S(1)}, bf16[288,128]{1,0:T(8,128)(2,1)S(1)}, u32[]{:S(2)}, u32[]{:S(2)}) %collective-permute-start.8) | collective-permute-done | bytes 73760 | tf_op jit(solution)/shard_map/ppermute | solution.py:70
  65.3 2.7 %collective-permute-start.9 = (bf16[288,128]{1,0:T(8,128)(2,1)S(1)}, bf16[288,128]{1,0:T(8,128)(2,1)S(1)}, u32[]{:S(2)}, u32[]{:S(2)}) collective-permute-start(bf16[288,128]{1,0:T(8,128)(2,1)S(1)} %fusion.4), channel_id=1, source_target_pairs={{0,2},{1,3},{2,0},{3,1},{4,6},{5,7},{6,4},{7,5},{8,10},{9,11},{10,... | collective-permute-start | bytes 221192 | tf_op jit(solution)/shard_map/ppermute | solution.py:72
  68.0 2.7 %collective-permute-done.9 = bf16[288,128]{1,0:T(8,128)(2,1)S(1)} collective-permute-done((bf16[288,128]{1,0:T(8,128)(2,1)S(1)}, bf16[288,128]{1,0:T(8,128)(2,1)S(1)}, u32[]{:S(2)}, u32[]{:S(2)}) %collective-permute-start.9) | collective-permute-done | bytes 73760 | tf_op jit(solution)/shard_map/ppermute | solution.py:72
  70.7 1.6 %collective-permute-start.10 = (bf16[288,128]{1,0:T(8,128)(2,1)S(1)}, bf16[288,128]{1,0:T(8,128)(2,1)S(1)}, u32[]{:S(2)}, u32[]{:S(2)}) collective-permute-start(bf16[288,128]{1,0:T(8,128)(2,1)S(1)} %add_convert_fusion), channel_id=1, source_target_pairs={{0,1},{1,0},{2,3},{3,2},{4,5},{5,4},{6,7},{7,6},{8,9},{9,8},{10,11... | collective-permute-start | bytes 221192 | tf_op jit(solution)/shard_map/ppermute | solution.py:75
  72.4 2.8 %collective-permute-done.10 = bf16[288,128]{1,0:T(8,128)(2,1)S(1)} collective-permute-done((bf16[288,128]{1,0:T(8,128)(2,1)S(1)}, bf16[288,128]{1,0:T(8,128)(2,1)S(1)}, u32[]{:S(2)}, u32[]{:S(2)}) %collective-permute-start.10) | collective-permute-done | bytes 73760 | tf_op jit(solution)/shard_map/ppermute | solution.py:75
  75.2 0.7 collective-permute-start.11
  75.8 1.7 %collective-permute-start.12 = (bf16[576,128]{1,0:T(8,128)(2,1)S(1)}, bf16[576,128]{1,0:T(8,128)(2,1)S(1)}, u32[]{:S(2)}, u32[]{:S(2)}) collective-permute-start(bf16[576,128]{1,0:T(8,128)(2,1)S(1)} %bitcast.68), channel_id=1, source_target_pairs={{0,8},{4,12},{8,0},{12,4},{1,9},{5,13},{9,1},{13,5},{2,10},{6,14},... | collective-permute-start | bytes 442376 | tf_op jit(solution)/shard_map/ppermute | solution.py:87
  77.6 1.1 %collective-permute-start.13 = (bf16[576,128]{1,0:T(8,128)(2,1)S(1)}, bf16[576,128]{1,0:T(8,128)(2,1)S(1)}, u32[]{:S(2)}, u32[]{:S(2)}) collective-permute-start(bf16[576,128]{1,0:T(8,128)(2,1)S(1)} %bitcast.69), channel_id=1, source_target_pairs={{0,12},{4,8},{8,4},{12,0},{1,13},{5,9},{9,5},{13,1},{2,14},{6,10},... | collective-permute-start | bytes 442376 | tf_op jit(solution)/shard_map/ppermute | solution.py:87
  78.7 0.1 broadcast_in_dim.8
  78.8 1.5 %collective-permute-done.11 = bf16[576,128]{1,0:T(8,128)(2,1)S(1)} collective-permute-done((bf16[576,128]{1,0:T(8,128)(2,1)S(1)}, bf16[576,128]{1,0:T(8,128)(2,1)S(1)}, u32[]{:S(2)}, u32[]{:S(2)}) %collective-permute-start.11) | collective-permute-done | bytes 147488 | tf_op jit(solution)/shard_map/ppermute | solution.py:87
  80.4 1.4 %collective-permute-done.12 = bf16[576,128]{1,0:T(8,128)(2,1)S(1)} collective-permute-done((bf16[576,128]{1,0:T(8,128)(2,1)S(1)}, bf16[576,128]{1,0:T(8,128)(2,1)S(1)}, u32[]{:S(2)}, u32[]{:S(2)}) %collective-permute-start.12) | collective-permute-done | bytes 147488 | tf_op jit(solution)/shard_map/ppermute | solution.py:87
  81.9 1.7 %collective-permute-done.13 = bf16[576,128]{1,0:T(8,128)(2,1)S(1)} collective-permute-done((bf16[576,128]{1,0:T(8,128)(2,1)S(1)}, bf16[576,128]{1,0:T(8,128)(2,1)S(1)}, u32[]{:S(2)}, u32[]{:S(2)}) %collective-permute-start.13) | collective-permute-done | bytes 147488 | tf_op jit(solution)/shard_map/ppermute | solution.py:87
  83.6 0.1 collective-permute-start.14
  83.7 2.0 %collective-permute-done.14.other = bf16[2304,128]{1,0:T(8,128)(2,1)S(1)} collective-permute-done((bf16[2304,128]{1,0:T(8,128)(2,1)S(1)}, bf16[2304,128]{1,0:T(8,128)(2,1)S(1)}, u32[]{:S(2)}, u32[]{:S(2)}) %collective-permute-start.14) | collective-permute-done | bytes 589856 | tf_op jit(solution)/shard_map/ppermute | solution.py:109
  85.7 1.6 %shard_map.86 = (f32[3456,128]{1,0:T(8,128)}, f32[1152,128]{1,0:T(8,128)}) custom-call(s32[1]{0:T(128)} %bitcast.4.core, bf16[2304,128]{1,0:T(8,128)(2,1)S(1)} %constant_dynamic-update-slice_fusion.mine, bf16[2304,128]{1,0:T(8,128)(2,1)S(1)} %collective-permute-done.14.other), custom_call_target="tpu_custom_call" | custom-call | tf_op jit(solution)/shard_map/pallas_call | solution.py:111
  (28 shorter events, 0.4 us)
Async XLA Ops:
  0.6 10.9 %copy-start.6 = (bf16[1,8,16,16,128]{4,3,2,1,0:T(8,128)(2,1)S(1)}, bf16[1,8,16,16,128]{4,3,2,1,0:T(8,128)(2,1)}, u32[]{:S(2)}) copy-start(bf16[1,8,16,16,128]{4,3,2,1,0:T(8,128)(2,1)} %param.5) | copy-start | bytes 1572868
  0.6 10.6 %copy-start = (bf16[1,8,8,8,128]{4,3,2,1,0:T(8,128)(2,1)S(1)}, bf16[1,8,8,8,128]{4,3,2,1,0:T(8,128)(2,1)}, u32[]{:S(2)}) copy-start(bf16[1,8,8,8,128]{4,3,2,1,0:T(8,128)(2,1)} %param.9) | copy-start | bytes 393220
  2.4 8.8 %collective-permute-start.1 = (bf16[320,128]{1,0:T(8,128)(2,1)S(1)}, bf16[320,128]{1,0:T(8,128)(2,1)S(1)}, u32[]{:S(2)}, u32[]{:S(2)}) collective-permute-start(bf16[320,128]{1,0:T(8,128)(2,1)S(1)} %pad_maximum_fusion.8), channel_id=1, source_target_pairs={{4,0},{8,4},{12,8},{5,1},{9,5},{13,9},{6,2},{10,6},{14,10},{7,3},{... | collective-permute-start | bytes 245768 | tf_op jit(solution)/shard_map/ppermute | solution.py:23
  3.7 7.5 %collective-permute-start = (bf16[320,128]{1,0:T(8,128)(2,1)S(1)}, bf16[320,128]{1,0:T(8,128)(2,1)S(1)}, u32[]{:S(2)}, u32[]{:S(2)}) collective-permute-start(bf16[320,128]{1,0:T(8,128)(2,1)S(1)} %pad_maximum_fusion.7), channel_id=1, source_target_pairs={{0,4},{4,8},{8,12},{1,5},{5,9},{9,13},{2,6},{6,10},{10,14},{3,7},{... | collective-permute-start | bytes 245768 | tf_op jit(solution)/shard_map/ppermute | solution.py:22
  11.7 6.2 %collective-permute-start.2 = (bf16[400,128]{1,0:T(8,128)(2,1)S(1)}, bf16[400,128]{1,0:T(8,128)(2,1)S(1)}, u32[]{:S(2)}, u32[]{:S(2)}) collective-permute-start(bf16[400,128]{1,0:T(8,128)(2,1)S(1)} %pad_maximum_fusion.2), channel_id=1, source_target_pairs={{0,1},{1,2},{2,3},{4,5},{5,6},{6,7},{8,9},{9,10},{10,11},{12,13},{... | collective-permute-start | bytes 307208 | tf_op jit(solution)/shard_map/ppermute | solution.py:22
  15.7 6.6 %collective-permute-start.3 = (bf16[400,128]{1,0:T(8,128)(2,1)S(1)}, bf16[400,128]{1,0:T(8,128)(2,1)S(1)}, u32[]{:S(2)}, u32[]{:S(2)}) collective-permute-start(bf16[400,128]{1,0:T(8,128)(2,1)S(1)} %pad_maximum_fusion.3), channel_id=1, source_target_pairs={{1,0},{2,1},{3,2},{5,4},{6,5},{7,6},{9,8},{10,9},{11,10},{13,12},{... | collective-permute-start | bytes 307208 | tf_op jit(solution)/shard_map/ppermute | solution.py:23
  17.1 6.1 %copy-start.1 = (bf16[3,3,128,128]{3,2,1,0:T(8,128)(2,1)S(1)}, bf16[3,3,128,128]{3,2,1,0:T(8,128)(2,1)}, u32[]{:S(2)}) copy-start(bf16[3,3,128,128]{3,2,1,0:T(8,128)(2,1)} %param.8) | copy-start | bytes 884740
  23.1 1.2 %copy-start.2 = (bf16[3,3,3,128,128]{4,3,2,1,0:T(8,128)(2,1)S(1)}, bf16[3,3,3,128,128]{4,3,2,1,0:T(8,128)(2,1)}, u32[]{:S(2)}) copy-start(bf16[3,3,3,128,128]{4,3,2,1,0:T(8,128)(2,1)} %param.7) | copy-start | bytes 2654212
  42.2 1.2 %copy-start.4 = (bf16[8,3,288,128]{3,2,1,0:T(8,128)(2,1)}, bf16[8,3,288,128]{3,2,1,0:T(8,128)(2,1)S(1)}, u32[]{:S(2)}) copy-start(bf16[8,3,288,128]{3,2,1,0:T(8,128)(2,1)S(1)} %get-tuple-element.17.grad_taps) | copy-start | bytes 5308420
  43.4 3.0 %collective-permute-start.4 = (f32[2304,128]{1,0:T(8,128)S(1)}, f32[2304,128]{1,0:T(8,128)}, u32[]{:S(2)}, u32[]{:S(2)}) collective-permute-start(f32[2304,128]{1,0:T(8,128)S(1)} %get-tuple-element.16), channel_id=1, source_target_pairs={{0,16},{16,0},{1,17},{17,1},{2,18},{18,2},{3,19},{19,3},{4,20},{20... | collective-permute-start | bytes 3538952 | tf_op jit(solution)/shard_map/ppermute | solution.py:106
  46.4 7.4 %copy-start.3 = (bf16[3,3,3,128,128]{4,3,2,1,0:T(8,128)(2,1)S(1)}, bf16[3,3,3,128,128]{4,3,2,1,0:T(8,128)(2,1)}, u32[]{:S(2)}) copy-start(bf16[3,3,3,128,128]{4,3,2,1,0:T(8,128)(2,1)} %param.7) | copy-start | bytes 2654212
  46.4 7.4 %copy-start.5 = (bf16[8,3,288,128]{3,2,1,0:T(8,128)(2,1)S(1)}, bf16[8,3,288,128]{3,2,1,0:T(8,128)(2,1)}, u32[]{:S(2)}) copy-start(bf16[8,3,288,128]{3,2,1,0:T(8,128)(2,1)} %copy-done.4) | copy-start | bytes 5308420
  48.0 10.8 %collective-permute-start.5 = (bf16[576,128]{1,0:T(8,128)(2,1)S(1)}, bf16[576,128]{1,0:T(8,128)(2,1)S(1)}, u32[]{:S(2)}, u32[]{:S(2)}) collective-permute-start(bf16[576,128]{1,0:T(8,128)(2,1)S(1)} %get-tuple-element.28), channel_id=1, source_target_pairs={{0,4},{4,0},{8,12},{12,8},{1,5},{5,1},{9,13},{13,9},{2,6},{6,2},{1... | collective-permute-start | bytes 442376 | tf_op jit(solution)/shard_map/ppermute | solution.py:57
  50.5 8.5 %collective-permute-start.6 = (bf16[576,128]{1,0:T(8,128)(2,1)S(1)}, bf16[576,128]{1,0:T(8,128)(2,1)S(1)}, u32[]{:S(2)}, u32[]{:S(2)}) collective-permute-start(bf16[576,128]{1,0:T(8,128)(2,1)S(1)} %get-tuple-element.27), channel_id=1, source_target_pairs={{0,8},{4,12},{8,0},{12,4},{1,9},{5,13},{9,1},{13,5},{2,10},{6,14},... | collective-permute-start | bytes 442376 | tf_op jit(solution)/shard_map/ppermute | solution.py:57
  52.4 8.4 %collective-permute-start.7 = (bf16[576,128]{1,0:T(8,128)(2,1)S(1)}, bf16[576,128]{1,0:T(8,128)(2,1)S(1)}, u32[]{:S(2)}, u32[]{:S(2)}) collective-permute-start(bf16[576,128]{1,0:T(8,128)(2,1)S(1)} %get-tuple-element.26), channel_id=1, source_target_pairs={{0,12},{4,8},{8,4},{12,0},{1,13},{5,9},{9,5},{13,1},{2,14},{6,10},... | collective-permute-start | bytes 442376 | tf_op jit(solution)/shard_map/ppermute | solution.py:57
  60.9 4.4 %collective-permute-start.8 = (bf16[288,128]{1,0:T(8,128)(2,1)S(1)}, bf16[288,128]{1,0:T(8,128)(2,1)S(1)}, u32[]{:S(2)}, u32[]{:S(2)}) collective-permute-start(bf16[288,128]{1,0:T(8,128)(2,1)S(1)} %dynamic-slice_convert_fusion.3), channel_id=1, source_target_pairs={{0,1},{1,0},{2,3},{3,2},{4,5},{5,4},{6,7},{7,6},{8,9},{9,8},{10,11... | collective-permute-start | bytes 221192 | tf_op jit(solution)/shard_map/ppermute | solution.py:70
  65.3 5.3 %collective-permute-start.9 = (bf16[288,128]{1,0:T(8,128)(2,1)S(1)}, bf16[288,128]{1,0:T(8,128)(2,1)S(1)}, u32[]{:S(2)}, u32[]{:S(2)}) collective-permute-start(bf16[288,128]{1,0:T(8,128)(2,1)S(1)} %fusion.4), channel_id=1, source_target_pairs={{0,2},{1,3},{2,0},{3,1},{4,6},{5,7},{6,4},{7,5},{8,10},{9,11},{10,... | collective-permute-start | bytes 221192 | tf_op jit(solution)/shard_map/ppermute | solution.py:72
  70.7 4.4 %collective-permute-start.10 = (bf16[288,128]{1,0:T(8,128)(2,1)S(1)}, bf16[288,128]{1,0:T(8,128)(2,1)S(1)}, u32[]{:S(2)}, u32[]{:S(2)}) collective-permute-start(bf16[288,128]{1,0:T(8,128)(2,1)S(1)} %add_convert_fusion), channel_id=1, source_target_pairs={{0,1},{1,0},{2,3},{3,2},{4,5},{5,4},{6,7},{7,6},{8,9},{9,8},{10,11... | collective-permute-start | bytes 221192 | tf_op jit(solution)/shard_map/ppermute | solution.py:75
  75.2 5.2 %collective-permute-start.11 = (bf16[576,128]{1,0:T(8,128)(2,1)S(1)}, bf16[576,128]{1,0:T(8,128)(2,1)S(1)}, u32[]{:S(2)}, u32[]{:S(2)}) collective-permute-start(bf16[576,128]{1,0:T(8,128)(2,1)S(1)} %bitcast.67), channel_id=1, source_target_pairs={{0,4},{4,0},{8,12},{12,8},{1,5},{5,1},{9,13},{13,9},{2,6},{6,2},{1... | collective-permute-start | bytes 442376 | tf_op jit(solution)/shard_map/ppermute | solution.py:87
  75.8 6.0 %collective-permute-start.12 = (bf16[576,128]{1,0:T(8,128)(2,1)S(1)}, bf16[576,128]{1,0:T(8,128)(2,1)S(1)}, u32[]{:S(2)}, u32[]{:S(2)}) collective-permute-start(bf16[576,128]{1,0:T(8,128)(2,1)S(1)} %bitcast.68), channel_id=1, source_target_pairs={{0,8},{4,12},{8,0},{12,4},{1,9},{5,13},{9,1},{13,5},{2,10},{6,14},... | collective-permute-start | bytes 442376 | tf_op jit(solution)/shard_map/ppermute | solution.py:87
  77.6 6.0 %collective-permute-start.13 = (bf16[576,128]{1,0:T(8,128)(2,1)S(1)}, bf16[576,128]{1,0:T(8,128)(2,1)S(1)}, u32[]{:S(2)}, u32[]{:S(2)}) collective-permute-start(bf16[576,128]{1,0:T(8,128)(2,1)S(1)} %bitcast.69), channel_id=1, source_target_pairs={{0,12},{4,8},{8,4},{12,0},{1,13},{5,9},{9,5},{13,1},{2,14},{6,10},... | collective-permute-start | bytes 442376 | tf_op jit(solution)/shard_map/ppermute | solution.py:87
  83.6 2.1 %collective-permute-start.14 = (bf16[2304,128]{1,0:T(8,128)(2,1)S(1)}, bf16[2304,128]{1,0:T(8,128)(2,1)S(1)}, u32[]{:S(2)}, u32[]{:S(2)}) collective-permute-start(bf16[2304,128]{1,0:T(8,128)(2,1)S(1)} %constant_dynamic-update-slice_fusion.mine), channel_id=1, source_target_pairs={{0,16},{16,0},{1,17},{17,1},{2,18},{18,2},{3,19},{19,3},{4,20},{20... | collective-permute-start | bytes 1769480 | tf_op jit(solution)/shard_map/ppermute | solution.py:109
where the time goes:
time: 87.6 us; the launch traced here: 87.3 us
  starting transfers between devices  27.4 us (31%)
  waiting for transfers between devices  25.1 us (29%)
  Pallas kernels  24.5 us (28%)
  local copies, waits for them, and re-layouts  5.76 us (7%)
  other arithmetic  2.88 us (3%)
  between operations  1.59 us (2%)
    pallas_call x1, Pallas kernels, on_device(): pl.pallas_call(main_kernel, out_shape=(jax.ShapeDtypeStruct((18 * channel...  17.9 us
    ppermute x2, starting transfers between devices, exchange(): up = lax.ppermute(high_edge, axis, [(i, i + 1) for i in range(count - 1)])  9.48 us
    ppermute x3, starting transfers between devices, direct_scatter(): got.append(lax.ppermute(sent, axis, flip(axis, mask)))  5.74 us
    pallas_call x1, Pallas kernels, on_device(): pl.pallas_call(back_kernel, out_shape=jax.ShapeDtypeStruct((frames, rows...  5.04 us
    ppermute x3, waiting for transfers between devices, direct_gather(): got = lax.ppermute(y, axis, flip(axis, mask))  4.73 us
    ppermute x2, waiting for transfers between devices, exchange(): down = lax.ppermute(low_edge, axis, [(i + 1, i) for i in range(count - 1)])  4.35 us
    unnamed x15, local copies, waits for them, and re-layouts  3.57 us
    ppermute x3, starting transfers between devices, direct_gather(): got = lax.ppermute(y, axis, flip(axis, mask))  3.55 us
  transfers between devices with their start and end apart: 15, of which 13 were waited for; matrix products, arithmetic and copies ran while one was open for 2% of the time, Pallas kernels for 6%

commit v1 on v0

v1 whole, which is shorter than its diff:
```python
import jax
import jax.numpy as jnp
from jax import lax
from jax.experimental import pallas as pl
from jax.experimental.pallas import tpu as pltpu
from jax.sharding import PartitionSpec as P

BF = jnp.bfloat16
F32 = jnp.float32


def flip(axis, mask):
    return [(i, i ^ mask) for i in range(lax.axis_size(axis))]


def part(x, index, size):
    return lax.dynamic_slice_in_dim(x, index * size, size, axis=0)


def exchange(low_edge, high_edge, axis):
    count = lax.axis_size(axis)
    even = lax.axis_index(axis) % 2 == 0
    inner = [(i, i ^ 1) for i in range(count - count % 2)]
    outer = [(i, ((i + 1) ^ 1) - 1) for i in range(1, count - 1 + count % 2)]
    a = lax.ppermute(jnp.where(even, high_edge, low_edge), axis, inner)
    b = lax.ppermute(jnp.where(even, low_edge, high_edge), axis, outer)
    return jnp.where(even, b, a), jnp.where(even, a, b)


def pack(a, b):
    return jnp.concatenate([a.reshape(-1, a.shape[-1]), b.reshape(-1, b.shape[-1])])


def unpack(buffer, a_shape, b_shape):
    rows = a_shape[0] * a_shape[1] * a_shape[2]
    return buffer[:rows].reshape(a_shape), buffer[rows:].reshape(b_shape)


def edges(video, grad, dim):
    size, gsize = video.shape[dim], grad.shape[dim]
    cut = lax.slice_in_dim
    low = cut(video, 0, 2, axis=dim), cut(grad, 0, 1, axis=dim)
    high = cut(video, size - 2, size, axis=dim), cut(grad, gsize - 1, gsize, axis=dim)
    return low, high


def joined(video, grad, low, high, before, after, dim):
    v_before, g_before = unpack(before, low[0].shape, low[1].shape)
    v_after, g_after = unpack(after, low[0].shape, low[1].shape)
    video = jnp.concatenate([v_before, video, v_after], axis=dim)
    return video, jnp.concatenate([g_before, grad, g_after], axis=dim)


def with_halo(video, grad, forward):
    low, high = edges(video, grad, 1)
    before, after = exchange(pack(*low), pack(*high), "row")
    tall, grad = joined(video, grad, low, high, before, after, 1)
    low, high = edges(tall, grad, 2)
    before, after = exchange(pack(*low), pack(*high), "col")
    (before, after), ready = lax.optimization_barrier(((before, after), forward(tall)))
    return joined(tall, grad, low, high, before, after, 2) + (ready,)


def direct_scatter(x, axis, beside):
    count, mine = lax.axis_size(axis), lax.axis_index(axis)
    share = x.shape[0] // count
    got = []
    for mask in range(1, count):
        sent = part(x, mine ^ mask, share).astype(BF)
        got.append(lax.ppermute(sent, axis, flip(axis, mask)))
    got, beside = lax.optimization_barrier((got, beside))
    total = part(x, mine, share)
    for term in got:
        total = total + term.astype(F32)
    return total, beside


def line_sum(x, axis):
    bits, mine = lax.axis_size(axis).bit_length() - 1, lax.axis_index(axis)
    for bit in range(bits - 1):
        side, half = (mine >> bit) & 1, x.shape[0] // 2
        sent = part(x, 1 - side, half).astype(BF)
        x = part(x, side, half) + lax.ppermute(sent, axis, flip(axis, 1 << bit)).astype(F32)
    x = lax.reduce_precision(x, 8, 7)
    got = lax.ppermute(x.astype(BF), axis, flip(axis, 1 << (bits - 1)))
    y = (x + got.astype(F32)).astype(BF)
    for bit in reversed(range(bits - 1)):
        got = lax.ppermute(y, axis, flip(axis, 1 << bit))
        low = ((mine >> bit) & 1) == 0
        y = jnp.where(low, jnp.stack([y, got]), jnp.stack([got, y])).reshape(-1, y.shape[-1])
    return y


def direct_gather(y, axis):
    count, mine = lax.axis_size(axis), lax.axis_index(axis)
    share = y.shape[0]
    whole = jnp.zeros((count * share,) + y.shape[1:], y.dtype)
    whole = lax.dynamic_update_slice_in_dim(whole, y, mine * share, 0)
    for mask in range(1, count):
        got = lax.ppermute(y, axis, flip(axis, mask))
        whole = lax.dynamic_update_slice_in_dim(whole, got, (mine ^ mask) * share, 0)
    return whole


def join_kernel(core, mine, other, main_grad, down_grad):
    split, end = mine.shape[0], main_grad.shape[0]
    for which, low, high in ((0, mine, other), (1, other, mine)):

        @pl.when(core[0] == which)
        def _():
            main_grad[0:split] = low[...].astype(F32)
            main_grad[split:end] = high[0 : end - split].astype(F32)
            down_grad[...] = high[end - split :].astype(F32)


def reduce_all(kept, sent, beside, main_rows):
    half, core = kept.shape[0], lax.axis_index("clip")
    swap = flip("clip", 1)
    x = kept + lax.ppermute(sent, "clip", swap).astype(F32)
    x, beside = direct_scatter(x, "row", beside)
    y = direct_gather(line_sum(x, "col"), "row")
    other = lax.ppermute(y, "clip", swap)
    vmem = pl.BlockSpec(memory_space=pltpu.VMEM)
    main_grad, down_grad = pl.pallas_call(
        join_kernel,
        out_shape=(
            jax.ShapeDtypeStruct((main_rows, x.shape[1]), F32),
            jax.ShapeDtypeStruct((2 * half - main_rows, x.shape[1]), F32),
        ),
        in_specs=[pl.BlockSpec(memory_space=pltpu.SMEM), vmem, vmem],
        out_specs=(vmem, vmem),
        compiler_params=pltpu.CompilerParams(vmem_limit_bytes=8 << 20),
    )(core[None], y, other)
    return main_grad, down_grad, beside


def dot(a, b):
    return lax.dot_general(a, b, (((1,), (0,)), ((), ())), preferred_element_type=F32)


LEFT = 8


GROUP = 4
PAIR = 8


def forward_kernel(tall, kernel_main, pre, w_main, x32, x_taps):
    frames, in_rows, cols, channels = tall.shape
    own = (in_rows - 2) * cols
    for kt in range(3):
        for tap in range(9):
            rows_at, cols_at = tap * channels, kt * channels
            w_main[rows_at : rows_at + channels, cols_at : cols_at + channels] = kernel_main[9 * kt + tap]
    pre[0:2] = jnp.zeros((2,) + pre.shape[1:], F32)
    x32[...] = jnp.zeros_like(x32)

    def group(i, carry):
        lines = []
        for g in range(GROUP):
            t = i * GROUP + g
            x32[:, LEFT : LEFT + cols, :] = tall[t].astype(F32)
            for kw in range(3):
                shifted = x32[:, pl.ds(LEFT - 1 + kw, cols), :].astype(BF)
                x_taps[g, kw] = shifted.reshape(in_rows * cols, channels)
            taps = [x_taps[g, kw, kh * cols : kh * cols + own] for kh in range(3) for kw in range(3)]
            lines.append(jnp.concatenate(taps, axis=1))
        out = dot(jnp.concatenate(lines, axis=0), w_main[...])
        parts = [out[:, k * channels : (k + 1) * channels] for k in range(3)]
        for g in range(GROUP):
            t, here = i * GROUP + g, slice(g * own, (g + 1) * own)
            pre[t + 2] = parts[0][here]
            pre[t + 1] += parts[1][here]
            pre[t] += parts[2][here]

        @pl.when(i == 0)
        def _():
            pre[0] += parts[0][:own] + parts[1][:own]
            pre[1] += parts[0][:own]

        return carry

    lax.fori_loop(0, frames // GROUP, group, 0)


def causal(out, channels):
    first, second, third = (out[..., k * channels : (k + 1) * channels] for k in range(3))
    frames = out.shape[-2]
    start = first[..., 0:1, :]
    back_two = jnp.concatenate([start, start, first[..., : frames - 2, :]], axis=-2)
    back_one = jnp.concatenate([second[..., 0:1, :], second[..., : frames - 1, :]], axis=-2)
    return third + back_one + back_two


def pointwise(v, grad, mask):
    logistic = 1.0 / (1.0 + jnp.exp(-v))
    out = (v * logistic * mask).astype(BF)
    back = (grad * logistic * (1.0 + v * (1.0 - logistic)) * mask).astype(BF)
    return out.astype(F32), back.astype(F32)


def main_kernel(
    flags, wide, grad_wide, pre, w_main, w_grad, w_down, latent_grad,
    kept, sent, grad_taps, latent,
    x32, side32, x_taps, v32, fix, l32, act_grad, side_back, side_act, side_grad, pre_grad, act,
    act_taps, grad_t, total, down_total,
):
    frames, in_rows, in_cols, channels = wide.shape
    rows, cols = in_rows - 4, in_cols - 4
    ext = rows + 2
    half_rows, half_cols = rows // 2, cols // 2
    own = ext * cols
    grad_t[frames:] = jnp.zeros((2,) + grad_t.shape[1:], BF)
    l32[...] = jnp.zeros_like(l32)
    count = flags[0]
    low_row, high_row = flags[1].astype(F32), flags[2].astype(F32)
    low_col, high_col = flags[3].astype(F32), flags[4].astype(F32)

    def spread(t, carry):
        x32[:, 0:in_cols, :] = wide[t].astype(F32)
        for kw in range(3):
            shifted = x32[:, pl.ds(1 + kw, cols), :].astype(BF)
            x_taps[t, kw] = shifted.reshape(in_rows * cols, channels)
            side32[kw, :, pl.ds(t, 1), :] = x32[:, kw : kw + 1, :]
            side32[kw, :, pl.ds(frames + t, 1), :] = x32[:, cols + 1 + kw : cols + 2 + kw, :]
        l32[:, 0 : half_cols + 2, :] = grad_wide[t].astype(F32)
        near = [l32[:, pl.ds(dq, 16), :].astype(BF) for dq in range(2)]
        grads = jnp.concatenate(
            [
                near[dq][dp : dp + half_rows + 1].reshape((half_rows + 1) * 16, channels)
                for dp in (1, 0)
                for dq in (1, 0)
            ],
            axis=1,
        )
        classes = dot(grads, w_grad[...])
        for p in range(half_rows + 1):
            for odd in range(2):
                line = classes[p * 16 : p * 16 + half_cols + 1]
                row = 2 * p + 1 - odd
                even_part = line[:, 2 * odd * channels : (2 * odd + 1) * channels]
                odd_part = line[:, (2 * odd + 1) * channels : (2 * odd + 2) * channels]
                act_grad[t, row, pl.ds(LEFT, half_cols + 1, stride=2), :] = even_part
                act_grad[t, row, pl.ds(LEFT - 1, half_cols + 1, stride=2), :] = odd_part
        side_back[:, pl.ds(t, 1), :] = act_grad[t, :, LEFT - 1 : LEFT, :]
        side_back[:, pl.ds(frames + t, 1), :] = act_grad[t, :, LEFT + cols : LEFT + cols + 1, :]
        return carry

    lax.fori_loop(0, frames, spread, 0)

    side_lhs = jnp.concatenate(
        [
            side32[kw, kh : kh + ext].reshape(ext * 2 * frames, channels).astype(BF)
            for kh in range(3)
            for kw in range(3)
        ],
        axis=1,
    )
    side_pre = dot(side_lhs, w_main[...]).reshape(ext, 2, frames, 3 * channels)
    side_pre = causal(side_pre, channels).reshape(ext, 2 * frames, channels)
    for side in range(2):
        at = side * frames
        lhs = jnp.concatenate(
            [
                side32[1, kh : kh + ext, at : at + frames].reshape(ext * frames, channels).astype(BF)
                for kh in range(3)
            ],
            axis=1,
        )
        weights_here = jnp.concatenate(
            [
                w_main[(3 * kh + 2 * side) * channels : (3 * kh + 2 * side + 1) * channels]
                for kh in range(3)
            ],
            axis=0,
        )
        out = dot(lhs, weights_here).reshape(ext, frames, 3 * channels)
        fix[:, at : at + frames, :] = causal(out, channels)

    def row_mask(width):
        place = lax.broadcasted_iota(jnp.int32, (ext, width, channels), 0)
        return jnp.where(place == 0, low_row, jnp.where(place == ext - 1, high_row, 1.0))

    place = lax.broadcasted_iota(jnp.int32, (ext, 2 * frames, channels), 1)
    side_mask = jnp.where(place < frames, low_col, high_col)
    side_mask = jnp.where(place % frames < count, side_mask, 0.0) * row_mask(2 * frames)
    side_act[...], side_grad[...] = pointwise(side_pre, side_back[...], side_mask)

    def frame(t, carry):
        live = jnp.where(t < count, 1.0, 0.0).astype(F32)
        last = frames + t
        v32[...] = pre[t].reshape(ext, cols, channels)
        v32[:, 0:1, :] += fix[:, pl.ds(t, 1), :]
        v32[:, cols - 1 : cols, :] += fix[:, pl.ds(last, 1), :]
        own_act, own_grad = pointwise(
            v32[...], act_grad[t, :, LEFT : LEFT + cols, :], row_mask(cols) * live
        )
        act[:, LEFT : LEFT + cols, :] = own_act
        act[:, LEFT + cols : LEFT + cols + 1, :] = side_act[:, pl.ds(last, 1), :]
        pre_grad[:, LEFT : LEFT + cols, :] = own_grad
        pre_grad[:, LEFT - 1 : LEFT, :] = side_grad[:, pl.ds(t, 1), :]
        pre_grad[:, LEFT + cols : LEFT + cols + 1, :] = side_grad[:, pl.ds(last, 1), :]
        inner = own_grad.reshape(own, channels)[cols : cols + rows * cols]
        grad_t[t] = inner.T.astype(BF)
        for kw in range(3):
            shifted = pre_grad[:, pl.ds(LEFT - 1 + kw, cols), :].astype(BF)
            grad_taps[t, kw] = shifted.reshape(own, channels)
        for a in range(3):
            for b in range(3):
                tap = jnp.concatenate(
                    [
                        act[2 * i + a + 1, pl.ds(LEFT + b, half_cols, stride=2), :]
                        for i in range(half_rows)
                    ],
                    axis=0,
                ).astype(BF)
                at = (3 * a + b) * channels
                act_taps[t, :, at : at + channels] = tap
        return carry

    lax.fori_loop(0, frames, frame, 0)

    flat = act_taps[...].reshape(frames * half_rows * half_cols, 9 * channels)
    latent[...] = dot(flat, w_down[...]).astype(BF)
    down = dot(latent_grad[...].astype(F32).T.astype(BF), flat)
    for tap in range(9):
        down_total[tap] = down[:, tap * channels : (tap + 1) * channels]

    def patches(s):
        taps = [
            x_taps[s, kw, (kh + 1) * cols : (kh + 1 + rows) * cols]
            for kh in range(3)
            for kw in range(3)
        ]
        return jnp.concatenate(taps, axis=1)

    total[:, 0:channels] = jnp.zeros((9, channels, channels), F32)
    early = dot(grad_t[0:2].reshape(2 * channels, rows * cols), patches(0))
    for tap in range(9):
        block = early[:, tap * channels : (tap + 1) * channels]
        total[tap, channels : 2 * channels] = block[:channels]
        total[tap, 2 * channels :] = block[:channels] + block[channels:]

    def weights(i, carry):
        left = [grad_t[pl.ds(PAIR * i + g, 3)].reshape(3 * channels, rows * cols) for g in range(PAIR)]
        right = [patches(PAIR * i + g) for g in range(PAIR)]
        out = dot(jnp.concatenate(left, axis=1), jnp.concatenate(right, axis=0))
        for tap in range(9):
            total[tap] += out[:, tap * channels : (tap + 1) * channels]
        return carry

    lax.fori_loop(0, frames // PAIR, weights, 0)

    def emit(low, high):
        def tap_out(tap, carry):
            at = pl.multiple_of(tap * channels, channels)
            after = pl.multiple_of((9 + tap) * channels, channels)
            low[pl.ds(at, channels), :] = total[tap, 2 * channels :].T.astype(low.dtype)
            low[pl.ds(after, channels), :] = total[tap, channels : 2 * channels].T.astype(low.dtype)
            high[pl.ds(at, channels), :] = total[tap, 0:channels].T.astype(high.dtype)
            high[pl.ds(after, channels), :] = down_total[tap].T.astype(high.dtype)
            return carry

        lax.fori_loop(0, 9, tap_out, 0)

    @pl.when(flags[5] == 0)
    def _():
        emit(kept, sent)

    @pl.when(flags[5] == 1)
    def _():
        emit(sent, kept)


def back_kernel(grad_taps, kernel_main, video_grad, w_back, total):
    frames, _, own, channels = grad_taps.shape
    inner = video_grad.shape[1]
    cols = (own - inner) // 2
    total[0:2] = jnp.zeros((2,) + total.shape[1:], F32)
    for kt in range(3):
        for tap in range(9):
            rows_at, cols_at = tap * channels, kt * channels
            block = kernel_main[9 * kt + 8 - tap].astype(F32).T.astype(BF)
            w_back[rows_at : rows_at + channels, cols_at : cols_at + channels] = block

    def group(i, carry):
        lines = []
        for t in range(GROUP):
            taps = [
                grad_taps[i * GROUP + t, kw, kh * cols : kh * cols + inner]
                for kh in range(3)
                for kw in range(3)
            ]
            lines.append(jnp.concatenate(taps, axis=1))
        out = dot(jnp.concatenate(lines, axis=0), w_back[...])
        parts = [out[:, k * channels : (k + 1) * channels] for k in range(3)]
        for g in range(GROUP):
            t, here = i * GROUP + g, slice(g * inner, (g + 1) * inner)
            total[t + 2] = parts[2][here]
            total[t + 1] += parts[1][here]
            total[t] += parts[0][here]
        return carry

    lax.fori_loop(0, frames // GROUP, group, 0)
    video_grad[0] = (total[0] + total[1] + total[2]).astype(BF)

    def store(t, carry):
        video_grad[t] = total[t + 2].astype(BF)
        return carry

    lax.fori_loop(1, frames, store, 0)


def grad_matrix(kernel_down):
    k = jnp.swapaxes(kernel_down, 2, 3)
    zero = jnp.zeros_like(k[0, 0])
    return jnp.concatenate(
        [
            jnp.concatenate([k[0, 0], zero, zero, zero], axis=1),
            jnp.concatenate([k[0, 2], k[0, 1], zero, zero], axis=1),
            jnp.concatenate([k[2, 0], zero, k[1, 0], zero], axis=1),
            jnp.concatenate([k[2, 2], k[2, 1], k[1, 2], k[1, 1]], axis=1),
        ]
    )


def on_device(video, frame_counts, kernel_main, kernel_down, latent_grad):
    _, frames, rows, cols, channels = video.shape
    ext = rows + 2
    own, outs = ext * cols, frames * rows * cols // 4
    pixels = frames * rows * cols
    vmem = pl.BlockSpec(memory_space=pltpu.VMEM)
    taps = kernel_main.reshape(27, channels, channels)

    def forward(tall):
        return pl.pallas_call(
            forward_kernel,
            out_shape=(
                jax.ShapeDtypeStruct((frames + 2, own, channels), F32),
                jax.ShapeDtypeStruct((9 * channels, 3 * channels), BF),
            ),
            in_specs=[vmem] * 2,
            out_specs=(vmem,) * 2,
            scratch_shapes=[
                pltpu.VMEM((rows + 4, cols + 16, channels), F32),
                pltpu.VMEM((GROUP, 3, (rows + 4) * cols, channels), BF),
            ],
            compiler_params=pltpu.CompilerParams(vmem_limit_bytes=16 << 20),
            cost_estimate=pl.CostEstimate(
                flops=2 * 27 * frames * own * channels * channels,
                bytes_accessed=4 << 20,
                transcendentals=0,
            ),
        )(tall, taps)

    wide, grad_wide, (pre, w_main) = with_halo(video[0], latent_grad[0], forward)
    row, col = lax.axis_index("row"), lax.axis_index("col")
    flags = jnp.stack(
        [
            frame_counts[0],
            (row > 0).astype(jnp.int32),
            (row < lax.axis_size("row") - 1).astype(jnp.int32),
            (col > 0).astype(jnp.int32),
            (col < lax.axis_size("col") - 1).astype(jnp.int32),
            lax.axis_index("clip"),
        ]
    )
    w_down = kernel_down.reshape(9 * channels, channels)
    kept, sent, grad_taps, latent = pl.pallas_call(
        main_kernel,
        out_shape=(
            jax.ShapeDtypeStruct((18 * channels, channels), F32),
            jax.ShapeDtypeStruct((18 * channels, channels), BF),
            jax.ShapeDtypeStruct((frames, 3, own, channels), BF),
            jax.ShapeDtypeStruct((outs, channels), BF),
        ),
        in_specs=[pl.BlockSpec(memory_space=pltpu.SMEM)] + [vmem] * 7,
        out_specs=(vmem,) * 4,
        scratch_shapes=[
            pltpu.VMEM((rows + 4, cols + 8, channels), F32),
            pltpu.VMEM((3, rows + 4, 2 * frames, channels), F32),
            pltpu.VMEM((frames, 3, (rows + 4) * cols, channels), BF),
            pltpu.VMEM((ext, cols, channels), F32),
            pltpu.VMEM((ext, 2 * frames, channels), F32),
            pltpu.VMEM((rows // 2 + 2, 24, channels), F32),
            pltpu.VMEM((frames, ext, cols + 16, channels), F32),
            pltpu.VMEM((ext, 2 * frames, channels), F32),
            pltpu.VMEM((ext, 2 * frames, channels), F32),
            pltpu.VMEM((ext, 2 * frames, channels), F32),
            pltpu.VMEM((ext, cols + 16, channels), F32),
            pltpu.VMEM((ext, cols + 16, channels), F32),
            pltpu.VMEM((frames, rows * cols // 4, 9 * channels), BF),
            pltpu.VMEM((frames + 2, channels, rows * cols), BF),
            pltpu.VMEM((9, 3 * channels, channels), F32),
            pltpu.VMEM((9, channels, channels), F32),
        ],
        compiler_params=pltpu.CompilerParams(vmem_limit_bytes=24 << 20),
        cost_estimate=pl.CostEstimate(
            flops=2 * 40 * pixels * channels * channels,
            bytes_accessed=12 << 20,
            transcendentals=pixels * channels,
        ),
    )(
        flags,
        wide,
        grad_wide,
        pre,
        w_main,
        grad_matrix(kernel_down),
        w_down,
        latent_grad.reshape(outs, channels),
    )
    video_grad = pl.pallas_call(
        back_kernel,
        out_shape=jax.ShapeDtypeStruct((frames, rows * cols, channels), BF),
        in_specs=[vmem] * 2,
        out_specs=vmem,
        scratch_shapes=[
            pltpu.VMEM((9 * channels, 3 * channels), BF),
            pltpu.VMEM((frames + 2, rows * cols, channels), F32),
        ],
        compiler_params=pltpu.CompilerParams(vmem_limit_bytes=12 << 20),
        cost_estimate=pl.CostEstimate(
            flops=2 * 27 * pixels * channels * channels,
            bytes_accessed=4 << 20,
            transcendentals=0,
        ),
    )(grad_taps, taps)
    main_grad, down_grad, video_grad = reduce_all(kept, sent, video_grad, 27 * channels)
    main_grad = main_grad.reshape(kernel_main.shape)
    down_grad = down_grad.reshape(kernel_down.shape)
    return (latent.reshape(latent_grad.shape), video_grad.reshape(video.shape), main_grad, down_grad)


def solution(mesh):
    tiles = P("clip", None, "row", "col", None)
    return jax.shard_map(
        on_device,
        mesh=mesh,
        in_specs=(tiles, P("clip"), P(), P(), tiles),
        out_specs=(tiles, tiles, P(), P()),
        check_vma=False,
    )
```

time: 87.6 us -> 76.4 us (0.87)
  starting transfers between devices: 27.4 us -> 18.9 us
  Pallas kernels: 24.5 us -> 20 us
  local copies, waits for them, and re-layouts: 5.76 us -> 7.56 us
  other arithmetic: 2.88 us -> 1.47 us
  waiting for transfers between devices: 25.1 us -> 26.4 us
    pallas_call x1, Pallas kernels: 17.9 us -> 10.7 us  [on_device(): pl.pallas_call(main_kernel, out_shape=(jax.ShapeDtypeStruct((18 * channel...]
    ppermute x5, waiting for transfers between devices: 8.2 us -> 3.89 us  [the longest x1 2.21 us: reduce_all(): x = kept + lax.ppermute(sent, 'clip', swap).astype(F32)]
    pallas_call x0 -> x1, Pallas kernels: none -> 3.67 us  [forward(): pl.pallas_call(forward_kernel, out_shape=(jax.ShapeDtypeStruct((frames +...]
    ppermute x1, waiting for transfers between devices: 2.68 us -> 5.51 us  [line_sum(): got = lax.ppermute(x.astype(BF), axis, flip(axis, 1 << bits - 1))]
    ppermute x1, starting transfers between devices: 2.67 us -> 0.07 us  [line_sum(): got = lax.ppermute(x.astype(BF), axis, flip(axis, 1 << bits - 1))]
    ppermute x3, starting transfers between devices: 5.74 us -> 3.55 us  [direct_scatter(): got.append(lax.ppermute(sent, axis, flip(axis, mask)))]
    unnamed x15 -> x21, local copies, waits for them, and re-layouts: 3.57 us -> 5.26 us
    ppermute x1, starting transfers between devices: 1.66 us -> 0.08 us  [line_sum(): lax.ppermute(sent, axis, flip(axis, 1 << bit)).astype(F32)]
  transfers between devices with their start and end apart: 15 -> 15, of which waited for: 13 -> 9; matrix products, arithmetic and copies ran while one was open for 2% -> 2% of each run, Pallas kernels for 6% -> 10%
where the time goes in v1:
time: 76.4 us; the launch traced here: 76.1 us
  waiting for transfers between devices  26.4 us (35%)
  Pallas kernels  20 us (26%)
  starting transfers between devices  18.9 us (25%)
  local copies, waits for them, and re-layouts  7.56 us (10%)
  between operations  1.76 us (2%)
  other arithmetic  1.47 us (2%)
    pallas_call x1, Pallas kernels, on_device(): pl.pallas_call(main_kernel, out_shape=(jax.ShapeDtypeStruct((18 * channel...  10.7 us
    ppermute x2, starting transfers between devices, exchange(): a = lax.ppermute(jnp.where(even, high_edge, low_edge), axis, inner)  10.2 us
    ppermute x1, waiting for transfers between devices, line_sum(): got = lax.ppermute(x.astype(BF), axis, flip(axis, 1 << bits - 1))  5.51 us
    unnamed x21, local copies, waits for them, and re-layouts  5.26 us
    ppermute x3, waiting for transfers between devices, direct_gather(): got = lax.ppermute(y, axis, flip(axis, mask))  4.5 us
    ppermute x1, waiting for transfers between devices, line_sum(): got = lax.ppermute(y, axis, flip(axis, 1 << bit))  4.33 us
    ppermute x1, waiting for transfers between devices, line_sum(): lax.ppermute(sent, axis, flip(axis, 1 << bit)).astype(F32)  4.33 us
    pallas_call x1, Pallas kernels, on_device(): pl.pallas_call(back_kernel, out_shape=jax.ShapeDtypeStruct((frames, rows...  4.06 us
  transfers between devices with their start and end apart: 15, of which 9 were waited for; matrix products, arithmetic and copies ran while one was open for 2% of the time, Pallas kernels for 10%

profile of v1, /device:TPU:0, one launch (start us, length us, event | category | flops | bytes accessed | tf_op | source)
XLA Modules:
  0.0 76.1 jit_solution(13099416987464889367)
XLA Ops:
  0.6 0.0 copy-start.9
  0.7 0.9 %fusion.7 = (bf16[8,2,16,128]{3,2,1,0:T(8,128)(2,1)S(1)}, bf16[8,2,16,128]{3,2,1,0:T(8,128)(2,1)S(1)}) fusion(bf16[8,16,16,128]{3,2,1,0:T(8,128)(2,1)} %bitcast.59), kind=kLoop, calls=%fused_computation.52 | loop fusion | bytes 262144 | tf_op jit(solution)/shard_map/slice | solution.py:42
  1.6 0.7 slice_bitcast_fusion.12
  2.4 0.7 collective-permute-start
  3.1 5.7 %collective-permute-start.1 = (bf16[320,128]{1,0:T(8,128)(2,1)S(1)}, bf16[320,128]{1,0:T(8,128)(2,1)S(1)}, u32[]{:S(2)}, u32[]{:S(2)}) collective-permute-start(bf16[320,128]{1,0:T(8,128)(2,1)S(1)} %get-tuple-element.61), channel_id=1, source_target_pairs={{0,4},{4,0},{8,12},{12,8},{1,5},{5,1},{9,13},{13,9},{2,6},{6,2},{1... | collective-permute-start | bytes 245768 | tf_op jit(solution)/shard_map/ppermute | solution.py:25
  8.8 1.2 %copy.12 = bf16[3,3,128,128]{2,3,1,0:T(8,128)(2,1)S(1)} copy(bf16[3,3,128,128]{3,2,1,0:T(8,128)(2,1)} %param.8) | data formatting | bytes 589824 | tf_op args[3]
  10.0 0.0 copy-start
  10.1 0.0 copy-start.2
  10.9 0.1 stack.53.flags
  10.9 0.0 collective-permute-done
  10.9 1.7 %collective-permute-done.1 = bf16[320,128]{1,0:T(8,128)(2,1)S(1)} collective-permute-done((bf16[320,128]{1,0:T(8,128)(2,1)S(1)}, bf16[320,128]{1,0:T(8,128)(2,1)S(1)}, u32[]{:S(2)}, u32[]{:S(2)}) %collective-permute-start.1) | collective-permute-done | bytes 81952 | tf_op jit(solution)/shard_map/ppermute | solution.py:25
  12.7 0.0 copy-done.9
  12.7 0.1 pad_maximum_fusion.1.tall
  12.8 0.1 fusion.6
  12.9 0.0 copy-done
  12.9 0.2 maximum_reduce_fusion
  13.3 0.7 collective-permute-start.2
  13.9 4.5 %collective-permute-start.3 = (bf16[400,128]{1,0:T(8,128)(2,1)S(1)}, bf16[400,128]{1,0:T(8,128)(2,1)S(1)}, u32[]{:S(2)}, u32[]{:S(2)}) collective-permute-start(bf16[400,128]{1,0:T(8,128)(2,1)S(1)} %get-tuple-element.56), channel_id=1, source_target_pairs={{0,1},{1,0},{2,3},{3,2},{4,5},{5,4},{6,7},{7,6},{8,9},{9,8},{10,11... | collective-permute-start | bytes 307208 | tf_op jit(solution)/shard_map/ppermute | solution.py:25
  18.4 0.0 copy-done.2
  18.4 3.7 %shard_map.84 = (f32[10,288,128]{2,1,0:T(8,128)S(1)}, bf16[1152,384]{1,0:T(8,128)(2,1)S(1)}) custom-call(bf16[8,20,16,128]{3,2,1,0:T(8,128)(2,1)S(1)} %pad_maximum_fusion.1.tall, bf16[27,128,128]{2,1,0:T(8,128)(2,1)S(1)} %bitcast.57), custom_call_target="tpu_custom_call" | custom-call | flops 2038431744 | bytes 4194304 | tf_op jit(solution)/shard_map/pallas_call | solution.py:436
  22.1 0.0 copy-start.5
  22.1 1.1 %copy-done.5 = f32[10,288,128]{2,1,0:T(8,128)} copy-done((f32[10,288,128]{2,1,0:T(8,128)}, f32[10,288,128]{2,1,0:T(8,128)S(1)}, u32[]{:S(2)}) %copy-start.5) | copy-done | bytes 1474584
  23.2 0.9 %copy-done.7 = bf16[1152,384]{1,0:T(8,128)(2,1)} copy-done((bf16[1152,384]{1,0:T(8,128)(2,1)}, bf16[1152,384]{1,0:T(8,128)(2,1)S(1)}, u32[]{:S(2)}) %copy-start.7) | copy-done | bytes 884760
  24.1 0.0 copy-start.1
  24.1 0.0 collective-permute-done.2
  24.1 0.0 collective-permute-done.3
  24.2 0.0 copy-start.6
  24.2 0.0 copy-start.8
  24.2 0.2 pad_maximum_fusion.2.grad_wide
  24.5 0.6 pad_maximum_fusion.wide
  25.0 0.0 copy-done.1
  25.1 0.6 copy-done.6
  25.6 0.2 copy-done.8
  25.9 10.7 %shard_map.85 = (f32[2304,128]{1,0:T(8,128)S(1)}, bf16[2304,128]{1,0:T(8,128)(2,1)}, bf16[8,3,288,128]{3,2,1,0:T(8,128)(2,1)S(1)}, bf16[512,128]{1,0:T(8,128)(2,1)}) custom-call(s32[6]{0:T(128)S(1)} %stack.53.flags, bf16[8,20,20,128]{3,2,1,0:T(8,128)(2,1)S(1)} %pad_maximum_fusion.wide, bf16[8,10,10,128]{3,2,1,0:T(8,128)(2,1)S(1)} %pad_maximum_fusion.2.grad_wide, ...), custom_call_target="tpu_custom_call" | custom-call | flops 2684354560 | bytes 12582912 | tf_op jit(solution)/shard_map/pallas_call | solution.py:469
  36.6 1.2 %copy-done.3 = bf16[8,3,288,128]{3,2,1,0:T(8,128)(2,1)} copy-done((bf16[8,3,288,128]{3,2,1,0:T(8,128)(2,1)}, bf16[8,3,288,128]{3,2,1,0:T(8,128)(2,1)S(1)}, u32[]{:S(2)}) %copy-start.3) | copy-done | bytes 1769496
  37.8 0.0 collective-permute-start.4
  37.8 2.2 %collective-permute-done.4 = bf16[2304,128]{1,0:T(8,128)(2,1)S(1)} collective-permute-done((bf16[2304,128]{1,0:T(8,128)(2,1)}, bf16[2304,128]{1,0:T(8,128)(2,1)S(1)}, u32[]{:S(2)}, u32[]{:S(2)}) %collective-permute-start.4) | collective-permute-done | bytes 589856 | tf_op jit(solution)/shard_map/ppermute | solution.py:119
  40.0 0.1 convert_add_fusion
  40.1 0.1 dynamic-slice_convert_fusion
  40.2 0.7 collective-permute-start.5
  40.9 1.4 %collective-permute-start.6 = (bf16[576,128]{1,0:T(8,128)(2,1)S(1)}, bf16[576,128]{1,0:T(8,128)(2,1)S(1)}, u32[]{:S(2)}, u32[]{:S(2)}) collective-permute-start(bf16[576,128]{1,0:T(8,128)(2,1)S(1)} %get-tuple-element.39), channel_id=1, source_target_pairs={{0,8},{4,12},{8,0},{12,4},{1,9},{5,13},{9,1},{13,5},{2,10},{6,14},... | collective-permute-start | bytes 442376 | tf_op jit(solution)/shard_map/ppermute | solution.py:70
  42.2 1.5 %collective-permute-start.7 = (bf16[576,128]{1,0:T(8,128)(2,1)S(1)}, bf16[576,128]{1,0:T(8,128)(2,1)S(1)}, u32[]{:S(2)}, u32[]{:S(2)}) collective-permute-start(bf16[576,128]{1,0:T(8,128)(2,1)S(1)} %get-tuple-element.38), channel_id=1, source_target_pairs={{0,12},{4,8},{8,4},{12,0},{1,13},{5,9},{9,5},{13,1},{2,14},{6,10},... | collective-permute-start | bytes 442376 | tf_op jit(solution)/shard_map/ppermute | solution.py:70
  43.7 0.0 copy-done.4
  43.7 4.1 %shard_map.86 = bf16[8,256,128]{2,1,0:T(8,128)(2,1)} custom-call(bf16[8,3,288,128]{3,2,1,0:T(8,128)(2,1)S(1)} %copy-done.4, bf16[27,128,128]{2,1,0:T(8,128)(2,1)S(1)} %bitcast.58), custom_call_target="tpu_custom_call" | custom-call | flops 1811939328 | bytes 4194304 | tf_op jit(solution)/shard_map/pallas_call | solution.py:513
  47.8 0.0 collective-permute-done.5
  47.8 1.8 %collective-permute-done.6 = bf16[576,128]{1,0:T(8,128)(2,1)S(1)} collective-permute-done((bf16[576,128]{1,0:T(8,128)(2,1)S(1)}, bf16[576,128]{1,0:T(8,128)(2,1)S(1)}, u32[]{:S(2)}, u32[]{:S(2)}) %collective-permute-start.6) | collective-permute-done | bytes 147488 | tf_op jit(solution)/shard_map/ppermute | solution.py:70
  49.6 0.0 collective-permute-done.7
  49.6 0.1 convert_add_fusion.1
  49.7 0.1 collective-permute-start.8
  49.8 4.3 %collective-permute-done.8 = bf16[288,128]{1,0:T(8,128)(2,1)S(1)} collective-permute-done((bf16[288,128]{1,0:T(8,128)(2,1)S(1)}, bf16[288,128]{1,0:T(8,128)(2,1)S(1)}, u32[]{:S(2)}, u32[]{:S(2)}) %collective-permute-start.8) | collective-permute-done | bytes 73760 | tf_op jit(solution)/shard_map/ppermute | solution.py:83
  54.2 0.1 collective-permute-start.9
  54.2 5.5 %collective-permute-done.9 = bf16[288,128]{1,0:T(8,128)(2,1)S(1)} collective-permute-done((bf16[288,128]{1,0:T(8,128)(2,1)S(1)}, bf16[288,128]{1,0:T(8,128)(2,1)S(1)}, u32[]{:S(2)}, u32[]{:S(2)}) %collective-permute-start.9) | collective-permute-done | bytes 73760 | tf_op jit(solution)/shard_map/ppermute | solution.py:85
  59.8 0.1 collective-permute-start.10
  59.9 4.3 %collective-permute-done.10 = bf16[288,128]{1,0:T(8,128)(2,1)S(1)} collective-permute-done((bf16[288,128]{1,0:T(8,128)(2,1)S(1)}, bf16[288,128]{1,0:T(8,128)(2,1)S(1)}, u32[]{:S(2)}, u32[]{:S(2)}) %collective-permute-start.10) | collective-permute-done | bytes 73760 | tf_op jit(solution)/shard_map/ppermute | solution.py:88
  64.2 1.5 %collective-permute-start.11 = (bf16[576,128]{1,0:T(8,128)(2,1)S(1)}, bf16[576,128]{1,0:T(8,128)(2,1)S(1)}, u32[]{:S(2)}, u32[]{:S(2)}) collective-permute-start(bf16[576,128]{1,0:T(8,128)(2,1)S(1)} %bitcast.67), channel_id=1, source_target_pairs={{0,4},{4,0},{8,12},{12,8},{1,5},{5,1},{9,13},{13,9},{2,6},{6,2},{1... | collective-permute-start | bytes 442376 | tf_op jit(solution)/shard_map/ppermute | solution.py:100
  65.7 0.6 collective-permute-start.12
  66.3 1.5 %collective-permute-start.13 = (bf16[576,128]{1,0:T(8,128)(2,1)S(1)}, bf16[576,128]{1,0:T(8,128)(2,1)S(1)}, u32[]{:S(2)}, u32[]{:S(2)}) collective-permute-start(bf16[576,128]{1,0:T(8,128)(2,1)S(1)} %bitcast.69), channel_id=1, source_target_pairs={{0,12},{4,8},{8,4},{12,0},{1,13},{5,9},{9,5},{13,1},{2,14},{6,10},... | collective-permute-start | bytes 442376 | tf_op jit(solution)/shard_map/ppermute | solution.py:100
  67.8 0.1 broadcast_in_dim.8
  67.9 1.5 %collective-permute-done.11 = bf16[576,128]{1,0:T(8,128)(2,1)S(1)} collective-permute-done((bf16[576,128]{1,0:T(8,128)(2,1)S(1)}, bf16[576,128]{1,0:T(8,128)(2,1)S(1)}, u32[]{:S(2)}, u32[]{:S(2)}) %collective-permute-start.11) | collective-permute-done | bytes 147488 | tf_op jit(solution)/shard_map/ppermute | solution.py:100
  69.5 3.0 %collective-permute-done.12 = bf16[576,128]{1,0:T(8,128)(2,1)S(1)} collective-permute-done((bf16[576,128]{1,0:T(8,128)(2,1)S(1)}, bf16[576,128]{1,0:T(8,128)(2,1)S(1)}, u32[]{:S(2)}, u32[]{:S(2)}) %collective-permute-start.12) | collective-permute-done | bytes 147488 | tf_op jit(solution)/shard_map/ppermute | solution.py:100
  72.5 0.0 collective-permute-done.13
  72.5 0.1 collective-permute-start.14
  72.6 2.0 %collective-permute-done.14.other = bf16[2304,128]{1,0:T(8,128)(2,1)S(1)} collective-permute-done((bf16[2304,128]{1,0:T(8,128)(2,1)S(1)}, bf16[2304,128]{1,0:T(8,128)(2,1)S(1)}, u32[]{:S(2)}, u32[]{:S(2)}) %collective-permute-start.14) | collective-permute-done | bytes 589856 | tf_op jit(solution)/shard_map/ppermute | solution.py:122
  74.6 1.6 %shard_map.87 = (f32[3456,128]{1,0:T(8,128)}, f32[1152,128]{1,0:T(8,128)}) custom-call(s32[1]{0:T(128)} %bitcast.4.core, bf16[2304,128]{1,0:T(8,128)(2,1)S(1)} %constant_dynamic-update-slice_fusion.mine, bf16[2304,128]{1,0:T(8,128)(2,1)S(1)} %collective-permute-done.14.other), custom_call_target="tpu_custom_call" | custom-call | tf_op jit(solution)/shard_map/pallas_call | solution.py:124
  (30 shorter events, 0.5 us)
Async XLA Ops:
  0.6 12.0 %copy-start.9 = (bf16[1,8,16,16,128]{4,3,2,1,0:T(8,128)(2,1)S(1)}, bf16[1,8,16,16,128]{4,3,2,1,0:T(8,128)(2,1)}, u32[]{:S(2)}) copy-start(bf16[1,8,16,16,128]{4,3,2,1,0:T(8,128)(2,1)} %param.5) | copy-start | bytes 1572868
  2.4 8.6 %collective-permute-start = (bf16[320,128]{1,0:T(8,128)(2,1)S(1)}, bf16[320,128]{1,0:T(8,128)(2,1)S(1)}, u32[]{:S(2)}, u32[]{:S(2)}) collective-permute-start(bf16[320,128]{1,0:T(8,128)(2,1)S(1)} %get-tuple-element.60), channel_id=1, source_target_pairs={{4,8},{8,4},{5,9},{9,5},{6,10},{10,6},{7,11},{11,7},{20,24},{24,20... | collective-permute-start | bytes 245768 | tf_op jit(solution)/shard_map/ppermute | solution.py:26
  3.1 9.6 %collective-permute-start.1 = (bf16[320,128]{1,0:T(8,128)(2,1)S(1)}, bf16[320,128]{1,0:T(8,128)(2,1)S(1)}, u32[]{:S(2)}, u32[]{:S(2)}) collective-permute-start(bf16[320,128]{1,0:T(8,128)(2,1)S(1)} %get-tuple-element.61), channel_id=1, source_target_pairs={{0,4},{4,0},{8,12},{12,8},{1,5},{5,1},{9,13},{13,9},{2,6},{6,2},{1... | collective-permute-start | bytes 245768 | tf_op jit(solution)/shard_map/ppermute | solution.py:25
  10.0 2.9 %copy-start = (bf16[1,8,8,8,128]{4,3,2,1,0:T(8,128)(2,1)S(1)}, bf16[1,8,8,8,128]{4,3,2,1,0:T(8,128)(2,1)}, u32[]{:S(2)}) copy-start(bf16[1,8,8,8,128]{4,3,2,1,0:T(8,128)(2,1)} %param.9) | copy-start | bytes 393220
  10.1 8.3 %copy-start.2 = (bf16[3,3,3,128,128]{4,3,2,1,0:T(8,128)(2,1)S(1)}, bf16[3,3,3,128,128]{4,3,2,1,0:T(8,128)(2,1)}, u32[]{:S(2)}) copy-start(bf16[3,3,3,128,128]{4,3,2,1,0:T(8,128)(2,1)} %param.7) | copy-start | bytes 2654212
  13.3 10.8 %collective-permute-start.2 = (bf16[400,128]{1,0:T(8,128)(2,1)S(1)}, bf16[400,128]{1,0:T(8,128)(2,1)S(1)}, u32[]{:S(2)}, u32[]{:S(2)}) collective-permute-start(bf16[400,128]{1,0:T(8,128)(2,1)S(1)} %get-tuple-element.57), channel_id=1, source_target_pairs={{1,2},{2,1},{5,6},{6,5},{9,10},{10,9},{13,14},{14,13},{17,18},{18,... | collective-permute-start | bytes 307208 | tf_op jit(solution)/shard_map/ppermute | solution.py:26
  13.9 10.2 %collective-permute-start.3 = (bf16[400,128]{1,0:T(8,128)(2,1)S(1)}, bf16[400,128]{1,0:T(8,128)(2,1)S(1)}, u32[]{:S(2)}, u32[]{:S(2)}) collective-permute-start(bf16[400,128]{1,0:T(8,128)(2,1)S(1)} %get-tuple-element.56), channel_id=1, source_target_pairs={{0,1},{1,0},{2,3},{3,2},{4,5},{5,4},{6,7},{7,6},{8,9},{9,8},{10,11... | collective-permute-start | bytes 307208 | tf_op jit(solution)/shard_map/ppermute | solution.py:25
  22.1 1.1 %copy-start.5 = (f32[10,288,128]{2,1,0:T(8,128)}, f32[10,288,128]{2,1,0:T(8,128)S(1)}, u32[]{:S(2)}) copy-start(f32[10,288,128]{2,1,0:T(8,128)S(1)} %get-tuple-element.24.pre) | copy-start | bytes 4423684
  23.2 0.9 %copy-start.7 = (bf16[1152,384]{1,0:T(8,128)(2,1)}, bf16[1152,384]{1,0:T(8,128)(2,1)S(1)}, u32[]{:S(2)}) copy-start(bf16[1152,384]{1,0:T(8,128)(2,1)S(1)} %get-tuple-element.25.w_main) | copy-start | bytes 2654212
  24.1 1.0 %copy-start.1 = (bf16[3,3,128,128]{3,2,1,0:T(8,128)(2,1)S(1)}, bf16[3,3,128,128]{3,2,1,0:T(8,128)(2,1)}, u32[]{:S(2)}) copy-start(bf16[3,3,128,128]{3,2,1,0:T(8,128)(2,1)} %param.8) | copy-start | bytes 884740
  24.2 1.4 %copy-start.6 = (f32[10,288,128]{2,1,0:T(8,128)S(1)}, f32[10,288,128]{2,1,0:T(8,128)}, u32[]{:S(2)}) copy-start(f32[10,288,128]{2,1,0:T(8,128)} %copy-done.5) | copy-start | bytes 4423684
  24.2 1.6 %copy-start.8 = (bf16[1152,384]{1,0:T(8,128)(2,1)S(1)}, bf16[1152,384]{1,0:T(8,128)(2,1)}, u32[]{:S(2)}) copy-start(bf16[1152,384]{1,0:T(8,128)(2,1)} %copy-done.7) | copy-start | bytes 2654212
  36.6 1.2 %copy-start.3 = (bf16[8,3,288,128]{3,2,1,0:T(8,128)(2,1)}, bf16[8,3,288,128]{3,2,1,0:T(8,128)(2,1)S(1)}, u32[]{:S(2)}) copy-start(bf16[8,3,288,128]{3,2,1,0:T(8,128)(2,1)S(1)} %get-tuple-element.29.grad_taps) | copy-start | bytes 5308420
  37.8 2.2 %collective-permute-start.4 = (bf16[2304,128]{1,0:T(8,128)(2,1)}, bf16[2304,128]{1,0:T(8,128)(2,1)S(1)}, u32[]{:S(2)}, u32[]{:S(2)}) collective-permute-start(bf16[2304,128]{1,0:T(8,128)(2,1)} %get-tuple-element.28), channel_id=1, source_target_pairs={{0,16},{16,0},{1,17},{17,1},{2,18},{18,2},{3,19},{19,3},{4,20},{20... | collective-permute-start | bytes 1769480 | tf_op jit(solution)/shard_map/ppermute | solution.py:119
  40.0 3.7 %copy-start.4 = (bf16[8,3,288,128]{3,2,1,0:T(8,128)(2,1)S(1)}, bf16[8,3,288,128]{3,2,1,0:T(8,128)(2,1)}, u32[]{:S(2)}) copy-start(bf16[8,3,288,128]{3,2,1,0:T(8,128)(2,1)} %copy-done.3) | copy-start | bytes 5308420
  40.2 7.6 %collective-permute-start.5 = (bf16[576,128]{1,0:T(8,128)(2,1)S(1)}, bf16[576,128]{1,0:T(8,128)(2,1)S(1)}, u32[]{:S(2)}, u32[]{:S(2)}) collective-permute-start(bf16[576,128]{1,0:T(8,128)(2,1)S(1)} %get-tuple-element.40), channel_id=1, source_target_pairs={{0,4},{4,0},{8,12},{12,8},{1,5},{5,1},{9,13},{13,9},{2,6},{6,2},{1... | collective-permute-start | bytes 442376 | tf_op jit(solution)/shard_map/ppermute | solution.py:70
  40.9 8.8 %collective-permute-start.6 = (bf16[576,128]{1,0:T(8,128)(2,1)S(1)}, bf16[576,128]{1,0:T(8,128)(2,1)S(1)}, u32[]{:S(2)}, u32[]{:S(2)}) collective-permute-start(bf16[576,128]{1,0:T(8,128)(2,1)S(1)} %get-tuple-element.39), channel_id=1, source_target_pairs={{0,8},{4,12},{8,0},{12,4},{1,9},{5,13},{9,1},{13,5},{2,10},{6,14},... | collective-permute-start | bytes 442376 | tf_op jit(solution)/shard_map/ppermute | solution.py:70
  42.2 7.4 %collective-permute-start.7 = (bf16[576,128]{1,0:T(8,128)(2,1)S(1)}, bf16[576,128]{1,0:T(8,128)(2,1)S(1)}, u32[]{:S(2)}, u32[]{:S(2)}) collective-permute-start(bf16[576,128]{1,0:T(8,128)(2,1)S(1)} %get-tuple-element.38), channel_id=1, source_target_pairs={{0,12},{4,8},{8,4},{12,0},{1,13},{5,9},{9,5},{13,1},{2,14},{6,10},... | collective-permute-start | bytes 442376 | tf_op jit(solution)/shard_map/ppermute | solution.py:70
  49.7 4.4 %collective-permute-start.8 = (bf16[288,128]{1,0:T(8,128)(2,1)S(1)}, bf16[288,128]{1,0:T(8,128)(2,1)S(1)}, u32[]{:S(2)}, u32[]{:S(2)}) collective-permute-start(bf16[288,128]{1,0:T(8,128)(2,1)S(1)} %dynamic-slice_convert_fusion.3), channel_id=1, source_target_pairs={{0,1},{1,0},{2,3},{3,2},{4,5},{5,4},{6,7},{7,6},{8,9},{9,8},{10,11... | collective-permute-start | bytes 221192 | tf_op jit(solution)/shard_map/ppermute | solution.py:83
  54.2 5.6 %collective-permute-start.9 = (bf16[288,128]{1,0:T(8,128)(2,1)S(1)}, bf16[288,128]{1,0:T(8,128)(2,1)S(1)}, u32[]{:S(2)}, u32[]{:S(2)}) collective-permute-start(bf16[288,128]{1,0:T(8,128)(2,1)S(1)} %fusion.4), channel_id=1, source_target_pairs={{0,2},{1,3},{2,0},{3,1},{4,6},{5,7},{6,4},{7,5},{8,10},{9,11},{10,... | collective-permute-start | bytes 221192 | tf_op jit(solution)/shard_map/ppermute | solution.py:85
  59.8 4.4 %collective-permute-start.10 = (bf16[288,128]{1,0:T(8,128)(2,1)S(1)}, bf16[288,128]{1,0:T(8,128)(2,1)S(1)}, u32[]{:S(2)}, u32[]{:S(2)}) collective-permute-start(bf16[288,128]{1,0:T(8,128)(2,1)S(1)} %add_convert_fusion), channel_id=1, source_target_pairs={{0,1},{1,0},{2,3},{3,2},{4,5},{5,4},{6,7},{7,6},{8,9},{9,8},{10,11... | collective-permute-start | bytes 221192 | tf_op jit(solution)/shard_map/ppermute | solution.py:88
  64.2 5.2 %collective-permute-start.11 = (bf16[576,128]{1,0:T(8,128)(2,1)S(1)}, bf16[576,128]{1,0:T(8,128)(2,1)S(1)}, u32[]{:S(2)}, u32[]{:S(2)}) collective-permute-start(bf16[576,128]{1,0:T(8,128)(2,1)S(1)} %bitcast.67), channel_id=1, source_target_pairs={{0,4},{4,0},{8,12},{12,8},{1,5},{5,1},{9,13},{13,9},{2,6},{6,2},{1... | collective-permute-start | bytes 442376 | tf_op jit(solution)/shard_map/ppermute | solution.py:100
  65.7 6.7 %collective-permute-start.12 = (bf16[576,128]{1,0:T(8,128)(2,1)S(1)}, bf16[576,128]{1,0:T(8,128)(2,1)S(1)}, u32[]{:S(2)}, u32[]{:S(2)}) collective-permute-start(bf16[576,128]{1,0:T(8,128)(2,1)S(1)} %bitcast.68), channel_id=1, source_target_pairs={{0,8},{4,12},{8,0},{12,4},{1,9},{5,13},{9,1},{13,5},{2,10},{6,14},... | collective-permute-start | bytes 442376 | tf_op jit(solution)/shard_map/ppermute | solution.py:100
  66.3 6.2 %collective-permute-start.13 = (bf16[576,128]{1,0:T(8,128)(2,1)S(1)}, bf16[576,128]{1,0:T(8,128)(2,1)S(1)}, u32[]{:S(2)}, u32[]{:S(2)}) collective-permute-start(bf16[576,128]{1,0:T(8,128)(2,1)S(1)} %bitcast.69), channel_id=1, source_target_pairs={{0,12},{4,8},{8,4},{12,0},{1,13},{5,9},{9,5},{13,1},{2,14},{6,10},... | collective-permute-start | bytes 442376 | tf_op jit(solution)/shard_map/ppermute | solution.py:100
  72.5 2.1 %collective-permute-start.14 = (bf16[2304,128]{1,0:T(8,128)(2,1)S(1)}, bf16[2304,128]{1,0:T(8,128)(2,1)S(1)}, u32[]{:S(2)}, u32[]{:S(2)}) collective-permute-start(bf16[2304,128]{1,0:T(8,128)(2,1)S(1)} %constant_dynamic-update-slice_fusion.mine), channel_id=1, source_target_pairs={{0,16},{16,0},{1,17},{17,1},{2,18},{18,2},{3,19},{19,3},{4,20},{20... | collective-permute-start | bytes 1769480 | tf_op jit(solution)/shard_map/ppermute | solution.py:122

commit v2 on v1

--- a/solution.py
+++ b/solution.py
@@ -61,16 +61,31 @@
     return joined(tall, grad, low, high, before, after, 2) + (ready,)
 
 
-def direct_scatter(x, axis, beside):
+def combine_kernel(index, kept, got, own, *sends):
+    share = own.shape[0]
+    for mask in range(1 + len(sends)):
+        here = pl.ds(pl.multiple_of((index[0] ^ mask) * share, share), share)
+        piece = kept[here, :] + got[here, :].astype(F32)
+        if mask:
+            sends[mask - 1][...] = piece.astype(BF)
+        else:
+            own[...] = piece
+
+
+def direct_scatter(kept, got, axis, beside):
     count, mine = lax.axis_size(axis), lax.axis_index(axis)
-    share = x.shape[0] // count
-    got = []
-    for mask in range(1, count):
-        sent = part(x, mine ^ mask, share).astype(BF)
-        got.append(lax.ppermute(sent, axis, flip(axis, mask)))
-    got, beside = lax.optimization_barrier((got, beside))
-    total = part(x, mine, share)
-    for term in got:
+    shape = (kept.shape[0] // count, kept.shape[1])
+    vmem = pl.BlockSpec(memory_space=pltpu.VMEM)
+    total, *sends = pl.pallas_call(
+        combine_kernel,
+        out_shape=(jax.ShapeDtypeStruct(shape, F32),) + (jax.ShapeDtypeStruct(shape, BF),) * (count - 1),
+        in_specs=[pl.BlockSpec(memory_space=pltpu.SMEM), vmem, vmem],
+        out_specs=(vmem,) * count,
+        compiler_params=pltpu.CompilerParams(vmem_limit_bytes=8 << 20),
+    )(mine[None], kept, got)
+    terms = [lax.ppermute(sends[mask - 1], axis, flip(axis, mask)) for mask in range(1, count)]
+    terms, beside = lax.optimization_barrier((terms, beside))
+    for term in terms:
         total = total + term.astype(F32)
     return total, beside
 
@@ -102,35 +117,55 @@
     return whole
 
 
-def join_kernel(core, mine, other, main_grad, down_grad):
-    split, end = mine.shape[0], main_grad.shape[0]
-    for which, low, high in ((0, mine, other), (1, other, mine)):
-
-        @pl.when(core[0] == which)
-        def _():
-            main_grad[0:split] = low[...].astype(F32)
-            main_grad[split:end] = high[0 : end - split].astype(F32)
-            down_grad[...] = high[end - split :].astype(F32)
+def half_kernel(which, half, *refs):
+    main_grad, down_grad, turned, sems = refs[-4:]
+    channels = half.shape[1]
+    run = half.shape[0] // 2
+    for j in range(2):
+        for at in range(j * run, (j + 1) * run, channels):
+            turned[at : at + channels, :] = half[at : at + channels, :].astype(F32).T
+        source = turned.at[j * run : (j + 1) * run]
+        for h in range(2):
+            place = 2 * h + j
+            target = down_grad if place == 3 else main_grad.at[place * run : (place + 1) * run]
+
+            @pl.when(which[0] == h)
+            def _():
+                pltpu.make_async_copy(source, target, sems.at[j]).start()
+
+    for j in range(2):
+        source = turned.at[j * run : (j + 1) * run]
+        pltpu.make_async_copy(source, down_grad, sems.at[j]).wait()
+
+
+def place_half(which, half, grads, shapes):
+    vmem, anywhere = (pl.BlockSpec(memory_space=m) for m in (pltpu.VMEM, pl.ANY))
+    return pl.pallas_call(
+        half_kernel,
+        out_shape=shapes,
+        in_specs=[pl.BlockSpec(memory_space=pltpu.SMEM), vmem] + [anywhere] * len(grads),
+        out_specs=(anywhere, anywhere),
+        input_output_aliases={2 + i: i for i in range(len(grads))},
+        scratch_shapes=[pltpu.VMEM(half.shape, F32), pltpu.SemaphoreType.DMA((2,))],
+        compiler_params=pltpu.CompilerParams(vmem_limit_bytes=8 << 20),
+        cost_estimate=pl.CostEstimate(flops=0, bytes_accessed=4 << 20, transcendentals=0),
+    )(which[None], half, *grads)
 
 
 def reduce_all(kept, sent, beside, main_rows):
     half, core = kept.shape[0], lax.axis_index("clip")
     swap = flip("clip", 1)
-    x = kept + lax.ppermute(sent, "clip", swap).astype(F32)
-    x, beside = direct_scatter(x, "row", beside)
+    got = lax.ppermute(sent, "clip", swap)
+    x, beside = direct_scatter(kept, got, "row", beside)
     y = direct_gather(line_sum(x, "col"), "row")
     other = lax.ppermute(y, "clip", swap)
-    vmem = pl.BlockSpec(memory_space=pltpu.VMEM)
-    main_grad, down_grad = pl.pallas_call(
-        join_kernel,
-        out_shape=(
-            jax.ShapeDtypeStruct((main_rows, x.shape[1]), F32),
-            jax.ShapeDtypeStruct((2 * half - main_rows, x.shape[1]), F32),
-        ),
-        in_specs=[pl.BlockSpec(memory_space=pltpu.SMEM), vmem, vmem],
-        out_specs=(vmem, vmem),
-        compiler_params=pltpu.CompilerParams(vmem_limit_bytes=8 << 20),
-    )(core[None], y, other)
+    shapes = (
+        jax.ShapeDtypeStruct((main_rows, y.shape[1]), F32),
+        jax.ShapeDtypeStruct((2 * half - main_rows, y.shape[1]), F32),
+    )
+    grads = place_half(core, y, (), shapes)
+    other, grads = lax.optimization_barrier((other, grads))
+    main_grad, down_grad = place_half(1 - core, other, grads, shapes)
     return main_grad, down_grad, beside
 
 
@@ -145,21 +180,23 @@
 PAIR = 8
 
 
-def forward_kernel(tall, kernel_main, pre, w_main, x32, x_taps):
-    frames, in_rows, cols, channels = tall.shape
-    own = (in_rows - 2) * cols
+def side_by_side(kernel_main, w_main):
+    channels = kernel_main.shape[1]
     for kt in range(3):
         for tap in range(9):
             rows_at, cols_at = tap * channels, kt * channels
             w_main[rows_at : rows_at + channels, cols_at : cols_at + channels] = kernel_main[9 * kt + tap]
-    pre[0:2] = jnp.zeros((2,) + pre.shape[1:], F32)
+
+
+def forward_kernel(tall, kernel_main, pre, w_main, x32, x_taps):
+    frames, in_rows, cols, channels = tall.shape
+    own = (in_rows - 2) * cols
+    side_by_side(kernel_main, w_main)
     x32[...] = jnp.zeros_like(x32)
-
-    def group(i, carry):
+    for first in range(0, frames, GROUP):
         lines = []
         for g in range(GROUP):
-            t = i * GROUP + g
-            x32[:, LEFT : LEFT + cols, :] = tall[t].astype(F32)
+            x32[:, LEFT : LEFT + cols, :] = tall[first + g].astype(F32)
             for kw in range(3):
                 shifted = x32[:, pl.ds(LEFT - 1 + kw, cols), :].astype(BF)
                 x_taps[g, kw] = shifted.reshape(in_rows * cols, channels)
@@ -168,19 +205,16 @@
         out = dot(jnp.concatenate(lines, axis=0), w_main[...])
         parts = [out[:, k * channels : (k + 1) * channels] for k in range(3)]
         for g in range(GROUP):
-            t, here = i * GROUP + g, slice(g * own, (g + 1) * own)
-            pre[t + 2] = parts[0][here]
-            pre[t + 1] += parts[1][here]
-            pre[t] += parts[2][here]
-
-        @pl.when(i == 0)
-        def _():
-            pre[0] += parts[0][:own] + parts[1][:own]
-            pre[1] += parts[0][:own]
-
-        return carry
-
-    lax.fori_loop(0, frames // GROUP, group, 0)
+            t, here = first + g, slice(g * own, (g + 1) * own)
+            if t == 0:
+                pre[0] = parts[0][here] + parts[1][here] + parts[2][here]
+                pre[1] = parts[0][here] + parts[1][here]
+            else:
+                pre[t] += parts[2][here]
+                if t + 1 < frames:
+                    pre[t + 1] += parts[1][here]
+            if t + 2 < frames:
+                pre[t + 2] = parts[0][here]
 
 
 def causal(out, channels):
@@ -200,9 +234,9 @@
 
 
 def main_kernel(
-    flags, wide, grad_wide, pre, w_main, w_grad, w_down, latent_grad,
-    kept, sent, grad_taps, latent,
-    x32, side32, x_taps, v32, fix, l32, act_grad, side_back, side_act, side_grad, pre_grad, act,
+    flags, wide, grad_wide, pre, kernel_main, w_grad, w_down, latent_grad,
+    kept, sent, own_out, side_out, latent,
+    w_main, x32, side32, x_taps, v32, fix, l32, act_grad, side_back, side_act, act,
     act_taps, grad_t, total, down_total,
 ):
     frames, in_rows, in_cols, channels = wide.shape
@@ -212,6 +246,7 @@
     own = ext * cols
     grad_t[frames:] = jnp.zeros((2,) + grad_t.shape[1:], BF)
     l32[...] = jnp.zeros_like(l32)
+    side_by_side(kernel_main, w_main)
     count = flags[0]
     low_row, high_row = flags[1].astype(F32), flags[2].astype(F32)
     low_col, high_col = flags[3].astype(F32), flags[4].astype(F32)
@@ -284,7 +319,8 @@
     place = lax.broadcasted_iota(jnp.int32, (ext, 2 * frames, channels), 1)
     side_mask = jnp.where(place < frames, low_col, high_col)
     side_mask = jnp.where(place % frames < count, side_mask, 0.0) * row_mask(2 * frames)
-    side_act[...], side_grad[...] = pointwise(side_pre, side_back[...], side_mask)
+    side_act[...], side_grad = pointwise(side_pre, side_back[...], side_mask)
+    side_out[...] = side_grad.astype(BF)
 
     def frame(t, carry):
         live = jnp.where(t < count, 1.0, 0.0).astype(F32)
@@ -297,14 +333,9 @@
         )
         act[:, LEFT : LEFT + cols, :] = own_act
         act[:, LEFT + cols : LEFT + cols + 1, :] = side_act[:, pl.ds(last, 1), :]
-        pre_grad[:, LEFT : LEFT + cols, :] = own_grad
-        pre_grad[:, LEFT - 1 : LEFT, :] = side_grad[:, pl.ds(t, 1), :]
-        pre_grad[:, LEFT + cols : LEFT + cols + 1, :] = side_grad[:, pl.ds(last, 1), :]
+        own_out[t] = own_grad.reshape(own, channels).astype(BF)
         inner = own_grad.reshape(own, channels)[cols : cols + rows * cols]
         grad_t[t] = inner.T.astype(BF)
-        for kw in range(3):
-            shifted = pre_grad[:, pl.ds(LEFT - 1 + kw, cols), :].astype(BF)
-            grad_taps[t, kw] = shifted.reshape(own, channels)
         for a in range(3):
             for b in range(3):
                 tap = jnp.concatenate(
@@ -355,10 +386,10 @@
         def tap_out(tap, carry):
             at = pl.multiple_of(tap * channels, channels)
             after = pl.multiple_of((9 + tap) * channels, channels)
-            low[pl.ds(at, channels), :] = total[tap, 2 * channels :].T.astype(low.dtype)
-            low[pl.ds(after, channels), :] = total[tap, channels : 2 * channels].T.astype(low.dtype)
-            high[pl.ds(at, channels), :] = total[tap, 0:channels].T.astype(high.dtype)
-            high[pl.ds(after, channels), :] = down_total[tap].T.astype(high.dtype)
+            low[pl.ds(at, channels), :] = total[tap, 2 * channels :].astype(low.dtype)
+            low[pl.ds(after, channels), :] = total[tap, channels : 2 * channels].astype(low.dtype)
+            high[pl.ds(at, channels), :] = total[tap, 0:channels].astype(high.dtype)
+            high[pl.ds(after, channels), :] = down_total[tap].astype(high.dtype)
             return carry
 
         lax.fori_loop(0, 9, tap_out, 0)
@@ -372,10 +403,12 @@
         emit(sent, kept)
 
 
-def back_kernel(grad_taps, kernel_main, video_grad, w_back, total):
-    frames, _, own, channels = grad_taps.shape
+def back_kernel(own_grad, side_grad, kernel_main, video_grad, w_back, total, side32, g32, grad_taps):
+    frames, own, channels = own_grad.shape
     inner = video_grad.shape[1]
     cols = (own - inner) // 2
+    ext = own // cols
+    side32[...] = side_grad[...].astype(F32)
     total[0:2] = jnp.zeros((2,) + total.shape[1:], F32)
     for kt in range(3):
         for tap in range(9):
@@ -385,9 +418,16 @@
 
     def group(i, carry):
         lines = []
-        for t in range(GROUP):
+        for g in range(GROUP):
+            t = i * GROUP + g
+            g32[:, LEFT : LEFT + cols, :] = own_grad[t].astype(F32).reshape(ext, cols, channels)
+            g32[:, LEFT - 1 : LEFT, :] = side32[:, pl.ds(t, 1), :]
+            g32[:, LEFT + cols : LEFT + cols + 1, :] = side32[:, pl.ds(frames + t, 1), :]
+            for kw in range(3):
+                shifted = g32[:, pl.ds(LEFT - 1 + kw, cols), :].astype(BF)
+                grad_taps[g, kw] = shifted.reshape(own, channels)
             taps = [
-                grad_taps[i * GROUP + t, kw, kh * cols : kh * cols + inner]
+                grad_taps[g, kw, kh * cols : kh * cols + inner]
                 for kh in range(3)
                 for kw in range(3)
             ]
@@ -436,12 +476,12 @@
         return pl.pallas_call(
             forward_kernel,
             out_shape=(
-                jax.ShapeDtypeStruct((frames + 2, own, channels), F32),
-                jax.ShapeDtypeStruct((9 * channels, 3 * channels), BF),
+                jax.ShapeDtypeStruct((frames, own, channels), F32),
             ),
             in_specs=[vmem] * 2,
-            out_specs=(vmem,) * 2,
+            out_specs=(vmem,),
             scratch_shapes=[
+                pltpu.VMEM((9 * channels, 3 * channels), BF),
                 pltpu.VMEM((rows + 4, cols + 16, channels), F32),
                 pltpu.VMEM((GROUP, 3, (rows + 4) * cols, channels), BF),
             ],
@@ -453,7 +493,7 @@
             ),
         )(tall, taps)
 
-    wide, grad_wide, (pre, w_main) = with_halo(video[0], latent_grad[0], forward)
+    wide, grad_wide, (pre,) = with_halo(video[0], latent_grad[0], forward)
     row, col = lax.axis_index("row"), lax.axis_index("col")
     flags = jnp.stack(
         [
@@ -466,17 +506,19 @@
         ]
     )
     w_down = kernel_down.reshape(9 * channels, channels)
-    kept, sent, grad_taps, latent = pl.pallas_call(
+    kept, sent, own_grad, side_grad, latent = pl.pallas_call(
         main_kernel,
         out_shape=(
             jax.ShapeDtypeStruct((18 * channels, channels), F32),
             jax.ShapeDtypeStruct((18 * channels, channels), BF),
-            jax.ShapeDtypeStruct((frames, 3, own, channels), BF),
+            jax.ShapeDtypeStruct((frames, own, channels), BF),
+            jax.ShapeDtypeStruct((ext, 2 * frames, channels), BF),
             jax.ShapeDtypeStruct((outs, channels), BF),
         ),
         in_specs=[pl.BlockSpec(memory_space=pltpu.SMEM)] + [vmem] * 7,
-        out_specs=(vmem,) * 4,
+        out_specs=(vmem,) * 5,
         scratch_shapes=[
+            pltpu.VMEM((9 * channels, 3 * channels), BF),
             pltpu.VMEM((rows + 4, cols + 8, channels), F32),
             pltpu.VMEM((3, rows + 4, 2 * frames, channels), F32),
             pltpu.VMEM((frames, 3, (rows + 4) * cols, channels), BF),
@@ -486,8 +528,6 @@
             pltpu.VMEM((frames, ext, cols + 16, channels), F32),
             pltpu.VMEM((ext, 2 * frames, channels), F32),
             pltpu.VMEM((ext, 2 * frames, channels), F32),
-            pltpu.VMEM((ext, 2 * frames, channels), F32),
-            pltpu.VMEM((ext, cols + 16, channels), F32),
             pltpu.VMEM((ext, cols + 16, channels), F32),
             pltpu.VMEM((frames, rows * cols // 4, 9 * channels), BF),
             pltpu.VMEM((frames + 2, channels, rows * cols), BF),
@@ -505,7 +545,7 @@
         wide,
         grad_wide,
         pre,
-        w_main,
+        taps,
         grad_matrix(kernel_down),
         w_down,
         latent_grad.reshape(outs, channels),
@@ -513,11 +553,14 @@
     video_grad = pl.pallas_call(
         back_kernel,
         out_shape=jax.ShapeDtypeStruct((frames, rows * cols, channels), BF),
-        in_specs=[vmem] * 2,
+        in_specs=[vmem] * 3,
         out_specs=vmem,
         scratch_shapes=[
             pltpu.VMEM((9 * channels, 3 * channels), BF),
             pltpu.VMEM((frames + 2, rows * cols, channels), F32),
+            pltpu.VMEM((ext, 2 * frames, channels), F32),
+            pltpu.VMEM((ext, cols + 16, channels), F32),
+            pltpu.VMEM((GROUP, 3, own, channels), BF),
         ],
         compiler_params=pltpu.CompilerParams(vmem_limit_bytes=12 << 20),
         cost_estimate=pl.CostEstimate(
@@ -525,7 +568,7 @@
             bytes_accessed=4 << 20,
             transcendentals=0,
         ),
-    )(grad_taps, taps)
+    )(own_grad, side_grad, taps)
     main_grad, down_grad, video_grad = reduce_all(kept, sent, video_grad, 27 * channels)
     main_grad = main_grad.reshape(kernel_main.shape)
     down_grad = down_grad.reshape(kernel_down.shape)

time: 76.4 us -> 73.2 us (0.958)
  waiting for transfers between devices: 26.4 us -> 19.1 us
  starting transfers between devices: 18.9 us -> 24.8 us
  local copies, waits for them, and re-layouts: 7.56 us -> 5.72 us
    ppermute x1, starting transfers between devices: 0.08 us -> 4.45 us  [line_sum(): lax.ppermute(sent, axis, flip(axis, 1 << bit)).astype(F32)]
    ppermute x2, starting transfers between devices: 10.2 us -> 7.38 us  [exchange(): a = lax.ppermute(jnp.where(even, high_edge, low_edge), axis, inner)]
    ppermute x1, starting transfers between devices: 0.07 us -> 2.68 us  [line_sum(): got = lax.ppermute(y, axis, flip(axis, 1 << bit))]
    ppermute x1, waiting for transfers between devices: 4.33 us -> 2.33 us  [line_sum(): got = lax.ppermute(y, axis, flip(axis, 1 << bit))]
    ppermute x1, waiting for transfers between devices: 4.33 us -> 2.33 us  [line_sum(): lax.ppermute(sent, axis, flip(axis, 1 << bit)).astype(F32)]
    ppermute x1, waiting for transfers between devices: 5.51 us -> 3.67 us  [line_sum(): got = lax.ppermute(x.astype(BF), axis, flip(axis, 1 << bits - 1))]
    unnamed x21 -> x17, local copies, waits for them, and re-layouts: 5.26 us -> 3.52 us
    ppermute x1, starting transfers between devices: 0.07 us -> 1.68 us  [line_sum(): got = lax.ppermute(x.astype(BF), axis, flip(axis, 1 << bits - 1))]
  transfers between devices with their start and end apart: 15 -> 15, of which waited for: 9 -> 10; matrix products, arithmetic and copies ran while one was open for 2% -> 2% of each run, Pallas kernels for 10% -> 12%
where the time goes in v2:
time: 73.2 us; the launch traced here: 72.9 us
  starting transfers between devices  24.8 us (34%)
  Pallas kernels  20 us (27%)
  waiting for transfers between devices  19.1 us (26%)
  local copies, waits for them, and re-layouts  5.72 us (8%)
  between operations  1.89 us (3%)
  other arithmetic  1.39 us (2%)
    pallas_call x1, Pallas kernels, on_device(): pl.pallas_call(main_kernel, out_shape=(jax.ShapeDtypeStruct((18 * channel...  9.72 us
    ppermute x2, starting transfers between devices, exchange(): a = lax.ppermute(jnp.where(even, high_edge, low_edge), axis, inner)  7.38 us
    ppermute x3, waiting for transfers between devices, direct_gather(): got = lax.ppermute(y, axis, flip(axis, mask))  4.49 us
    ppermute x1, starting transfers between devices, line_sum(): lax.ppermute(sent, axis, flip(axis, 1 << bit)).astype(F32)  4.45 us
    pallas_call x1, Pallas kernels, on_device(): pl.pallas_call(back_kernel, out_shape=jax.ShapeDtypeStruct((frames, rows...  4.34 us
    ppermute x1, waiting for transfers between devices, line_sum(): got = lax.ppermute(x.astype(BF), axis, flip(axis, 1 << bits - 1))  3.67 us
    ppermute x3, starting transfers between devices, direct_scatter(): lax.ppermute(sends[mask - 1], axis, flip(axis, mask))  3.55 us
    ppermute x3, starting transfers between devices, direct_gather(): got = lax.ppermute(y, axis, flip(axis, mask))  3.55 us
  transfers between devices with their start and end apart: 15, of which 10 were waited for; matrix products, arithmetic and copies ran while one was open for 2% of the time, Pallas kernels for 12%

profile of v2, /device:TPU:0, one launch (start us, length us, event | category | flops | bytes accessed | tf_op | source)
XLA Modules:
  0.0 72.9 jit_solution(6139603322246689917)
XLA Ops:
  0.6 0.7 %slice_bitcast_fusion.12 = (bf16[64,128]{1,0:T(8,128)(2,1)S(1)}, bf16[64,128]{1,0:T(8,128)(2,1)S(1)}) fusion(bf16[8,8,8,128]{3,2,1,0:T(8,128)(2,1)} %bitcast.54), kind=kLoop, calls=%fused_computation.42 | loop fusion | bytes 65536 | tf_op jit(solution)/shard_map/reshape | solution.py:31
  1.4 0.0 copy-start
  1.4 0.9 %fusion.7 = (bf16[8,2,16,128]{3,2,1,0:T(8,128)(2,1)S(1)}, bf16[8,2,16,128]{3,2,1,0:T(8,128)(2,1)S(1)}) fusion(bf16[8,16,16,128]{3,2,1,0:T(8,128)(2,1)} %bitcast.62), kind=kLoop, calls=%fused_computation.48 | loop fusion | bytes 262144 | tf_op jit(solution)/shard_map/slice | solution.py:42
  2.3 0.0 copy-start.7
  2.4 0.8 %collective-permute-start = (bf16[320,128]{1,0:T(8,128)(2,1)S(1)}, bf16[320,128]{1,0:T(8,128)(2,1)S(1)}, u32[]{:S(2)}, u32[]{:S(2)}) collective-permute-start(bf16[320,128]{1,0:T(8,128)(2,1)S(1)} %get-tuple-element.71), channel_id=1, source_target_pairs={{4,8},{8,4},{5,9},{9,5},{6,10},{10,6},{7,11},{11,7},{20,24},{24,20... | collective-permute-start | bytes 245768 | tf_op jit(solution)/shard_map/ppermute | solution.py:26
  3.2 5.7 %collective-permute-start.1 = (bf16[320,128]{1,0:T(8,128)(2,1)S(1)}, bf16[320,128]{1,0:T(8,128)(2,1)S(1)}, u32[]{:S(2)}, u32[]{:S(2)}) collective-permute-start(bf16[320,128]{1,0:T(8,128)(2,1)S(1)} %get-tuple-element.72), channel_id=1, source_target_pairs={{0,4},{4,0},{8,12},{12,8},{1,5},{5,1},{9,13},{13,9},{2,6},{6,2},{1... | collective-permute-start | bytes 245768 | tf_op jit(solution)/shard_map/ppermute | solution.py:25
  8.9 1.2 %copy.14 = bf16[3,3,128,128]{2,3,1,0:T(8,128)(2,1)S(1)} copy(bf16[3,3,128,128]{3,2,1,0:T(8,128)(2,1)} %param.8) | data formatting | bytes 589824 | tf_op args[3]
  10.2 0.0 copy-start.2
  11.0 0.1 stack.53.flags
  11.0 0.0 collective-permute-done
  11.0 1.7 %collective-permute-done.1 = bf16[320,128]{1,0:T(8,128)(2,1)S(1)} collective-permute-done((bf16[320,128]{1,0:T(8,128)(2,1)S(1)}, bf16[320,128]{1,0:T(8,128)(2,1)S(1)}, u32[]{:S(2)}, u32[]{:S(2)}) %collective-permute-start.1) | collective-permute-done | bytes 81952 | tf_op jit(solution)/shard_map/ppermute | solution.py:25
  12.8 0.0 copy-done
  12.8 0.2 maximum_reduce_fusion
  13.1 0.0 copy-done.7
  13.1 0.1 pad_maximum_fusion.1.tall
  13.2 0.1 fusion.6
  13.4 1.6 %collective-permute-start.3 = (bf16[400,128]{1,0:T(8,128)(2,1)S(1)}, bf16[400,128]{1,0:T(8,128)(2,1)S(1)}, u32[]{:S(2)}, u32[]{:S(2)}) collective-permute-start(bf16[400,128]{1,0:T(8,128)(2,1)S(1)} %get-tuple-element.67), channel_id=1, source_target_pairs={{0,1},{1,0},{2,3},{3,2},{4,5},{5,4},{6,7},{7,6},{8,9},{9,8},{10,11... | collective-permute-start | bytes 307208 | tf_op jit(solution)/shard_map/ppermute | solution.py:25
  15.0 0.7 collective-permute-start.2
  15.7 0.0 copy-done.2
  15.7 3.4 %shard_map.84.pre = f32[8,288,128]{2,1,0:T(8,128)S(1)} custom-call(bf16[8,20,16,128]{3,2,1,0:T(8,128)(2,1)S(1)} %pad_maximum_fusion.1.tall, bf16[27,128,128]{2,1,0:T(8,128)(2,1)S(1)} %bitcast.59), custom_call_target="tpu_custom_call" | custom-call | flops 2038431744 | bytes 4194304 | tf_op jit(solution)/shard_map/pallas_call | solution.py:476
  19.1 0.0 copy-start.3
  19.1 1.0 %copy-done.3 = f32[8,288,128]{2,1,0:T(8,128)} copy-done((f32[8,288,128]{2,1,0:T(8,128)}, f32[8,288,128]{2,1,0:T(8,128)S(1)}, u32[]{:S(2)}) %copy-start.3) | copy-done | bytes 1179672
  20.1 0.0 copy-start.1
  20.1 0.0 collective-permute-done.3
  20.1 0.0 collective-permute-done.2
  20.3 0.0 copy-start.4
  20.3 0.6 pad_maximum_fusion.wide
  20.9 0.2 pad_maximum_fusion.2.grad_wide
  21.1 0.0 copy-done.1
  21.1 0.5 copy-done.4
  21.6 9.7 %shard_map.85 = (f32[2304,128]{1,0:T(8,128)S(1)}, bf16[2304,128]{1,0:T(8,128)(2,1)}, bf16[8,288,128]{2,1,0:T(8,128)(2,1)S(1)}, bf16[18,16,128]{2,1,0:T(8,128)(2,1)S(1)}, bf16[512,128]{1,0:T(8,128)(2,1)}) custom-call(s32[6]{0:T(128)S(1)} %stack.53.flags, bf16[8,20,20,128]{3,2,1,0:T(8,128)(2,1)S(1)} %pad_maximum_fusion.wide, ...), custom_call_target="tpu_custom_call" | custom-call | flops 2684354560 | bytes 12582912 | tf_op jit(solution)/shard_map/pallas_call | solution.py:509
  31.3 0.0 copy-start.5
  31.3 0.8 %copy-done.5 = bf16[8,288,128]{2,1,0:T(8,128)(2,1)} copy-done((bf16[8,288,128]{2,1,0:T(8,128)(2,1)}, bf16[8,288,128]{2,1,0:T(8,128)(2,1)S(1)}, u32[]{:S(2)}) %copy-start.5) | copy-done | bytes 589848
  32.1 0.0 collective-permute-start.4
  32.1 0.0 copy-start.6
  32.1 2.2 %collective-permute-done.4.got = bf16[2304,128]{1,0:T(8,128)(2,1)S(1)} collective-permute-done((bf16[2304,128]{1,0:T(8,128)(2,1)}, bf16[2304,128]{1,0:T(8,128)(2,1)S(1)}, u32[]{:S(2)}, u32[]{:S(2)}) %collective-permute-start.4) | collective-permute-done | bytes 589856 | tf_op jit(solution)/shard_map/ppermute | solution.py:158
  34.3 0.1 shard_map.86
  34.4 0.7 collective-permute-start.5
  35.1 1.4 %collective-permute-start.6 = (bf16[576,128]{1,0:T(8,128)(2,1)S(1)}, bf16[576,128]{1,0:T(8,128)(2,1)S(1)}, u32[]{:S(2)}, u32[]{:S(2)}) collective-permute-start(bf16[576,128]{1,0:T(8,128)(2,1)S(1)} %get-tuple-element.34), channel_id=1, source_target_pairs={{0,8},{4,12},{8,0},{12,4},{1,9},{5,13},{9,1},{13,5},{2,10},{6,14},... | collective-permute-start | bytes 442376 | tf_op jit(solution)/shard_map/ppermute | solution.py:86
  36.5 1.5 %collective-permute-start.7 = (bf16[576,128]{1,0:T(8,128)(2,1)S(1)}, bf16[576,128]{1,0:T(8,128)(2,1)S(1)}, u32[]{:S(2)}, u32[]{:S(2)}) collective-permute-start(bf16[576,128]{1,0:T(8,128)(2,1)S(1)} %get-tuple-element.35), channel_id=1, source_target_pairs={{0,12},{4,8},{8,4},{12,0},{1,13},{5,9},{9,5},{13,1},{2,14},{6,10},... | collective-permute-start | bytes 442376 | tf_op jit(solution)/shard_map/ppermute | solution.py:86
  38.0 0.0 copy-done.6
  38.0 4.3 %shard_map.87 = bf16[8,256,128]{2,1,0:T(8,128)(2,1)} custom-call(bf16[8,288,128]{2,1,0:T(8,128)(2,1)S(1)} %copy-done.6, bf16[18,16,128]{2,1,0:T(8,128)(2,1)S(1)} %get-tuple-element.37.side_grad, bf16[27,128,128]{2,1,0:T(8,128)(2,1)S(1)} %bitcast.61), custom_call_target="tpu_custom_call" | custom-call | flops 1811939328 | bytes 4194304 | tf_op jit(solution)/shard_map/pallas_call | solution.py:553
  42.3 0.0 collective-permute-done.5
  42.3 1.6 %collective-permute-done.6 = bf16[576,128]{1,0:T(8,128)(2,1)S(1)} collective-permute-done((bf16[576,128]{1,0:T(8,128)(2,1)S(1)}, bf16[576,128]{1,0:T(8,128)(2,1)S(1)}, u32[]{:S(2)}, u32[]{:S(2)}) %collective-permute-start.6) | collective-permute-done | bytes 147488 | tf_op jit(solution)/shard_map/ppermute | solution.py:86
  43.9 0.0 collective-permute-done.7
  43.9 0.1 convert_add_fusion
  44.0 4.4 %collective-permute-start.8 = (bf16[288,128]{1,0:T(8,128)(2,1)S(1)}, bf16[288,128]{1,0:T(8,128)(2,1)S(1)}, u32[]{:S(2)}, u32[]{:S(2)}) collective-permute-start(bf16[288,128]{1,0:T(8,128)(2,1)S(1)} %dynamic-slice_convert_fusion), channel_id=1, source_target_pairs={{0,1},{1,0},{2,3},{3,2},{4,5},{5,4},{6,7},{7,6},{8,9},{9,8},{10,11... | collective-permute-start | bytes 221192 | tf_op jit(solution)/shard_map/ppermute | solution.py:98
  48.4 2.3 %collective-permute-done.8 = bf16[288,128]{1,0:T(8,128)(2,1)S(1)} collective-permute-done((bf16[288,128]{1,0:T(8,128)(2,1)S(1)}, bf16[288,128]{1,0:T(8,128)(2,1)S(1)}, u32[]{:S(2)}, u32[]{:S(2)}) %collective-permute-start.8) | collective-permute-done | bytes 73760 | tf_op jit(solution)/shard_map/ppermute | solution.py:98
  50.8 1.7 %collective-permute-start.9 = (bf16[288,128]{1,0:T(8,128)(2,1)S(1)}, bf16[288,128]{1,0:T(8,128)(2,1)S(1)}, u32[]{:S(2)}, u32[]{:S(2)}) collective-permute-start(bf16[288,128]{1,0:T(8,128)(2,1)S(1)} %fusion.4), channel_id=1, source_target_pairs={{0,2},{1,3},{2,0},{3,1},{4,6},{5,7},{6,4},{7,5},{8,10},{9,11},{10,... | collective-permute-start | bytes 221192 | tf_op jit(solution)/shard_map/ppermute | solution.py:100
  52.5 3.7 %collective-permute-done.9 = bf16[288,128]{1,0:T(8,128)(2,1)S(1)} collective-permute-done((bf16[288,128]{1,0:T(8,128)(2,1)S(1)}, bf16[288,128]{1,0:T(8,128)(2,1)S(1)}, u32[]{:S(2)}, u32[]{:S(2)}) %collective-permute-start.9) | collective-permute-done | bytes 73760 | tf_op jit(solution)/shard_map/ppermute | solution.py:100
  56.2 2.7 %collective-permute-start.10 = (bf16[288,128]{1,0:T(8,128)(2,1)S(1)}, bf16[288,128]{1,0:T(8,128)(2,1)S(1)}, u32[]{:S(2)}, u32[]{:S(2)}) collective-permute-start(bf16[288,128]{1,0:T(8,128)(2,1)S(1)} %add_convert_fusion), channel_id=1, source_target_pairs={{0,1},{1,0},{2,3},{3,2},{4,5},{5,4},{6,7},{7,6},{8,9},{9,8},{10,11... | collective-permute-start | bytes 221192 | tf_op jit(solution)/shard_map/ppermute | solution.py:103
  58.9 2.3 %collective-permute-done.10 = bf16[288,128]{1,0:T(8,128)(2,1)S(1)} collective-permute-done((bf16[288,128]{1,0:T(8,128)(2,1)S(1)}, bf16[288,128]{1,0:T(8,128)(2,1)S(1)}, u32[]{:S(2)}, u32[]{:S(2)}) %collective-permute-start.10) | collective-permute-done | bytes 73760 | tf_op jit(solution)/shard_map/ppermute | solution.py:103
  61.2 1.5 %collective-permute-start.11 = (bf16[576,128]{1,0:T(8,128)(2,1)S(1)}, bf16[576,128]{1,0:T(8,128)(2,1)S(1)}, u32[]{:S(2)}, u32[]{:S(2)}) collective-permute-start(bf16[576,128]{1,0:T(8,128)(2,1)S(1)} %bitcast.71), channel_id=1, source_target_pairs={{0,4},{4,0},{8,12},{12,8},{1,5},{5,1},{9,13},{13,9},{2,6},{6,2},{1... | collective-permute-start | bytes 442376 | tf_op jit(solution)/shard_map/ppermute | solution.py:115
  62.7 0.6 collective-permute-start.12
  63.3 1.4 %collective-permute-start.13 = (bf16[576,128]{1,0:T(8,128)(2,1)S(1)}, bf16[576,128]{1,0:T(8,128)(2,1)S(1)}, u32[]{:S(2)}, u32[]{:S(2)}) collective-permute-start(bf16[576,128]{1,0:T(8,128)(2,1)S(1)} %bitcast.73), channel_id=1, source_target_pairs={{0,12},{4,8},{8,4},{12,0},{1,13},{5,9},{9,5},{13,1},{2,14},{6,10},... | collective-permute-start | bytes 442376 | tf_op jit(solution)/shard_map/ppermute | solution.py:115
  64.8 0.1 broadcast_in_dim.16
  64.9 1.5 %collective-permute-done.11 = bf16[576,128]{1,0:T(8,128)(2,1)S(1)} collective-permute-done((bf16[576,128]{1,0:T(8,128)(2,1)S(1)}, bf16[576,128]{1,0:T(8,128)(2,1)S(1)}, u32[]{:S(2)}, u32[]{:S(2)}) %collective-permute-start.11) | collective-permute-done | bytes 147488 | tf_op jit(solution)/shard_map/ppermute | solution.py:115
  66.5 1.4 %collective-permute-done.12 = bf16[576,128]{1,0:T(8,128)(2,1)S(1)} collective-permute-done((bf16[576,128]{1,0:T(8,128)(2,1)S(1)}, bf16[576,128]{1,0:T(8,128)(2,1)S(1)}, u32[]{:S(2)}, u32[]{:S(2)}) %collective-permute-start.12) | collective-permute-done | bytes 147488 | tf_op jit(solution)/shard_map/ppermute | solution.py:115
  67.9 1.5 %collective-permute-done.13 = bf16[576,128]{1,0:T(8,128)(2,1)S(1)} collective-permute-done((bf16[576,128]{1,0:T(8,128)(2,1)S(1)}, bf16[576,128]{1,0:T(8,128)(2,1)S(1)}, u32[]{:S(2)}, u32[]{:S(2)}) %collective-permute-start.13) | collective-permute-done | bytes 147488 | tf_op jit(solution)/shard_map/ppermute | solution.py:115
  69.5 0.1 collective-permute-start.14
  69.5 1.2 %shard_map.88 = (f32[3456,128]{1,0:T(8,128)}, f32[1152,128]{1,0:T(8,128)}) custom-call(s32[1]{0:T(128)} %bitcast.4.which, bf16[2304,128]{1,0:T(8,128)(2,1)S(1)} %constant_dynamic-update-slice_fusion.half), custom_call_target="tpu_custom_call" | custom-call | bytes 4194304 | tf_op jit(solution)/shard_map/pallas_call | solution.py:143
  70.7 0.8 %collective-permute-done.14.half = bf16[2304,128]{1,0:T(8,128)(2,1)S(1)} collective-permute-done((bf16[2304,128]{1,0:T(8,128)(2,1)S(1)}, bf16[2304,128]{1,0:T(8,128)(2,1)S(1)}, u32[]{:S(2)}, u32[]{:S(2)}) %collective-permute-start.14) | collective-permute-done | bytes 589856 | tf_op jit(solution)/shard_map/ppermute | solution.py:161
  71.5 1.2 %shard_map.89 = (f32[3456,128]{1,0:T(8,128)}, f32[1152,128]{1,0:T(8,128)}) custom-call(s32[1]{0:T(128)} %bitcast.35.which, bf16[2304,128]{1,0:T(8,128)(2,1)S(1)} %collective-permute-done.14.half, f32[3456,128]{1,0:T(8,128)} %get-tuple-element.46.refs_0_, f32[1152,128]{1,0:T(8,128)} %get-tuple-element.47.refs_1_), custom_call_target="tpu_custom_call", output_to_operand_aliasing={{0}: (2, {}), {1}: (3, {})} | custom-call | bytes 4194304 | tf_op jit(solution)/shard_map/pallas_call | solution.py:143
  (27 shorter events, 0.5 us)
Async XLA Ops:
  1.4 11.4 %copy-start = (bf16[1,8,8,8,128]{4,3,2,1,0:T(8,128)(2,1)S(1)}, bf16[1,8,8,8,128]{4,3,2,1,0:T(8,128)(2,1)}, u32[]{:S(2)}) copy-start(bf16[1,8,8,8,128]{4,3,2,1,0:T(8,128)(2,1)} %param.9) | copy-start | bytes 393220
  2.3 10.7 %copy-start.7 = (bf16[1,8,16,16,128]{4,3,2,1,0:T(8,128)(2,1)S(1)}, bf16[1,8,16,16,128]{4,3,2,1,0:T(8,128)(2,1)}, u32[]{:S(2)}) copy-start(bf16[1,8,16,16,128]{4,3,2,1,0:T(8,128)(2,1)} %param.5) | copy-start | bytes 1572868
  2.4 8.7 %collective-permute-start = (bf16[320,128]{1,0:T(8,128)(2,1)S(1)}, bf16[320,128]{1,0:T(8,128)(2,1)S(1)}, u32[]{:S(2)}, u32[]{:S(2)}) collective-permute-start(bf16[320,128]{1,0:T(8,128)(2,1)S(1)} %get-tuple-element.71), channel_id=1, source_target_pairs={{4,8},{8,4},{5,9},{9,5},{6,10},{10,6},{7,11},{11,7},{20,24},{24,20... | collective-permute-start | bytes 245768 | tf_op jit(solution)/shard_map/ppermute | solution.py:26
  3.2 9.6 %collective-permute-start.1 = (bf16[320,128]{1,0:T(8,128)(2,1)S(1)}, bf16[320,128]{1,0:T(8,128)(2,1)S(1)}, u32[]{:S(2)}, u32[]{:S(2)}) collective-permute-start(bf16[320,128]{1,0:T(8,128)(2,1)S(1)} %get-tuple-element.72), channel_id=1, source_target_pairs={{0,4},{4,0},{8,12},{12,8},{1,5},{5,1},{9,13},{13,9},{2,6},{6,2},{1... | collective-permute-start | bytes 245768 | tf_op jit(solution)/shard_map/ppermute | solution.py:25
  10.2 5.5 %copy-start.2 = (bf16[3,3,3,128,128]{4,3,2,1,0:T(8,128)(2,1)S(1)}, bf16[3,3,3,128,128]{4,3,2,1,0:T(8,128)(2,1)}, u32[]{:S(2)}) copy-start(bf16[3,3,3,128,128]{4,3,2,1,0:T(8,128)(2,1)} %param.7) | copy-start | bytes 2654212
  13.4 6.8 %collective-permute-start.3 = (bf16[400,128]{1,0:T(8,128)(2,1)S(1)}, bf16[400,128]{1,0:T(8,128)(2,1)S(1)}, u32[]{:S(2)}, u32[]{:S(2)}) collective-permute-start(bf16[400,128]{1,0:T(8,128)(2,1)S(1)} %get-tuple-element.67), channel_id=1, source_target_pairs={{0,1},{1,0},{2,3},{3,2},{4,5},{5,4},{6,7},{7,6},{8,9},{9,8},{10,11... | collective-permute-start | bytes 307208 | tf_op jit(solution)/shard_map/ppermute | solution.py:25
  15.0 5.1 %collective-permute-start.2 = (bf16[400,128]{1,0:T(8,128)(2,1)S(1)}, bf16[400,128]{1,0:T(8,128)(2,1)S(1)}, u32[]{:S(2)}, u32[]{:S(2)}) collective-permute-start(bf16[400,128]{1,0:T(8,128)(2,1)S(1)} %get-tuple-element.68), channel_id=1, source_target_pairs={{1,2},{2,1},{5,6},{6,5},{9,10},{10,9},{13,14},{14,13},{17,18},{18,... | collective-permute-start | bytes 307208 | tf_op jit(solution)/shard_map/ppermute | solution.py:26
  19.1 1.0 %copy-start.3 = (f32[8,288,128]{2,1,0:T(8,128)}, f32[8,288,128]{2,1,0:T(8,128)S(1)}, u32[]{:S(2)}) copy-start(f32[8,288,128]{2,1,0:T(8,128)S(1)} %shard_map.84.pre) | copy-start | bytes 3538948
  20.1 1.0 %copy-start.1 = (bf16[3,3,128,128]{3,2,1,0:T(8,128)(2,1)S(1)}, bf16[3,3,128,128]{3,2,1,0:T(8,128)(2,1)}, u32[]{:S(2)}) copy-start(bf16[3,3,128,128]{3,2,1,0:T(8,128)(2,1)} %param.8) | copy-start | bytes 884740
  20.3 1.3 %copy-start.4 = (f32[8,288,128]{2,1,0:T(8,128)S(1)}, f32[8,288,128]{2,1,0:T(8,128)}, u32[]{:S(2)}) copy-start(f32[8,288,128]{2,1,0:T(8,128)} %copy-done.3) | copy-start | bytes 3538948
  31.3 0.8 %copy-start.5 = (bf16[8,288,128]{2,1,0:T(8,128)(2,1)}, bf16[8,288,128]{2,1,0:T(8,128)(2,1)S(1)}, u32[]{:S(2)}) copy-start(bf16[8,288,128]{2,1,0:T(8,128)(2,1)S(1)} %get-tuple-element.36.own_grad) | copy-start | bytes 1769476
  32.1 2.2 %collective-permute-start.4 = (bf16[2304,128]{1,0:T(8,128)(2,1)}, bf16[2304,128]{1,0:T(8,128)(2,1)S(1)}, u32[]{:S(2)}, u32[]{:S(2)}) collective-permute-start(bf16[2304,128]{1,0:T(8,128)(2,1)} %get-tuple-element.32), channel_id=1, source_target_pairs={{0,16},{16,0},{1,17},{17,1},{2,18},{18,2},{3,19},{19,3},{4,20},{20... | collective-permute-start | bytes 1769480 | tf_op jit(solution)/shard_map/ppermute | solution.py:158
  32.1 5.9 %copy-start.6 = (bf16[8,288,128]{2,1,0:T(8,128)(2,1)S(1)}, bf16[8,288,128]{2,1,0:T(8,128)(2,1)}, u32[]{:S(2)}) copy-start(bf16[8,288,128]{2,1,0:T(8,128)(2,1)} %copy-done.5) | copy-start | bytes 1769476
  34.4 7.9 %collective-permute-start.5 = (bf16[576,128]{1,0:T(8,128)(2,1)S(1)}, bf16[576,128]{1,0:T(8,128)(2,1)S(1)}, u32[]{:S(2)}, u32[]{:S(2)}) collective-permute-start(bf16[576,128]{1,0:T(8,128)(2,1)S(1)} %get-tuple-element.33), channel_id=1, source_target_pairs={{0,4},{4,0},{8,12},{12,8},{1,5},{5,1},{9,13},{13,9},{2,6},{6,2},{1... | collective-permute-start | bytes 442376 | tf_op jit(solution)/shard_map/ppermute | solution.py:86
  35.1 8.8 %collective-permute-start.6 = (bf16[576,128]{1,0:T(8,128)(2,1)S(1)}, bf16[576,128]{1,0:T(8,128)(2,1)S(1)}, u32[]{:S(2)}, u32[]{:S(2)}) collective-permute-start(bf16[576,128]{1,0:T(8,128)(2,1)S(1)} %get-tuple-element.34), channel_id=1, source_target_pairs={{0,8},{4,12},{8,0},{12,4},{1,9},{5,13},{9,1},{13,5},{2,10},{6,14},... | collective-permute-start | bytes 442376 | tf_op jit(solution)/shard_map/ppermute | solution.py:86
  36.5 7.4 %collective-permute-start.7 = (bf16[576,128]{1,0:T(8,128)(2,1)S(1)}, bf16[576,128]{1,0:T(8,128)(2,1)S(1)}, u32[]{:S(2)}, u32[]{:S(2)}) collective-permute-start(bf16[576,128]{1,0:T(8,128)(2,1)S(1)} %get-tuple-element.35), channel_id=1, source_target_pairs={{0,12},{4,8},{8,4},{12,0},{1,13},{5,9},{9,5},{13,1},{2,14},{6,10},... | collective-permute-start | bytes 442376 | tf_op jit(solution)/shard_map/ppermute | solution.py:86
  44.0 6.8 %collective-permute-start.8 = (bf16[288,128]{1,0:T(8,128)(2,1)S(1)}, bf16[288,128]{1,0:T(8,128)(2,1)S(1)}, u32[]{:S(2)}, u32[]{:S(2)}) collective-permute-start(bf16[288,128]{1,0:T(8,128)(2,1)S(1)} %dynamic-slice_convert_fusion), channel_id=1, source_target_pairs={{0,1},{1,0},{2,3},{3,2},{4,5},{5,4},{6,7},{7,6},{8,9},{9,8},{10,11... | collective-permute-start | bytes 221192 | tf_op jit(solution)/shard_map/ppermute | solution.py:98
  50.8 5.3 %collective-permute-start.9 = (bf16[288,128]{1,0:T(8,128)(2,1)S(1)}, bf16[288,128]{1,0:T(8,128)(2,1)S(1)}, u32[]{:S(2)}, u32[]{:S(2)}) collective-permute-start(bf16[288,128]{1,0:T(8,128)(2,1)S(1)} %fusion.4), channel_id=1, source_target_pairs={{0,2},{1,3},{2,0},{3,1},{4,6},{5,7},{6,4},{7,5},{8,10},{9,11},{10,... | collective-permute-start | bytes 221192 | tf_op jit(solution)/shard_map/ppermute | solution.py:100
  56.2 5.0 %collective-permute-start.10 = (bf16[288,128]{1,0:T(8,128)(2,1)S(1)}, bf16[288,128]{1,0:T(8,128)(2,1)S(1)}, u32[]{:S(2)}, u32[]{:S(2)}) collective-permute-start(bf16[288,128]{1,0:T(8,128)(2,1)S(1)} %add_convert_fusion), channel_id=1, source_target_pairs={{0,1},{1,0},{2,3},{3,2},{4,5},{5,4},{6,7},{7,6},{8,9},{9,8},{10,11... | collective-permute-start | bytes 221192 | tf_op jit(solution)/shard_map/ppermute | solution.py:103
  61.2 5.2 %collective-permute-start.11 = (bf16[576,128]{1,0:T(8,128)(2,1)S(1)}, bf16[576,128]{1,0:T(8,128)(2,1)S(1)}, u32[]{:S(2)}, u32[]{:S(2)}) collective-permute-start(bf16[576,128]{1,0:T(8,128)(2,1)S(1)} %bitcast.71), channel_id=1, source_target_pairs={{0,4},{4,0},{8,12},{12,8},{1,5},{5,1},{9,13},{13,9},{2,6},{6,2},{1... | collective-permute-start | bytes 442376 | tf_op jit(solution)/shard_map/ppermute | solution.py:115
  62.7 5.2 %collective-permute-start.12 = (bf16[576,128]{1,0:T(8,128)(2,1)S(1)}, bf16[576,128]{1,0:T(8,128)(2,1)S(1)}, u32[]{:S(2)}, u32[]{:S(2)}) collective-permute-start(bf16[576,128]{1,0:T(8,128)(2,1)S(1)} %bitcast.72), channel_id=1, source_target_pairs={{0,8},{4,12},{8,0},{12,4},{1,9},{5,13},{9,1},{13,5},{2,10},{6,14},... | collective-permute-start | bytes 442376 | tf_op jit(solution)/shard_map/ppermute | solution.py:115
  63.3 6.1 %collective-permute-start.13 = (bf16[576,128]{1,0:T(8,128)(2,1)S(1)}, bf16[576,128]{1,0:T(8,128)(2,1)S(1)}, u32[]{:S(2)}, u32[]{:S(2)}) collective-permute-start(bf16[576,128]{1,0:T(8,128)(2,1)S(1)} %bitcast.73), channel_id=1, source_target_pairs={{0,12},{4,8},{8,4},{12,0},{1,13},{5,9},{9,5},{13,1},{2,14},{6,10},... | collective-permute-start | bytes 442376 | tf_op jit(solution)/shard_map/ppermute | solution.py:115
  69.5 2.1 %collective-permute-start.14 = (bf16[2304,128]{1,0:T(8,128)(2,1)S(1)}, bf16[2304,128]{1,0:T(8,128)(2,1)S(1)}, u32[]{:S(2)}, u32[]{:S(2)}) collective-permute-start(bf16[2304,128]{1,0:T(8,128)(2,1)S(1)} %constant_dynamic-update-slice_fusion.half), channel_id=1, source_target_pairs={{0,16},{16,0},{1,17},{17,1},{2,18},{18,2},{3,19},{19,3},{4,20},{20... | collective-permute-start | bytes 1769480 | tf_op jit(solution)/shard_map/ppermute | solution.py:161

commit v3 on v2

--- a/solution.py
+++ b/solution.py
@@ -83,7 +83,8 @@
         out_specs=(vmem,) * count,
         compiler_params=pltpu.CompilerParams(vmem_limit_bytes=8 << 20),
     )(mine[None], kept, got)
-    terms = [lax.ppermute(sends[mask - 1], axis, flip(axis, mask)) for mask in range(1, count)]
+    order = range(count - 1, 0, -1)
+    terms = [lax.ppermute(sends[mask - 1], axis, flip(axis, mask)) for mask in order]
     terms, beside = lax.optimization_barrier((terms, beside))
     for term in terms:
         total = total + term.astype(F32)
@@ -111,7 +112,7 @@
     share = y.shape[0]
     whole = jnp.zeros((count * share,) + y.shape[1:], y.dtype)
     whole = lax.dynamic_update_slice_in_dim(whole, y, mine * share, 0)
-    for mask in range(1, count):
+    for mask in range(count - 1, 0, -1):
         got = lax.ppermute(y, axis, flip(axis, mask))
         whole = lax.dynamic_update_slice_in_dim(whole, got, (mine ^ mask) * share, 0)
     return whole
@@ -177,7 +178,6 @@
 
 
 GROUP = 4
-PAIR = 8
 
 
 def side_by_side(kernel_main, w_main):
@@ -251,37 +251,41 @@
     low_row, high_row = flags[1].astype(F32), flags[2].astype(F32)
     low_col, high_col = flags[3].astype(F32), flags[4].astype(F32)
 
-    def spread(t, carry):
-        x32[:, 0:in_cols, :] = wide[t].astype(F32)
-        for kw in range(3):
-            shifted = x32[:, pl.ds(1 + kw, cols), :].astype(BF)
-            x_taps[t, kw] = shifted.reshape(in_rows * cols, channels)
-            side32[kw, :, pl.ds(t, 1), :] = x32[:, kw : kw + 1, :]
-            side32[kw, :, pl.ds(frames + t, 1), :] = x32[:, cols + 1 + kw : cols + 2 + kw, :]
-        l32[:, 0 : half_cols + 2, :] = grad_wide[t].astype(F32)
-        near = [l32[:, pl.ds(dq, 16), :].astype(BF) for dq in range(2)]
-        grads = jnp.concatenate(
-            [
+    def spread(i, carry):
+        lines = []
+        for g in range(GROUP):
+            t = i * GROUP + g
+            x32[:, 0:in_cols, :] = wide[t].astype(F32)
+            for kw in range(3):
+                shifted = x32[:, pl.ds(1 + kw, cols), :].astype(BF)
+                x_taps[t, kw] = shifted.reshape(in_rows * cols, channels)
+                side32[kw, :, pl.ds(t, 1), :] = x32[:, kw : kw + 1, :]
+                side32[kw, :, pl.ds(frames + t, 1), :] = x32[:, cols + 1 + kw : cols + 2 + kw, :]
+            l32[:, 0 : half_cols + 2, :] = grad_wide[t].astype(F32)
+            near = [l32[:, pl.ds(dq, 16), :].astype(BF) for dq in range(2)]
+            shifts = [
                 near[dq][dp : dp + half_rows + 1].reshape((half_rows + 1) * 16, channels)
                 for dp in (1, 0)
                 for dq in (1, 0)
-            ],
-            axis=1,
-        )
-        classes = dot(grads, w_grad[...])
-        for p in range(half_rows + 1):
-            for odd in range(2):
-                line = classes[p * 16 : p * 16 + half_cols + 1]
-                row = 2 * p + 1 - odd
-                even_part = line[:, 2 * odd * channels : (2 * odd + 1) * channels]
-                odd_part = line[:, (2 * odd + 1) * channels : (2 * odd + 2) * channels]
-                act_grad[t, row, pl.ds(LEFT, half_cols + 1, stride=2), :] = even_part
-                act_grad[t, row, pl.ds(LEFT - 1, half_cols + 1, stride=2), :] = odd_part
-        side_back[:, pl.ds(t, 1), :] = act_grad[t, :, LEFT - 1 : LEFT, :]
-        side_back[:, pl.ds(frames + t, 1), :] = act_grad[t, :, LEFT + cols : LEFT + cols + 1, :]
+            ]
+            lines.append(jnp.concatenate(shifts, axis=1))
+        classes = dot(jnp.concatenate(lines, axis=0), w_grad[...])
+        for g in range(GROUP):
+            t = i * GROUP + g
+            for p in range(half_rows + 1):
+                at = (g * (half_rows + 1) + p) * 16
+                for odd in range(2):
+                    line = classes[at : at + half_cols + 1]
+                    row = 2 * p + 1 - odd
+                    even_part = line[:, 2 * odd * channels : (2 * odd + 1) * channels]
+                    odd_part = line[:, (2 * odd + 1) * channels : (2 * odd + 2) * channels]
+                    act_grad[t, row, pl.ds(LEFT, half_cols + 1, stride=2), :] = even_part
+                    act_grad[t, row, pl.ds(LEFT - 1, half_cols + 1, stride=2), :] = odd_part
+            side_back[:, pl.ds(t, 1), :] = act_grad[t, :, LEFT - 1 : LEFT, :]
+            side_back[:, pl.ds(frames + t, 1), :] = act_grad[t, :, LEFT + cols : LEFT + cols + 1, :]
         return carry
 
-    lax.fori_loop(0, frames, spread, 0)
+    lax.fori_loop(0, frames // GROUP, spread, 0)
 
     side_lhs = jnp.concatenate(
         [
@@ -365,34 +369,25 @@
         ]
         return jnp.concatenate(taps, axis=1)
 
-    total[:, 0:channels] = jnp.zeros((9, channels, channels), F32)
     early = dot(grad_t[0:2].reshape(2 * channels, rows * cols), patches(0))
     for tap in range(9):
         block = early[:, tap * channels : (tap + 1) * channels]
-        total[tap, channels : 2 * channels] = block[:channels]
-        total[tap, 2 * channels :] = block[:channels] + block[channels:]
-
-    def weights(i, carry):
-        left = [grad_t[pl.ds(PAIR * i + g, 3)].reshape(3 * channels, rows * cols) for g in range(PAIR)]
-        right = [patches(PAIR * i + g) for g in range(PAIR)]
-        out = dot(jnp.concatenate(left, axis=1), jnp.concatenate(right, axis=0))
+        total[tap, 0:channels] = block[:channels]
+        total[tap, channels:] = block[:channels] + block[channels:]
+
+    left = [grad_t[t : t + 3].reshape(3 * channels, rows * cols) for t in range(frames)]
+    right = [patches(t) for t in range(frames)]
+    out = dot(jnp.concatenate(left, axis=1), jnp.concatenate(right, axis=0))
+
+    def emit(low, high):
         for tap in range(9):
-            total[tap] += out[:, tap * channels : (tap + 1) * channels]
-        return carry
-
-    lax.fori_loop(0, frames // PAIR, weights, 0)
-
-    def emit(low, high):
-        def tap_out(tap, carry):
-            at = pl.multiple_of(tap * channels, channels)
-            after = pl.multiple_of((9 + tap) * channels, channels)
-            low[pl.ds(at, channels), :] = total[tap, 2 * channels :].astype(low.dtype)
-            low[pl.ds(after, channels), :] = total[tap, channels : 2 * channels].astype(low.dtype)
-            high[pl.ds(at, channels), :] = total[tap, 0:channels].astype(high.dtype)
-            high[pl.ds(after, channels), :] = down_total[tap].astype(high.dtype)
-            return carry
-
-        lax.fori_loop(0, 9, tap_out, 0)
+            at, after = tap * channels, (9 + tap) * channels
+            block = out[:, tap * channels : (tap + 1) * channels]
+            first, second, third = (block[k * channels : (k + 1) * channels] for k in (2, 1, 0))
+            low[at : at + channels, :] = (first + total[tap, channels:]).astype(low.dtype)
+            low[after : after + channels, :] = (second + total[tap, 0:channels]).astype(low.dtype)
+            high[at : at + channels, :] = third.astype(high.dtype)
+            high[after : after + channels, :] = down_total[tap].astype(high.dtype)
 
     @pl.when(flags[5] == 0)
     def _():
@@ -531,7 +526,7 @@
             pltpu.VMEM((ext, cols + 16, channels), F32),
             pltpu.VMEM((frames, rows * cols // 4, 9 * channels), BF),
             pltpu.VMEM((frames + 2, channels, rows * cols), BF),
-            pltpu.VMEM((9, 3 * channels, channels), F32),
+            pltpu.VMEM((9, 2 * channels, channels), F32),
             pltpu.VMEM((9, channels, channels), F32),
         ],
         compiler_params=pltpu.CompilerParams(vmem_limit_bytes=24 << 20),

time: 73.2 us -> 71.9 us (0.982)
  Pallas kernels: 20 us -> 19 us
  starting transfers between devices: 24.8 us -> 23.9 us
    pallas_call x1, Pallas kernels: 9.72 us -> 8.75 us  [on_device(): pl.pallas_call(main_kernel, out_shape=(jax.ShapeDtypeStruct((18 * channel...]
    ppermute x1, starting transfers between devices: 2.68 us -> 1.87 us  [line_sum(): got = lax.ppermute(y, axis, flip(axis, 1 << bit))]
  transfers between devices with their start and end apart: 15 -> 15, of which waited for: 10 -> 9; matrix products, arithmetic and copies ran while one was open for 2% -> 2% of each run, Pallas kernels for 12% -> 13%
where the time goes in v3:
time: 71.9 us; the launch traced here: 71.6 us
  starting transfers between devices  23.9 us (33%)
  waiting for transfers between devices  19.7 us (27%)
  Pallas kernels  19 us (26%)
  local copies, waits for them, and re-layouts  5.73 us (8%)
  between operations  1.9 us (3%)
  other arithmetic  1.39 us (2%)
    pallas_call x1, Pallas kernels, on_device(): pl.pallas_call(main_kernel, out_shape=(jax.ShapeDtypeStruct((18 * channel...  8.75 us
    ppermute x2, starting transfers between devices, exchange(): a = lax.ppermute(jnp.where(even, high_edge, low_edge), axis, inner)  7.38 us
    ppermute x1, starting transfers between devices, line_sum(): lax.ppermute(sent, axis, flip(axis, 1 << bit)).astype(F32)  4.46 us
    pallas_call x1, Pallas kernels, on_device(): pl.pallas_call(back_kernel, out_shape=jax.ShapeDtypeStruct((frames, rows...  4.34 us
    ppermute x3, waiting for transfers between devices, direct_gather(): got = lax.ppermute(y, axis, flip(axis, mask))  3.99 us
    ppermute x1, waiting for transfers between devices, line_sum(): got = lax.ppermute(x.astype(BF), axis, flip(axis, 1 << bits - 1))  3.86 us
    ppermute x3, starting transfers between devices, direct_gather(): got = lax.ppermute(y, axis, flip(axis, mask))  3.55 us
    ppermute x3, starting transfers between devices, direct_scatter(): lax.ppermute(sends[mask - 1], axis, flip(axis, mask))  3.55 us
  transfers between devices with their start and end apart: 15, of which 9 were waited for; matrix products, arithmetic and copies ran while one was open for 2% of the time, Pallas kernels for 13%

profile of v3, /device:TPU:0, one launch (start us, length us, event | category | flops | bytes accessed | tf_op | source)
XLA Modules:
  0.0 71.6 jit_solution(2156147437445333403)
XLA Ops:
  0.6 0.7 %slice_bitcast_fusion.12 = (bf16[64,128]{1,0:T(8,128)(2,1)S(1)}, bf16[64,128]{1,0:T(8,128)(2,1)S(1)}) fusion(bf16[8,8,8,128]{3,2,1,0:T(8,128)(2,1)} %bitcast.54), kind=kLoop, calls=%fused_computation.42 | loop fusion | bytes 65536 | tf_op jit(solution)/shard_map/reshape | solution.py:31
  1.4 0.0 copy-start
  1.4 0.9 %fusion.7 = (bf16[8,2,16,128]{3,2,1,0:T(8,128)(2,1)S(1)}, bf16[8,2,16,128]{3,2,1,0:T(8,128)(2,1)S(1)}) fusion(bf16[8,16,16,128]{3,2,1,0:T(8,128)(2,1)} %bitcast.62), kind=kLoop, calls=%fused_computation.48 | loop fusion | bytes 262144 | tf_op jit(solution)/shard_map/slice | solution.py:42
  2.3 0.0 copy-start.7
  2.4 0.8 %collective-permute-start = (bf16[320,128]{1,0:T(8,128)(2,1)S(1)}, bf16[320,128]{1,0:T(8,128)(2,1)S(1)}, u32[]{:S(2)}, u32[]{:S(2)}) collective-permute-start(bf16[320,128]{1,0:T(8,128)(2,1)S(1)} %get-tuple-element.71), channel_id=1, source_target_pairs={{4,8},{8,4},{5,9},{9,5},{6,10},{10,6},{7,11},{11,7},{20,24},{24,20... | collective-permute-start | bytes 245768 | tf_op jit(solution)/shard_map/ppermute | solution.py:26
  3.2 5.7 %collective-permute-start.1 = (bf16[320,128]{1,0:T(8,128)(2,1)S(1)}, bf16[320,128]{1,0:T(8,128)(2,1)S(1)}, u32[]{:S(2)}, u32[]{:S(2)}) collective-permute-start(bf16[320,128]{1,0:T(8,128)(2,1)S(1)} %get-tuple-element.72), channel_id=1, source_target_pairs={{0,4},{4,0},{8,12},{12,8},{1,5},{5,1},{9,13},{13,9},{2,6},{6,2},{1... | collective-permute-start | bytes 245768 | tf_op jit(solution)/shard_map/ppermute | solution.py:25
  8.9 1.2 %copy.14 = bf16[3,3,128,128]{2,3,1,0:T(8,128)(2,1)S(1)} copy(bf16[3,3,128,128]{3,2,1,0:T(8,128)(2,1)} %param.8) | data formatting | bytes 589824 | tf_op args[3]
  10.2 0.0 copy-start.2
  11.0 0.1 stack.53.flags
  11.0 0.0 collective-permute-done
  11.0 1.7 %collective-permute-done.1 = bf16[320,128]{1,0:T(8,128)(2,1)S(1)} collective-permute-done((bf16[320,128]{1,0:T(8,128)(2,1)S(1)}, bf16[320,128]{1,0:T(8,128)(2,1)S(1)}, u32[]{:S(2)}, u32[]{:S(2)}) %collective-permute-start.1) | collective-permute-done | bytes 81952 | tf_op jit(solution)/shard_map/ppermute | solution.py:25
  12.8 0.0 copy-done
  12.8 0.2 maximum_reduce_fusion
  13.1 0.0 copy-done.7
  13.1 0.1 pad_maximum_fusion.1.tall
  13.2 0.1 fusion.6
  13.4 1.6 %collective-permute-start.3 = (bf16[400,128]{1,0:T(8,128)(2,1)S(1)}, bf16[400,128]{1,0:T(8,128)(2,1)S(1)}, u32[]{:S(2)}, u32[]{:S(2)}) collective-permute-start(bf16[400,128]{1,0:T(8,128)(2,1)S(1)} %get-tuple-element.67), channel_id=1, source_target_pairs={{0,1},{1,0},{2,3},{3,2},{4,5},{5,4},{6,7},{7,6},{8,9},{9,8},{10,11... | collective-permute-start | bytes 307208 | tf_op jit(solution)/shard_map/ppermute | solution.py:25
  15.0 0.7 collective-permute-start.2
  15.7 0.0 copy-done.2
  15.7 3.4 %shard_map.84.pre = f32[8,288,128]{2,1,0:T(8,128)S(1)} custom-call(bf16[8,20,16,128]{3,2,1,0:T(8,128)(2,1)S(1)} %pad_maximum_fusion.1.tall, bf16[27,128,128]{2,1,0:T(8,128)(2,1)S(1)} %bitcast.59), custom_call_target="tpu_custom_call" | custom-call | flops 2038431744 | bytes 4194304 | tf_op jit(solution)/shard_map/pallas_call | solution.py:471
  19.1 0.0 copy-start.3
  19.1 1.0 %copy-done.3 = f32[8,288,128]{2,1,0:T(8,128)} copy-done((f32[8,288,128]{2,1,0:T(8,128)}, f32[8,288,128]{2,1,0:T(8,128)S(1)}, u32[]{:S(2)}) %copy-start.3) | copy-done | bytes 1179672
  20.1 0.0 copy-start.1
  20.1 0.0 collective-permute-done.3
  20.1 0.0 collective-permute-done.2
  20.3 0.0 copy-start.4
  20.3 0.6 pad_maximum_fusion.wide
  20.9 0.2 pad_maximum_fusion.2.grad_wide
  21.1 0.0 copy-done.1
  21.1 0.5 copy-done.4
  21.6 8.7 %shard_map.85 = (f32[2304,128]{1,0:T(8,128)S(1)}, bf16[2304,128]{1,0:T(8,128)(2,1)}, bf16[8,288,128]{2,1,0:T(8,128)(2,1)S(1)}, bf16[18,16,128]{2,1,0:T(8,128)(2,1)S(1)}, bf16[512,128]{1,0:T(8,128)(2,1)}) custom-call(s32[6]{0:T(128)S(1)} %stack.53.flags, bf16[8,20,20,128]{3,2,1,0:T(8,128)(2,1)S(1)} %pad_maximum_fusion.wide, ...), custom_call_target="tpu_custom_call" | custom-call | flops 2684354560 | bytes 12582912 | tf_op jit(solution)/shard_map/pallas_call | solution.py:504
  30.3 0.0 copy-start.5
  30.3 0.8 %copy-done.5 = bf16[8,288,128]{2,1,0:T(8,128)(2,1)} copy-done((bf16[8,288,128]{2,1,0:T(8,128)(2,1)}, bf16[8,288,128]{2,1,0:T(8,128)(2,1)S(1)}, u32[]{:S(2)}) %copy-start.5) | copy-done | bytes 589848
  31.1 0.0 collective-permute-start.4
  31.1 0.0 copy-start.6
  31.1 2.2 %collective-permute-done.4.got = bf16[2304,128]{1,0:T(8,128)(2,1)S(1)} collective-permute-done((bf16[2304,128]{1,0:T(8,128)(2,1)}, bf16[2304,128]{1,0:T(8,128)(2,1)S(1)}, u32[]{:S(2)}, u32[]{:S(2)}) %collective-permute-start.4) | collective-permute-done | bytes 589856 | tf_op jit(solution)/shard_map/ppermute | solution.py:159
  33.3 0.1 shard_map.86
  33.4 1.5 %collective-permute-start.5 = (bf16[576,128]{1,0:T(8,128)(2,1)S(1)}, bf16[576,128]{1,0:T(8,128)(2,1)S(1)}, u32[]{:S(2)}, u32[]{:S(2)}) collective-permute-start(bf16[576,128]{1,0:T(8,128)(2,1)S(1)} %get-tuple-element.33), channel_id=1, source_target_pairs={{0,12},{4,8},{8,4},{12,0},{1,13},{5,9},{9,5},{13,1},{2,14},{6,10},... | collective-permute-start | bytes 442376 | tf_op jit(solution)/shard_map/ppermute | solution.py:87
  34.9 0.6 collective-permute-start.6
  35.6 1.4 %collective-permute-start.7 = (bf16[576,128]{1,0:T(8,128)(2,1)S(1)}, bf16[576,128]{1,0:T(8,128)(2,1)S(1)}, u32[]{:S(2)}, u32[]{:S(2)}) collective-permute-start(bf16[576,128]{1,0:T(8,128)(2,1)S(1)} %get-tuple-element.35), channel_id=1, source_target_pairs={{0,4},{4,0},{8,12},{12,8},{1,5},{5,1},{9,13},{13,9},{2,6},{6,2},{1... | collective-permute-start | bytes 442376 | tf_op jit(solution)/shard_map/ppermute | solution.py:87
  37.0 0.0 copy-done.6
  37.0 4.3 %shard_map.87 = bf16[8,256,128]{2,1,0:T(8,128)(2,1)} custom-call(bf16[8,288,128]{2,1,0:T(8,128)(2,1)S(1)} %copy-done.6, bf16[18,16,128]{2,1,0:T(8,128)(2,1)S(1)} %get-tuple-element.37.side_grad, bf16[27,128,128]{2,1,0:T(8,128)(2,1)S(1)} %bitcast.61), custom_call_target="tpu_custom_call" | custom-call | flops 1811939328 | bytes 4194304 | tf_op jit(solution)/shard_map/pallas_call | solution.py:548
  41.3 0.0 collective-permute-done.5
  41.3 2.1 %collective-permute-done.6 = bf16[576,128]{1,0:T(8,128)(2,1)S(1)} collective-permute-done((bf16[576,128]{1,0:T(8,128)(2,1)S(1)}, bf16[576,128]{1,0:T(8,128)(2,1)S(1)}, u32[]{:S(2)}, u32[]{:S(2)}) %collective-permute-start.6) | collective-permute-done | bytes 147488 | tf_op jit(solution)/shard_map/ppermute | solution.py:87
  43.5 0.0 collective-permute-done.7
  43.5 0.1 convert_add_fusion
  43.6 4.5 %collective-permute-start.8 = (bf16[288,128]{1,0:T(8,128)(2,1)S(1)}, bf16[288,128]{1,0:T(8,128)(2,1)S(1)}, u32[]{:S(2)}, u32[]{:S(2)}) collective-permute-start(bf16[288,128]{1,0:T(8,128)(2,1)S(1)} %dynamic-slice_convert_fusion), channel_id=1, source_target_pairs={{0,1},{1,0},{2,3},{3,2},{4,5},{5,4},{6,7},{7,6},{8,9},{9,8},{10,11... | collective-permute-start | bytes 221192 | tf_op jit(solution)/shard_map/ppermute | solution.py:99
  48.0 2.4 %collective-permute-done.8 = bf16[288,128]{1,0:T(8,128)(2,1)S(1)} collective-permute-done((bf16[288,128]{1,0:T(8,128)(2,1)S(1)}, bf16[288,128]{1,0:T(8,128)(2,1)S(1)}, u32[]{:S(2)}, u32[]{:S(2)}) %collective-permute-start.8) | collective-permute-done | bytes 73760 | tf_op jit(solution)/shard_map/ppermute | solution.py:99
  50.5 1.6 %collective-permute-start.9 = (bf16[288,128]{1,0:T(8,128)(2,1)S(1)}, bf16[288,128]{1,0:T(8,128)(2,1)S(1)}, u32[]{:S(2)}, u32[]{:S(2)}) collective-permute-start(bf16[288,128]{1,0:T(8,128)(2,1)S(1)} %fusion.4), channel_id=1, source_target_pairs={{0,2},{1,3},{2,0},{3,1},{4,6},{5,7},{6,4},{7,5},{8,10},{9,11},{10,... | collective-permute-start | bytes 221192 | tf_op jit(solution)/shard_map/ppermute | solution.py:101
  52.1 3.9 %collective-permute-done.9 = bf16[288,128]{1,0:T(8,128)(2,1)S(1)} collective-permute-done((bf16[288,128]{1,0:T(8,128)(2,1)S(1)}, bf16[288,128]{1,0:T(8,128)(2,1)S(1)}, u32[]{:S(2)}, u32[]{:S(2)}) %collective-permute-start.9) | collective-permute-done | bytes 73760 | tf_op jit(solution)/shard_map/ppermute | solution.py:101
  56.0 1.9 %collective-permute-start.10 = (bf16[288,128]{1,0:T(8,128)(2,1)S(1)}, bf16[288,128]{1,0:T(8,128)(2,1)S(1)}, u32[]{:S(2)}, u32[]{:S(2)}) collective-permute-start(bf16[288,128]{1,0:T(8,128)(2,1)S(1)} %add_convert_fusion), channel_id=1, source_target_pairs={{0,1},{1,0},{2,3},{3,2},{4,5},{5,4},{6,7},{7,6},{8,9},{9,8},{10,11... | collective-permute-start | bytes 221192 | tf_op jit(solution)/shard_map/ppermute | solution.py:104
  57.8 2.5 %collective-permute-done.10 = bf16[288,128]{1,0:T(8,128)(2,1)S(1)} collective-permute-done((bf16[288,128]{1,0:T(8,128)(2,1)S(1)}, bf16[288,128]{1,0:T(8,128)(2,1)S(1)}, u32[]{:S(2)}, u32[]{:S(2)}) %collective-permute-start.10) | collective-permute-done | bytes 73760 | tf_op jit(solution)/shard_map/ppermute | solution.py:104
  60.4 1.5 %collective-permute-start.11 = (bf16[576,128]{1,0:T(8,128)(2,1)S(1)}, bf16[576,128]{1,0:T(8,128)(2,1)S(1)}, u32[]{:S(2)}, u32[]{:S(2)}) collective-permute-start(bf16[576,128]{1,0:T(8,128)(2,1)S(1)} %bitcast.71), channel_id=1, source_target_pairs={{0,12},{4,8},{8,4},{12,0},{1,13},{5,9},{9,5},{13,1},{2,14},{6,10},... | collective-permute-start | bytes 442376 | tf_op jit(solution)/shard_map/ppermute | solution.py:116
  61.9 0.6 collective-permute-start.12
  62.5 1.4 %collective-permute-start.13 = (bf16[576,128]{1,0:T(8,128)(2,1)S(1)}, bf16[576,128]{1,0:T(8,128)(2,1)S(1)}, u32[]{:S(2)}, u32[]{:S(2)}) collective-permute-start(bf16[576,128]{1,0:T(8,128)(2,1)S(1)} %bitcast.73), channel_id=1, source_target_pairs={{0,4},{4,0},{8,12},{12,8},{1,5},{5,1},{9,13},{13,9},{2,6},{6,2},{1... | collective-permute-start | bytes 442376 | tf_op jit(solution)/shard_map/ppermute | solution.py:116
  64.0 0.1 broadcast_in_dim.16
  64.1 2.5 %collective-permute-done.11 = bf16[576,128]{1,0:T(8,128)(2,1)S(1)} collective-permute-done((bf16[576,128]{1,0:T(8,128)(2,1)S(1)}, bf16[576,128]{1,0:T(8,128)(2,1)S(1)}, u32[]{:S(2)}, u32[]{:S(2)}) %collective-permute-start.11) | collective-permute-done | bytes 147488 | tf_op jit(solution)/shard_map/ppermute | solution.py:116
  66.6 1.5 %collective-permute-done.12 = bf16[576,128]{1,0:T(8,128)(2,1)S(1)} collective-permute-done((bf16[576,128]{1,0:T(8,128)(2,1)S(1)}, bf16[576,128]{1,0:T(8,128)(2,1)S(1)}, u32[]{:S(2)}, u32[]{:S(2)}) %collective-permute-start.12) | collective-permute-done | bytes 147488 | tf_op jit(solution)/shard_map/ppermute | solution.py:116
  68.1 0.0 collective-permute-done.13
  68.2 0.1 collective-permute-start.14
  68.2 1.2 %shard_map.88 = (f32[3456,128]{1,0:T(8,128)}, f32[1152,128]{1,0:T(8,128)}) custom-call(s32[1]{0:T(128)} %bitcast.4.which, bf16[2304,128]{1,0:T(8,128)(2,1)S(1)} %constant_dynamic-update-slice_fusion.half), custom_call_target="tpu_custom_call" | custom-call | bytes 4194304 | tf_op jit(solution)/shard_map/pallas_call | solution.py:144
  69.4 0.8 %collective-permute-done.14.half = bf16[2304,128]{1,0:T(8,128)(2,1)S(1)} collective-permute-done((bf16[2304,128]{1,0:T(8,128)(2,1)S(1)}, bf16[2304,128]{1,0:T(8,128)(2,1)S(1)}, u32[]{:S(2)}, u32[]{:S(2)}) %collective-permute-start.14) | collective-permute-done | bytes 589856 | tf_op jit(solution)/shard_map/ppermute | solution.py:162
  70.2 1.2 %shard_map.89 = (f32[3456,128]{1,0:T(8,128)}, f32[1152,128]{1,0:T(8,128)}) custom-call(s32[1]{0:T(128)} %bitcast.35.which, bf16[2304,128]{1,0:T(8,128)(2,1)S(1)} %collective-permute-done.14.half, f32[3456,128]{1,0:T(8,128)} %get-tuple-element.46.refs_0_, f32[1152,128]{1,0:T(8,128)} %get-tuple-element.47.refs_1_), custom_call_target="tpu_custom_call", output_to_operand_aliasing={{0}: (2, {}), {1}: (3, {})} | custom-call | bytes 4194304 | tf_op jit(solution)/shard_map/pallas_call | solution.py:144
  (27 shorter events, 0.5 us)
Async XLA Ops:
  1.4 11.4 %copy-start = (bf16[1,8,8,8,128]{4,3,2,1,0:T(8,128)(2,1)S(1)}, bf16[1,8,8,8,128]{4,3,2,1,0:T(8,128)(2,1)}, u32[]{:S(2)}) copy-start(bf16[1,8,8,8,128]{4,3,2,1,0:T(8,128)(2,1)} %param.9) | copy-start | bytes 393220
  2.3 10.7 %copy-start.7 = (bf16[1,8,16,16,128]{4,3,2,1,0:T(8,128)(2,1)S(1)}, bf16[1,8,16,16,128]{4,3,2,1,0:T(8,128)(2,1)}, u32[]{:S(2)}) copy-start(bf16[1,8,16,16,128]{4,3,2,1,0:T(8,128)(2,1)} %param.5) | copy-start | bytes 1572868
  2.4 8.7 %collective-permute-start = (bf16[320,128]{1,0:T(8,128)(2,1)S(1)}, bf16[320,128]{1,0:T(8,128)(2,1)S(1)}, u32[]{:S(2)}, u32[]{:S(2)}) collective-permute-start(bf16[320,128]{1,0:T(8,128)(2,1)S(1)} %get-tuple-element.71), channel_id=1, source_target_pairs={{4,8},{8,4},{5,9},{9,5},{6,10},{10,6},{7,11},{11,7},{20,24},{24,20... | collective-permute-start | bytes 245768 | tf_op jit(solution)/shard_map/ppermute | solution.py:26
  3.2 9.6 %collective-permute-start.1 = (bf16[320,128]{1,0:T(8,128)(2,1)S(1)}, bf16[320,128]{1,0:T(8,128)(2,1)S(1)}, u32[]{:S(2)}, u32[]{:S(2)}) collective-permute-start(bf16[320,128]{1,0:T(8,128)(2,1)S(1)} %get-tuple-element.72), channel_id=1, source_target_pairs={{0,4},{4,0},{8,12},{12,8},{1,5},{5,1},{9,13},{13,9},{2,6},{6,2},{1... | collective-permute-start | bytes 245768 | tf_op jit(solution)/shard_map/ppermute | solution.py:25
  10.2 5.5 %copy-start.2 = (bf16[3,3,3,128,128]{4,3,2,1,0:T(8,128)(2,1)S(1)}, bf16[3,3,3,128,128]{4,3,2,1,0:T(8,128)(2,1)}, u32[]{:S(2)}) copy-start(bf16[3,3,3,128,128]{4,3,2,1,0:T(8,128)(2,1)} %param.7) | copy-start | bytes 2654212
  13.4 6.8 %collective-permute-start.3 = (bf16[400,128]{1,0:T(8,128)(2,1)S(1)}, bf16[400,128]{1,0:T(8,128)(2,1)S(1)}, u32[]{:S(2)}, u32[]{:S(2)}) collective-permute-start(bf16[400,128]{1,0:T(8,128)(2,1)S(1)} %get-tuple-element.67), channel_id=1, source_target_pairs={{0,1},{1,0},{2,3},{3,2},{4,5},{5,4},{6,7},{7,6},{8,9},{9,8},{10,11... | collective-permute-start | bytes 307208 | tf_op jit(solution)/shard_map/ppermute | solution.py:25
  15.0 5.1 %collective-permute-start.2 = (bf16[400,128]{1,0:T(8,128)(2,1)S(1)}, bf16[400,128]{1,0:T(8,128)(2,1)S(1)}, u32[]{:S(2)}, u32[]{:S(2)}) collective-permute-start(bf16[400,128]{1,0:T(8,128)(2,1)S(1)} %get-tuple-element.68), channel_id=1, source_target_pairs={{1,2},{2,1},{5,6},{6,5},{9,10},{10,9},{13,14},{14,13},{17,18},{18,... | collective-permute-start | bytes 307208 | tf_op jit(solution)/shard_map/ppermute | solution.py:26
  19.1 1.0 %copy-start.3 = (f32[8,288,128]{2,1,0:T(8,128)}, f32[8,288,128]{2,1,0:T(8,128)S(1)}, u32[]{:S(2)}) copy-start(f32[8,288,128]{2,1,0:T(8,128)S(1)} %shard_map.84.pre) | copy-start | bytes 3538948
  20.1 1.0 %copy-start.1 = (bf16[3,3,128,128]{3,2,1,0:T(8,128)(2,1)S(1)}, bf16[3,3,128,128]{3,2,1,0:T(8,128)(2,1)}, u32[]{:S(2)}) copy-start(bf16[3,3,128,128]{3,2,1,0:T(8,128)(2,1)} %param.8) | copy-start | bytes 884740
  20.3 1.3 %copy-start.4 = (f32[8,288,128]{2,1,0:T(8,128)S(1)}, f32[8,288,128]{2,1,0:T(8,128)}, u32[]{:S(2)}) copy-start(f32[8,288,128]{2,1,0:T(8,128)} %copy-done.3) | copy-start | bytes 3538948
  30.3 0.8 %copy-start.5 = (bf16[8,288,128]{2,1,0:T(8,128)(2,1)}, bf16[8,288,128]{2,1,0:T(8,128)(2,1)S(1)}, u32[]{:S(2)}) copy-start(bf16[8,288,128]{2,1,0:T(8,128)(2,1)S(1)} %get-tuple-element.36.own_grad) | copy-start | bytes 1769476
  31.1 2.2 %collective-permute-start.4 = (bf16[2304,128]{1,0:T(8,128)(2,1)}, bf16[2304,128]{1,0:T(8,128)(2,1)S(1)}, u32[]{:S(2)}, u32[]{:S(2)}) collective-permute-start(bf16[2304,128]{1,0:T(8,128)(2,1)} %get-tuple-element.32), channel_id=1, source_target_pairs={{0,16},{16,0},{1,17},{17,1},{2,18},{18,2},{3,19},{19,3},{4,20},{20... | collective-permute-start | bytes 1769480 | tf_op jit(solution)/shard_map/ppermute | solution.py:159
  31.1 5.9 %copy-start.6 = (bf16[8,288,128]{2,1,0:T(8,128)(2,1)S(1)}, bf16[8,288,128]{2,1,0:T(8,128)(2,1)}, u32[]{:S(2)}) copy-start(bf16[8,288,128]{2,1,0:T(8,128)(2,1)} %copy-done.5) | copy-start | bytes 1769476
  33.4 7.9 %collective-permute-start.5 = (bf16[576,128]{1,0:T(8,128)(2,1)S(1)}, bf16[576,128]{1,0:T(8,128)(2,1)S(1)}, u32[]{:S(2)}, u32[]{:S(2)}) collective-permute-start(bf16[576,128]{1,0:T(8,128)(2,1)S(1)} %get-tuple-element.33), channel_id=1, source_target_pairs={{0,12},{4,8},{8,4},{12,0},{1,13},{5,9},{9,5},{13,1},{2,14},{6,10},... | collective-permute-start | bytes 442376 | tf_op jit(solution)/shard_map/ppermute | solution.py:87
  34.9 8.5 %collective-permute-start.6 = (bf16[576,128]{1,0:T(8,128)(2,1)S(1)}, bf16[576,128]{1,0:T(8,128)(2,1)S(1)}, u32[]{:S(2)}, u32[]{:S(2)}) collective-permute-start(bf16[576,128]{1,0:T(8,128)(2,1)S(1)} %get-tuple-element.34), channel_id=1, source_target_pairs={{0,8},{4,12},{8,0},{12,4},{1,9},{5,13},{9,1},{13,5},{2,10},{6,14},... | collective-permute-start | bytes 442376 | tf_op jit(solution)/shard_map/ppermute | solution.py:87
  35.6 7.9 %collective-permute-start.7 = (bf16[576,128]{1,0:T(8,128)(2,1)S(1)}, bf16[576,128]{1,0:T(8,128)(2,1)S(1)}, u32[]{:S(2)}, u32[]{:S(2)}) collective-permute-start(bf16[576,128]{1,0:T(8,128)(2,1)S(1)} %get-tuple-element.35), channel_id=1, source_target_pairs={{0,4},{4,0},{8,12},{12,8},{1,5},{5,1},{9,13},{13,9},{2,6},{6,2},{1... | collective-permute-start | bytes 442376 | tf_op jit(solution)/shard_map/ppermute | solution.py:87
  43.6 6.9 %collective-permute-start.8 = (bf16[288,128]{1,0:T(8,128)(2,1)S(1)}, bf16[288,128]{1,0:T(8,128)(2,1)S(1)}, u32[]{:S(2)}, u32[]{:S(2)}) collective-permute-start(bf16[288,128]{1,0:T(8,128)(2,1)S(1)} %dynamic-slice_convert_fusion), channel_id=1, source_target_pairs={{0,1},{1,0},{2,3},{3,2},{4,5},{5,4},{6,7},{7,6},{8,9},{9,8},{10,11... | collective-permute-start | bytes 221192 | tf_op jit(solution)/shard_map/ppermute | solution.py:99
  50.5 5.4 %collective-permute-start.9 = (bf16[288,128]{1,0:T(8,128)(2,1)S(1)}, bf16[288,128]{1,0:T(8,128)(2,1)S(1)}, u32[]{:S(2)}, u32[]{:S(2)}) collective-permute-start(bf16[288,128]{1,0:T(8,128)(2,1)S(1)} %fusion.4), channel_id=1, source_target_pairs={{0,2},{1,3},{2,0},{3,1},{4,6},{5,7},{6,4},{7,5},{8,10},{9,11},{10,... | collective-permute-start | bytes 221192 | tf_op jit(solution)/shard_map/ppermute | solution.py:101
  56.0 4.4 %collective-permute-start.10 = (bf16[288,128]{1,0:T(8,128)(2,1)S(1)}, bf16[288,128]{1,0:T(8,128)(2,1)S(1)}, u32[]{:S(2)}, u32[]{:S(2)}) collective-permute-start(bf16[288,128]{1,0:T(8,128)(2,1)S(1)} %add_convert_fusion), channel_id=1, source_target_pairs={{0,1},{1,0},{2,3},{3,2},{4,5},{5,4},{6,7},{7,6},{8,9},{9,8},{10,11... | collective-permute-start | bytes 221192 | tf_op jit(solution)/shard_map/ppermute | solution.py:104
  60.4 6.2 %collective-permute-start.11 = (bf16[576,128]{1,0:T(8,128)(2,1)S(1)}, bf16[576,128]{1,0:T(8,128)(2,1)S(1)}, u32[]{:S(2)}, u32[]{:S(2)}) collective-permute-start(bf16[576,128]{1,0:T(8,128)(2,1)S(1)} %bitcast.71), channel_id=1, source_target_pairs={{0,12},{4,8},{8,4},{12,0},{1,13},{5,9},{9,5},{13,1},{2,14},{6,10},... | collective-permute-start | bytes 442376 | tf_op jit(solution)/shard_map/ppermute | solution.py:116
  61.9 6.2 %collective-permute-start.12 = (bf16[576,128]{1,0:T(8,128)(2,1)S(1)}, bf16[576,128]{1,0:T(8,128)(2,1)S(1)}, u32[]{:S(2)}, u32[]{:S(2)}) collective-permute-start(bf16[576,128]{1,0:T(8,128)(2,1)S(1)} %bitcast.72), channel_id=1, source_target_pairs={{0,8},{4,12},{8,0},{12,4},{1,9},{5,13},{9,1},{13,5},{2,10},{6,14},... | collective-permute-start | bytes 442376 | tf_op jit(solution)/shard_map/ppermute | solution.py:116
  62.5 5.6 %collective-permute-start.13 = (bf16[576,128]{1,0:T(8,128)(2,1)S(1)}, bf16[576,128]{1,0:T(8,128)(2,1)S(1)}, u32[]{:S(2)}, u32[]{:S(2)}) collective-permute-start(bf16[576,128]{1,0:T(8,128)(2,1)S(1)} %bitcast.73), channel_id=1, source_target_pairs={{0,4},{4,0},{8,12},{12,8},{1,5},{5,1},{9,13},{13,9},{2,6},{6,2},{1... | collective-permute-start | bytes 442376 | tf_op jit(solution)/shard_map/ppermute | solution.py:116
  68.2 2.1 %collective-permute-start.14 = (bf16[2304,128]{1,0:T(8,128)(2,1)S(1)}, bf16[2304,128]{1,0:T(8,128)(2,1)S(1)}, u32[]{:S(2)}, u32[]{:S(2)}) collective-permute-start(bf16[2304,128]{1,0:T(8,128)(2,1)S(1)} %constant_dynamic-update-slice_fusion.half), channel_id=1, source_target_pairs={{0,16},{16,0},{1,17},{17,1},{2,18},{18,2},{3,19},{19,3},{4,20},{20... | collective-permute-start | bytes 1769480 | tf_op jit(solution)/shard_map/ppermute | solution.py:162

commit v4 on v3

--- a/solution.py
+++ b/solution.py
@@ -1,3 +1,5 @@
+import functools
+
 import jax
 import jax.numpy as jnp
 from jax import lax
@@ -22,8 +24,8 @@
     even = lax.axis_index(axis) % 2 == 0
     inner = [(i, i ^ 1) for i in range(count - count % 2)]
     outer = [(i, ((i + 1) ^ 1) - 1) for i in range(1, count - 1 + count % 2)]
+    b = lax.ppermute(jnp.where(even, low_edge, high_edge), axis, outer)
     a = lax.ppermute(jnp.where(even, high_edge, low_edge), axis, inner)
-    b = lax.ppermute(jnp.where(even, low_edge, high_edge), axis, outer)
     return jnp.where(even, b, a), jnp.where(even, a, b)
 
 
@@ -91,22 +93,6 @@
     return total, beside
 
 
-def line_sum(x, axis):
-    bits, mine = lax.axis_size(axis).bit_length() - 1, lax.axis_index(axis)
-    for bit in range(bits - 1):
-        side, half = (mine >> bit) & 1, x.shape[0] // 2
-        sent = part(x, 1 - side, half).astype(BF)
-        x = part(x, side, half) + lax.ppermute(sent, axis, flip(axis, 1 << bit)).astype(F32)
-    x = lax.reduce_precision(x, 8, 7)
-    got = lax.ppermute(x.astype(BF), axis, flip(axis, 1 << (bits - 1)))
-    y = (x + got.astype(F32)).astype(BF)
-    for bit in reversed(range(bits - 1)):
-        got = lax.ppermute(y, axis, flip(axis, 1 << bit))
-        low = ((mine >> bit) & 1) == 0
-        y = jnp.where(low, jnp.stack([y, got]), jnp.stack([got, y])).reshape(-1, y.shape[-1])
-    return y
-
-
 def direct_gather(y, axis):
     count, mine = lax.axis_size(axis), lax.axis_index(axis)
     share = y.shape[0]
@@ -158,7 +144,13 @@
     swap = flip("clip", 1)
     got = lax.ppermute(sent, "clip", swap)
     x, beside = direct_scatter(kept, got, "row", beside)
-    y = direct_gather(line_sum(x, "col"), "row")
+    count, mine = lax.axis_size("col"), lax.axis_index("col")
+    share = x.shape[0] // count
+    sums = part(x, mine, share)
+    for mask in range(1, count):
+        term = lax.ppermute(part(x, mine ^ mask, share).astype(BF), "col", flip("col", mask))
+        sums = sums + term.astype(F32)
+    y = direct_gather(direct_gather(sums.astype(BF), "col"), "row")
     other = lax.ppermute(y, "clip", swap)
     shapes = (
         jax.ShapeDtypeStruct((main_rows, y.shape[1]), F32),
@@ -235,7 +227,7 @@
 
 def main_kernel(
     flags, wide, grad_wide, pre, kernel_main, w_grad, w_down, latent_grad,
-    kept, sent, own_out, side_out, latent,
+    kept, sent, early_out, late_out, side_out, latent,
     w_main, x32, side32, x_taps, v32, fix, l32, act_grad, side_back, side_act, act,
     act_taps, grad_t, total, down_total,
 ):
@@ -326,7 +318,7 @@
     side_act[...], side_grad = pointwise(side_pre, side_back[...], side_mask)
     side_out[...] = side_grad.astype(BF)
 
-    def frame(t, carry):
+    def frame(own_out, base, t, carry):
         live = jnp.where(t < count, 1.0, 0.0).astype(F32)
         last = frames + t
         v32[...] = pre[t].reshape(ext, cols, channels)
@@ -337,7 +329,7 @@
         )
         act[:, LEFT : LEFT + cols, :] = own_act
         act[:, LEFT + cols : LEFT + cols + 1, :] = side_act[:, pl.ds(last, 1), :]
-        own_out[t] = own_grad.reshape(own, channels).astype(BF)
+        own_out[t - base] = own_grad.reshape(own, channels).astype(BF)
         inner = own_grad.reshape(own, channels)[cols : cols + rows * cols]
         grad_t[t] = inner.T.astype(BF)
         for a in range(3):
@@ -353,7 +345,8 @@
                 act_taps[t, :, at : at + channels] = tap
         return carry
 
-    lax.fori_loop(0, frames, frame, 0)
+    for base, own_out in ((0, early_out), (frames // 2, late_out)):
+        lax.fori_loop(base, base + frames // 2, functools.partial(frame, own_out, base), 0)
 
     flat = act_taps[...].reshape(frames * half_rows * half_cols, 9 * channels)
     latent[...] = dot(flat, w_down[...]).astype(BF)
@@ -398,8 +391,9 @@
         emit(sent, kept)
 
 
-def back_kernel(own_grad, side_grad, kernel_main, video_grad, w_back, total, side32, g32, grad_taps):
-    frames, own, channels = own_grad.shape
+def back_kernel(early_grad, late_grad, side_grad, kernel_main, video_grad, w_back, total, side32, g32, grad_taps):
+    half, own, channels = early_grad.shape
+    frames = 2 * half
     inner = video_grad.shape[1]
     cols = (own - inner) // 2
     ext = own // cols
@@ -411,11 +405,11 @@
             block = kernel_main[9 * kt + 8 - tap].astype(F32).T.astype(BF)
             w_back[rows_at : rows_at + channels, cols_at : cols_at + channels] = block
 
-    def group(i, carry):
+    def group(own_grad, i, carry):
         lines = []
         for g in range(GROUP):
             t = i * GROUP + g
-            g32[:, LEFT : LEFT + cols, :] = own_grad[t].astype(F32).reshape(ext, cols, channels)
+            g32[:, LEFT : LEFT + cols, :] = own_grad[t % half].astype(F32).reshape(ext, cols, channels)
             g32[:, LEFT - 1 : LEFT, :] = side32[:, pl.ds(t, 1), :]
             g32[:, LEFT + cols : LEFT + cols + 1, :] = side32[:, pl.ds(frames + t, 1), :]
             for kw in range(3):
@@ -436,7 +430,9 @@
             total[t] += parts[0][here]
         return carry
 
-    lax.fori_loop(0, frames // GROUP, group, 0)
+    for base, own_grad in ((0, early_grad), (half, late_grad)):
+        first, last = base // GROUP, (base + half) // GROUP
+        lax.fori_loop(first, last, functools.partial(group, own_grad), 0)
     video_grad[0] = (total[0] + total[1] + total[2]).astype(BF)
 
     def store(t, carry):
@@ -501,17 +497,18 @@
         ]
     )
     w_down = kernel_down.reshape(9 * channels, channels)
-    kept, sent, own_grad, side_grad, latent = pl.pallas_call(
+    kept, sent, early_grad, late_grad, side_grad, latent = pl.pallas_call(
         main_kernel,
         out_shape=(
             jax.ShapeDtypeStruct((18 * channels, channels), F32),
             jax.ShapeDtypeStruct((18 * channels, channels), BF),
-            jax.ShapeDtypeStruct((frames, own, channels), BF),
+            jax.ShapeDtypeStruct((frames // 2, own, channels), BF),
+            jax.ShapeDtypeStruct((frames // 2, own, channels), BF),
             jax.ShapeDtypeStruct((ext, 2 * frames, channels), BF),
             jax.ShapeDtypeStruct((outs, channels), BF),
         ),
         in_specs=[pl.BlockSpec(memory_space=pltpu.SMEM)] + [vmem] * 7,
-        out_specs=(vmem,) * 5,
+        out_specs=(vmem,) * 6,
         scratch_shapes=[
             pltpu.VMEM((9 * channels, 3 * channels), BF),
             pltpu.VMEM((rows + 4, cols + 8, channels), F32),
@@ -548,7 +545,7 @@
     video_grad = pl.pallas_call(
         back_kernel,
         out_shape=jax.ShapeDtypeStruct((frames, rows * cols, channels), BF),
-        in_specs=[vmem] * 3,
+        in_specs=[vmem] * 4,
         out_specs=vmem,
         scratch_shapes=[
             pltpu.VMEM((9 * channels, 3 * channels), BF),
@@ -563,7 +560,7 @@
             bytes_accessed=4 << 20,
             transcendentals=0,
         ),
-    )(own_grad, side_grad, taps)
+    )(early_grad, late_grad, side_grad, taps)
     main_grad, down_grad, video_grad = reduce_all(kept, sent, video_grad, 27 * channels)
     main_grad = main_grad.reshape(kernel_main.shape)
     down_grad = down_grad.reshape(kernel_down.shape)

time: 71.9 us -> 71.7 us (level)
  starting transfers between devices: 23.9 us -> 26.4 us
  waiting for transfers between devices: 19.7 us -> 17.3 us
    ppermute x3, waiting for transfers between devices: 8.86 us -> 3.95 us  [reduce_all(): lax.ppermute(part(x, mine ^ mask, share).astype(BF), 'col', flip('col', m...]
    ppermute x3 -> x6, starting transfers between devices: 3.55 us -> 8 us  [direct_gather(): got = lax.ppermute(y, axis, flip(axis, mask))]
    ppermute x3 -> x6, waiting for transfers between devices: 3.99 us -> 6.26 us  [direct_gather(): got = lax.ppermute(y, axis, flip(axis, mask))]
    ppermute x3, starting transfers between devices: 7.89 us -> 5.93 us  [reduce_all(): lax.ppermute(part(x, mine ^ mask, share).astype(BF), 'col', flip('col', m...]
  transfers between devices with their start and end apart: 15 -> 18, of which waited for: 9 -> 11; matrix products, arithmetic and copies ran while one was open for 2% -> 2% of each run, Pallas kernels for 13% -> 12%
where the time goes in v4:
time: 71.7 us; the launch traced here: 71.4 us
  starting transfers between devices  26.4 us (37%)
  Pallas kernels  18.7 us (26%)
  waiting for transfers between devices  17.3 us (24%)
  local copies, waits for them, and re-layouts  5.69 us (8%)
  between operations  1.9 us (3%)
  other arithmetic  1.36 us (2%)
    pallas_call x1, Pallas kernels, on_device(): pl.pallas_call(main_kernel, out_shape=(jax.ShapeDtypeStruct((18 * channel...  8.75 us
    ppermute x6, starting transfers between devices, direct_gather(): got = lax.ppermute(y, axis, flip(axis, mask))  8 us
    ppermute x2, starting transfers between devices, exchange(): a = lax.ppermute(jnp.where(even, high_edge, low_edge), axis, inner)  7.38 us
    ppermute x6, waiting for transfers between devices, direct_gather(): got = lax.ppermute(y, axis, flip(axis, mask))  6.26 us
    ppermute x3, starting transfers between devices, reduce_all(): lax.ppermute(part(x, mine ^ mask, share).astype(BF), 'col', flip('col', m...  5.93 us
    pallas_call x1, Pallas kernels, on_device(): pl.pallas_call(back_kernel, out_shape=jax.ShapeDtypeStruct((frames, rows...  4.07 us
    ppermute x3, waiting for transfers between devices, reduce_all(): lax.ppermute(part(x, mine ^ mask, share).astype(BF), 'col', flip('col', m...  3.95 us
    ppermute x3, starting transfers between devices, direct_scatter(): lax.ppermute(sends[mask - 1], axis, flip(axis, mask))  3.55 us
  transfers between devices with their start and end apart: 18, of which 11 were waited for; matrix products, arithmetic and copies ran while one was open for 2% of the time, Pallas kernels for 12%

profile of v4, /device:TPU:0, one launch (start us, length us, event | category | flops | bytes accessed | tf_op | source)
XLA Modules:
  0.0 71.4 jit_solution(760888567396996972)
XLA Ops:
  0.6 0.7 %slice_bitcast_fusion.12 = (bf16[64,128]{1,0:T(8,128)(2,1)S(1)}, bf16[64,128]{1,0:T(8,128)(2,1)S(1)}) fusion(bf16[8,8,8,128]{3,2,1,0:T(8,128)(2,1)} %bitcast.51), kind=kLoop, calls=%fused_computation.41 | loop fusion | bytes 65536 | tf_op jit(solution)/shard_map/reshape | solution.py:33
  1.4 0.9 %fusion.6 = (bf16[8,2,16,128]{3,2,1,0:T(8,128)(2,1)S(1)}, bf16[8,2,16,128]{3,2,1,0:T(8,128)(2,1)S(1)}) fusion(bf16[8,16,16,128]{3,2,1,0:T(8,128)(2,1)} %bitcast.59), kind=kLoop, calls=%fused_computation.51 | loop fusion | bytes 262144 | tf_op jit(solution)/shard_map/slice | solution.py:44
  2.3 0.0 copy-start.7
  2.4 0.8 %collective-permute-start = (bf16[320,128]{1,0:T(8,128)(2,1)S(1)}, bf16[320,128]{1,0:T(8,128)(2,1)S(1)}, u32[]{:S(2)}, u32[]{:S(2)}) collective-permute-start(bf16[320,128]{1,0:T(8,128)(2,1)S(1)} %get-tuple-element.78), channel_id=1, source_target_pairs={{4,8},{8,4},{5,9},{9,5},{6,10},{10,6},{7,11},{11,7},{20,24},{24,20... | collective-permute-start | bytes 245768 | tf_op jit(solution)/shard_map/ppermute | solution.py:27
  3.2 5.7 %collective-permute-start.1 = (bf16[320,128]{1,0:T(8,128)(2,1)S(1)}, bf16[320,128]{1,0:T(8,128)(2,1)S(1)}, u32[]{:S(2)}, u32[]{:S(2)}) collective-permute-start(bf16[320,128]{1,0:T(8,128)(2,1)S(1)} %get-tuple-element.79), channel_id=1, source_target_pairs={{0,4},{4,0},{8,12},{12,8},{1,5},{5,1},{9,13},{13,9},{2,6},{6,2},{1... | collective-permute-start | bytes 245768 | tf_op jit(solution)/shard_map/ppermute | solution.py:28
  8.9 1.2 %copy.14 = bf16[3,3,128,128]{2,3,1,0:T(8,128)(2,1)S(1)} copy(bf16[3,3,128,128]{3,2,1,0:T(8,128)(2,1)} %param.8) | data formatting | bytes 589824 | tf_op args[3]
  10.2 0.0 copy-start.2
  11.0 0.1 stack.39.flags
  11.0 0.0 collective-permute-done
  11.0 1.7 %collective-permute-done.1 = bf16[320,128]{1,0:T(8,128)(2,1)S(1)} collective-permute-done((bf16[320,128]{1,0:T(8,128)(2,1)S(1)}, bf16[320,128]{1,0:T(8,128)(2,1)S(1)}, u32[]{:S(2)}, u32[]{:S(2)}) %collective-permute-start.1) | collective-permute-done | bytes 81952 | tf_op jit(solution)/shard_map/ppermute | solution.py:28
  12.8 0.0 copy-done
  12.8 0.2 maximum_reduce_fusion
  13.1 0.0 copy-done.7
  13.1 0.1 pad_maximum_fusion.1.tall
  13.2 0.1 fusion.5
  13.4 1.6 %collective-permute-start.3 = (bf16[400,128]{1,0:T(8,128)(2,1)S(1)}, bf16[400,128]{1,0:T(8,128)(2,1)S(1)}, u32[]{:S(2)}, u32[]{:S(2)}) collective-permute-start(bf16[400,128]{1,0:T(8,128)(2,1)S(1)} %get-tuple-element.74), channel_id=1, source_target_pairs={{0,1},{1,0},{2,3},{3,2},{4,5},{5,4},{6,7},{7,6},{8,9},{9,8},{10,11... | collective-permute-start | bytes 307208 | tf_op jit(solution)/shard_map/ppermute | solution.py:28
  15.0 0.7 collective-permute-start.2
  15.7 0.0 copy-done.2
  15.7 3.4 %shard_map.84.pre = f32[8,288,128]{2,1,0:T(8,128)S(1)} custom-call(bf16[8,20,16,128]{3,2,1,0:T(8,128)(2,1)S(1)} %pad_maximum_fusion.1.tall, bf16[27,128,128]{2,1,0:T(8,128)(2,1)S(1)} %bitcast.56), custom_call_target="tpu_custom_call" | custom-call | flops 2038431744 | bytes 4194304 | tf_op jit(solution)/shard_map/pallas_call | solution.py:467
  19.1 0.0 copy-start.3
  19.1 1.0 %copy-done.3 = f32[8,288,128]{2,1,0:T(8,128)} copy-done((f32[8,288,128]{2,1,0:T(8,128)}, f32[8,288,128]{2,1,0:T(8,128)S(1)}, u32[]{:S(2)}) %copy-start.3) | copy-done | bytes 1179672
  20.1 0.0 collective-permute-done.3
  20.1 0.0 collective-permute-done.2
  20.3 0.0 copy-start.4
  20.3 0.6 pad_maximum_fusion.wide
  20.9 0.2 pad_maximum_fusion.2.grad_wide
  21.1 0.0 copy-done.1
  21.1 0.5 copy-done.4
  21.6 8.7 %shard_map.85 = (f32[2304,128]{1,0:T(8,128)S(1)}, bf16[2304,128]{1,0:T(8,128)(2,1)}, bf16[4,288,128]{2,1,0:T(8,128)(2,1)S(1)}, bf16[4,288,128]{2,1,0:T(8,128)(2,...) custom-call(s32[6]{0:T(128)S(1)} %stack.39.flags, bf16[8,20,20,128]{3,2,1,0:T(8,128)(2,1)S(1)} %pad_maximum_fusion.wide, ...), custom_call_target="tpu_custom_call" | custom-call | flops 2684354560 | bytes 12582912 | tf_op jit(solution)/shard_map/pallas_call | solution.py:500
  30.3 0.7 copy-done.5
  31.0 0.0 collective-permute-start.4
  31.0 2.2 %collective-permute-done.4.got = bf16[2304,128]{1,0:T(8,128)(2,1)S(1)} collective-permute-done((bf16[2304,128]{1,0:T(8,128)(2,1)}, bf16[2304,128]{1,0:T(8,128)(2,1)S(1)}, u32[]{:S(2)}, u32[]{:S(2)}) %collective-permute-start.4) | collective-permute-done | bytes 589856 | tf_op jit(solution)/shard_map/ppermute | solution.py:145
  33.2 0.1 shard_map.86
  33.3 1.5 %collective-permute-start.5 = (bf16[576,128]{1,0:T(8,128)(2,1)S(1)}, bf16[576,128]{1,0:T(8,128)(2,1)S(1)}, u32[]{:S(2)}, u32[]{:S(2)}) collective-permute-start(bf16[576,128]{1,0:T(8,128)(2,1)S(1)} %get-tuple-element.34), channel_id=1, source_target_pairs={{0,12},{4,8},{8,4},{12,0},{1,13},{5,9},{9,5},{13,1},{2,14},{6,10},... | collective-permute-start | bytes 442376 | tf_op jit(solution)/shard_map/ppermute | solution.py:89
  34.8 0.6 collective-permute-start.6
  35.5 1.4 %collective-permute-start.7 = (bf16[576,128]{1,0:T(8,128)(2,1)S(1)}, bf16[576,128]{1,0:T(8,128)(2,1)S(1)}, u32[]{:S(2)}, u32[]{:S(2)}) collective-permute-start(bf16[576,128]{1,0:T(8,128)(2,1)S(1)} %get-tuple-element.36), channel_id=1, source_target_pairs={{0,4},{4,0},{8,12},{12,8},{1,5},{5,1},{9,13},{13,9},{2,6},{6,2},{1... | collective-permute-start | bytes 442376 | tf_op jit(solution)/shard_map/ppermute | solution.py:89
  36.9 4.1 %shard_map.87 = bf16[8,256,128]{2,1,0:T(8,128)(2,1)} custom-call(bf16[4,288,128]{2,1,0:T(8,128)(2,1)S(1)} %get-tuple-element.37.early_grad, bf16[4,288,128]{2,1,0:T(8,128)(2,1)S(1)} %copy-done.6, bf16[18,16,128]{2,1,0:T(8,128)(2,1)S(1)} %get-tuple-element.39.side_grad, bf16[27,128,128]{2,1,0:T(8,128)(2,1)S(1)} %bitcast.58), custom_call_target="tpu_custom_call" | custom-call | flops 1811939328 | bytes 4194304 | tf_op jit(solution)/shard_map/pallas_call | solution.py:545
  41.0 0.1 collective-permute-done.5
  41.0 2.3 %collective-permute-done.6 = bf16[576,128]{1,0:T(8,128)(2,1)S(1)} collective-permute-done((bf16[576,128]{1,0:T(8,128)(2,1)S(1)}, bf16[576,128]{1,0:T(8,128)(2,1)S(1)}, u32[]{:S(2)}, u32[]{:S(2)}) %collective-permute-start.6) | collective-permute-done | bytes 147488 | tf_op jit(solution)/shard_map/ppermute | solution.py:89
  43.4 0.0 collective-permute-done.7
  43.4 0.1 convert_add_fusion
  43.5 2.5 %collective-permute-start.10 = (bf16[144,128]{1,0:T(8,128)(2,1)S(1)}, bf16[144,128]{1,0:T(8,128)(2,1)S(1)}, u32[]{:S(2)}, u32[]{:S(2)}) collective-permute-start(bf16[144,128]{1,0:T(8,128)(2,1)S(1)} %get-tuple-element.61), channel_id=1, source_target_pairs={{0,3},{1,2},{2,1},{3,0},{4,7},{5,6},{6,5},{7,4},{8,11},{9,10},{10,... | collective-permute-start | bytes 110600 | tf_op jit(solution)/shard_map/ppermute | solution.py:151
  46.0 3.4 %collective-permute-start.9 = (bf16[144,128]{1,0:T(8,128)(2,1)S(1)}, bf16[144,128]{1,0:T(8,128)(2,1)S(1)}, u32[]{:S(2)}, u32[]{:S(2)}) collective-permute-start(bf16[144,128]{1,0:T(8,128)(2,1)S(1)} %get-tuple-element.62), channel_id=1, source_target_pairs={{0,2},{1,3},{2,0},{3,1},{4,6},{5,7},{6,4},{7,5},{8,10},{9,11},{10,... | collective-permute-start | bytes 110600 | tf_op jit(solution)/shard_map/ppermute | solution.py:151
  49.4 0.0 collective-permute-start.8
  49.4 0.0 collective-permute-done.10
  49.4 3.1 %collective-permute-done.9 = bf16[144,128]{1,0:T(8,128)(2,1)S(1)} collective-permute-done((bf16[144,128]{1,0:T(8,128)(2,1)S(1)}, bf16[144,128]{1,0:T(8,128)(2,1)S(1)}, u32[]{:S(2)}, u32[]{:S(2)}) %collective-permute-start.9) | collective-permute-done | bytes 36896 | tf_op jit(solution)/shard_map/ppermute | solution.py:151
  52.5 0.8 %collective-permute-done.8 = bf16[144,128]{1,0:T(8,128)(2,1)S(1)} collective-permute-done((bf16[144,128]{1,0:T(8,128)(2,1)S(1)}, bf16[144,128]{1,0:T(8,128)(2,1)S(1)}, u32[]{:S(2)}, u32[]{:S(2)}) %collective-permute-start.8) | collective-permute-done | bytes 36896 | tf_op jit(solution)/shard_map/ppermute | solution.py:151
  53.4 1.1 %collective-permute-start.11 = (bf16[144,128]{1,0:T(8,128)(2,1)S(1)}, bf16[144,128]{1,0:T(8,128)(2,1)S(1)}, u32[]{:S(2)}, u32[]{:S(2)}) collective-permute-start(bf16[144,128]{1,0:T(8,128)(2,1)S(1)} %get-tuple-element.55), channel_id=1, source_target_pairs={{0,3},{1,2},{2,1},{3,0},{4,7},{5,6},{6,5},{7,4},{8,11},{9,10},{10,... | collective-permute-start | bytes 110600 | tf_op jit(solution)/shard_map/ppermute | solution.py:102
  54.6 0.8 %collective-permute-start.12 = (bf16[144,128]{1,0:T(8,128)(2,1)S(1)}, bf16[144,128]{1,0:T(8,128)(2,1)S(1)}, u32[]{:S(2)}, u32[]{:S(2)}) collective-permute-start(bf16[144,128]{1,0:T(8,128)(2,1)S(1)} %get-tuple-element.55), channel_id=1, source_target_pairs={{0,2},{1,3},{2,0},{3,1},{4,6},{5,7},{6,4},{7,5},{8,10},{9,11},{10,... | collective-permute-start | bytes 110600 | tf_op jit(solution)/shard_map/ppermute | solution.py:102
  55.4 2.5 %collective-permute-start.13 = (bf16[144,128]{1,0:T(8,128)(2,1)S(1)}, bf16[144,128]{1,0:T(8,128)(2,1)S(1)}, u32[]{:S(2)}, u32[]{:S(2)}) collective-permute-start(bf16[144,128]{1,0:T(8,128)(2,1)S(1)} %get-tuple-element.55), channel_id=1, source_target_pairs={{0,1},{1,0},{2,3},{3,2},{4,5},{5,4},{6,7},{7,6},{8,9},{9,8},{10,11... | collective-permute-start | bytes 110600 | tf_op jit(solution)/shard_map/ppermute | solution.py:102
  57.9 1.4 %collective-permute-done.11 = bf16[144,128]{1,0:T(8,128)(2,1)S(1)} collective-permute-done((bf16[144,128]{1,0:T(8,128)(2,1)S(1)}, bf16[144,128]{1,0:T(8,128)(2,1)S(1)}, u32[]{:S(2)}, u32[]{:S(2)}) %collective-permute-start.11) | collective-permute-done | bytes 36896 | tf_op jit(solution)/shard_map/ppermute | solution.py:102
  59.3 0.9 %collective-permute-done.12 = bf16[144,128]{1,0:T(8,128)(2,1)S(1)} collective-permute-done((bf16[144,128]{1,0:T(8,128)(2,1)S(1)}, bf16[144,128]{1,0:T(8,128)(2,1)S(1)}, u32[]{:S(2)}, u32[]{:S(2)}) %collective-permute-start.12) | collective-permute-done | bytes 36896 | tf_op jit(solution)/shard_map/ppermute | solution.py:102
  60.2 0.0 collective-permute-done.13
  60.2 1.5 %collective-permute-start.14 = (bf16[576,128]{1,0:T(8,128)(2,1)S(1)}, bf16[576,128]{1,0:T(8,128)(2,1)S(1)}, u32[]{:S(2)}, u32[]{:S(2)}) collective-permute-start(bf16[576,128]{1,0:T(8,128)(2,1)S(1)} %constant_dynamic-update-slice_fusion.4), channel_id=1, source_target_pairs={{0,12},{4,8},{8,4},{12,0},{1,13},{5,9},{9,5},{13,1},{2,14},{6,10},... | collective-permute-start | bytes 442376 | tf_op jit(solution)/shard_map/ppermute | solution.py:102
  61.7 0.6 collective-permute-start.15
  62.3 1.4 %collective-permute-start.16 = (bf16[576,128]{1,0:T(8,128)(2,1)S(1)}, bf16[576,128]{1,0:T(8,128)(2,1)S(1)}, u32[]{:S(2)}, u32[]{:S(2)}) collective-permute-start(bf16[576,128]{1,0:T(8,128)(2,1)S(1)} %constant_dynamic-update-slice_fusion.4), channel_id=1, source_target_pairs={{0,4},{4,0},{8,12},{12,8},{1,5},{5,1},{9,13},{13,9},{2,6},{6,2},{1... | collective-permute-start | bytes 442376 | tf_op jit(solution)/shard_map/ppermute | solution.py:102
  63.7 0.1 broadcast_in_dim.19
  63.9 2.5 %collective-permute-done.14 = bf16[576,128]{1,0:T(8,128)(2,1)S(1)} collective-permute-done((bf16[576,128]{1,0:T(8,128)(2,1)S(1)}, bf16[576,128]{1,0:T(8,128)(2,1)S(1)}, u32[]{:S(2)}, u32[]{:S(2)}) %collective-permute-start.14) | collective-permute-done | bytes 147488 | tf_op jit(solution)/shard_map/ppermute | solution.py:102
  66.4 1.5 %collective-permute-done.15 = bf16[576,128]{1,0:T(8,128)(2,1)S(1)} collective-permute-done((bf16[576,128]{1,0:T(8,128)(2,1)S(1)}, bf16[576,128]{1,0:T(8,128)(2,1)S(1)}, u32[]{:S(2)}, u32[]{:S(2)}) %collective-permute-start.15) | collective-permute-done | bytes 147488 | tf_op jit(solution)/shard_map/ppermute | solution.py:102
  67.9 0.0 collective-permute-done.16
  67.9 0.1 collective-permute-start.17
  68.0 1.2 %shard_map.88 = (f32[3456,128]{1,0:T(8,128)}, f32[1152,128]{1,0:T(8,128)}) custom-call(s32[1]{0:T(128)} %bitcast.4.which, bf16[2304,128]{1,0:T(8,128)(2,1)S(1)} %constant_dynamic-update-slice_fusion.half), custom_call_target="tpu_custom_call" | custom-call | bytes 4194304 | tf_op jit(solution)/shard_map/pallas_call | solution.py:130
  69.2 0.8 %collective-permute-done.17.half = bf16[2304,128]{1,0:T(8,128)(2,1)S(1)} collective-permute-done((bf16[2304,128]{1,0:T(8,128)(2,1)S(1)}, bf16[2304,128]{1,0:T(8,128)(2,1)S(1)}, u32[]{:S(2)}, u32[]{:S(2)}) %collective-permute-start.17) | collective-permute-done | bytes 589856 | tf_op jit(solution)/shard_map/ppermute | solution.py:154
  70.0 1.2 %shard_map.89 = (f32[3456,128]{1,0:T(8,128)}, f32[1152,128]{1,0:T(8,128)}) custom-call(s32[1]{0:T(128)} %bitcast.35.which, bf16[2304,128]{1,0:T(8,128)(2,1)S(1)} %collective-permute-done.17.half, f32[3456,128]{1,0:T(8,128)} %get-tuple-element.48.refs_0_, f32[1152,128]{1,0:T(8,128)} %get-tuple-element.49.refs_1_), custom_call_target="tpu_custom_call", output_to_operand_aliasing={{0}: (2, {}), {1}: (3, {})} | custom-call | bytes 4194304 | tf_op jit(solution)/shard_map/pallas_call | solution.py:130
  (34 shorter events, 0.5 us)
Async XLA Ops:
  1.4 11.4 %copy-start = (bf16[1,8,8,8,128]{4,3,2,1,0:T(8,128)(2,1)S(1)}, bf16[1,8,8,8,128]{4,3,2,1,0:T(8,128)(2,1)}, u32[]{:S(2)}) copy-start(bf16[1,8,8,8,128]{4,3,2,1,0:T(8,128)(2,1)} %param.9) | copy-start | bytes 393220
  2.3 10.7 %copy-start.7 = (bf16[1,8,16,16,128]{4,3,2,1,0:T(8,128)(2,1)S(1)}, bf16[1,8,16,16,128]{4,3,2,1,0:T(8,128)(2,1)}, u32[]{:S(2)}) copy-start(bf16[1,8,16,16,128]{4,3,2,1,0:T(8,128)(2,1)} %param.5) | copy-start | bytes 1572868
  2.4 8.7 %collective-permute-start = (bf16[320,128]{1,0:T(8,128)(2,1)S(1)}, bf16[320,128]{1,0:T(8,128)(2,1)S(1)}, u32[]{:S(2)}, u32[]{:S(2)}) collective-permute-start(bf16[320,128]{1,0:T(8,128)(2,1)S(1)} %get-tuple-element.78), channel_id=1, source_target_pairs={{4,8},{8,4},{5,9},{9,5},{6,10},{10,6},{7,11},{11,7},{20,24},{24,20... | collective-permute-start | bytes 245768 | tf_op jit(solution)/shard_map/ppermute | solution.py:27
  3.2 9.6 %collective-permute-start.1 = (bf16[320,128]{1,0:T(8,128)(2,1)S(1)}, bf16[320,128]{1,0:T(8,128)(2,1)S(1)}, u32[]{:S(2)}, u32[]{:S(2)}) collective-permute-start(bf16[320,128]{1,0:T(8,128)(2,1)S(1)} %get-tuple-element.79), channel_id=1, source_target_pairs={{0,4},{4,0},{8,12},{12,8},{1,5},{5,1},{9,13},{13,9},{2,6},{6,2},{1... | collective-permute-start | bytes 245768 | tf_op jit(solution)/shard_map/ppermute | solution.py:28
  10.2 5.5 %copy-start.2 = (bf16[3,3,3,128,128]{4,3,2,1,0:T(8,128)(2,1)S(1)}, bf16[3,3,3,128,128]{4,3,2,1,0:T(8,128)(2,1)}, u32[]{:S(2)}) copy-start(bf16[3,3,3,128,128]{4,3,2,1,0:T(8,128)(2,1)} %param.7) | copy-start | bytes 2654212
  13.4 6.8 %collective-permute-start.3 = (bf16[400,128]{1,0:T(8,128)(2,1)S(1)}, bf16[400,128]{1,0:T(8,128)(2,1)S(1)}, u32[]{:S(2)}, u32[]{:S(2)}) collective-permute-start(bf16[400,128]{1,0:T(8,128)(2,1)S(1)} %get-tuple-element.74), channel_id=1, source_target_pairs={{0,1},{1,0},{2,3},{3,2},{4,5},{5,4},{6,7},{7,6},{8,9},{9,8},{10,11... | collective-permute-start | bytes 307208 | tf_op jit(solution)/shard_map/ppermute | solution.py:28
  15.0 5.1 %collective-permute-start.2 = (bf16[400,128]{1,0:T(8,128)(2,1)S(1)}, bf16[400,128]{1,0:T(8,128)(2,1)S(1)}, u32[]{:S(2)}, u32[]{:S(2)}) collective-permute-start(bf16[400,128]{1,0:T(8,128)(2,1)S(1)} %get-tuple-element.75), channel_id=1, source_target_pairs={{1,2},{2,1},{5,6},{6,5},{9,10},{10,9},{13,14},{14,13},{17,18},{18,... | collective-permute-start | bytes 307208 | tf_op jit(solution)/shard_map/ppermute | solution.py:27
  19.1 1.0 %copy-start.3 = (f32[8,288,128]{2,1,0:T(8,128)}, f32[8,288,128]{2,1,0:T(8,128)S(1)}, u32[]{:S(2)}) copy-start(f32[8,288,128]{2,1,0:T(8,128)S(1)} %shard_map.84.pre) | copy-start | bytes 3538948
  20.1 1.0 %copy-start.1 = (bf16[3,3,128,128]{3,2,1,0:T(8,128)(2,1)S(1)}, bf16[3,3,128,128]{3,2,1,0:T(8,128)(2,1)}, u32[]{:S(2)}) copy-start(bf16[3,3,128,128]{3,2,1,0:T(8,128)(2,1)} %param.8) | copy-start | bytes 884740
  20.3 1.3 %copy-start.4 = (f32[8,288,128]{2,1,0:T(8,128)S(1)}, f32[8,288,128]{2,1,0:T(8,128)}, u32[]{:S(2)}) copy-start(f32[8,288,128]{2,1,0:T(8,128)} %copy-done.3) | copy-start | bytes 3538948
  30.3 0.7 copy-start.5
  31.0 2.2 %collective-permute-start.4 = (bf16[2304,128]{1,0:T(8,128)(2,1)}, bf16[2304,128]{1,0:T(8,128)(2,1)S(1)}, u32[]{:S(2)}, u32[]{:S(2)}) collective-permute-start(bf16[2304,128]{1,0:T(8,128)(2,1)} %get-tuple-element.33), channel_id=1, source_target_pairs={{0,16},{16,0},{1,17},{17,1},{2,18},{18,2},{3,19},{19,3},{4,20},{20... | collective-permute-start | bytes 1769480 | tf_op jit(solution)/shard_map/ppermute | solution.py:145
  31.0 5.9 %copy-start.6 = (bf16[4,288,128]{2,1,0:T(8,128)(2,1)S(1)}, bf16[4,288,128]{2,1,0:T(8,128)(2,1)}, u32[]{:S(2)}) copy-start(bf16[4,288,128]{2,1,0:T(8,128)(2,1)} %copy-done.5) | copy-start | bytes 884740
  33.3 7.7 %collective-permute-start.5 = (bf16[576,128]{1,0:T(8,128)(2,1)S(1)}, bf16[576,128]{1,0:T(8,128)(2,1)S(1)}, u32[]{:S(2)}, u32[]{:S(2)}) collective-permute-start(bf16[576,128]{1,0:T(8,128)(2,1)S(1)} %get-tuple-element.34), channel_id=1, source_target_pairs={{0,12},{4,8},{8,4},{12,0},{1,13},{5,9},{9,5},{13,1},{2,14},{6,10},... | collective-permute-start | bytes 442376 | tf_op jit(solution)/shard_map/ppermute | solution.py:89
  34.8 8.5 %collective-permute-start.6 = (bf16[576,128]{1,0:T(8,128)(2,1)S(1)}, bf16[576,128]{1,0:T(8,128)(2,1)S(1)}, u32[]{:S(2)}, u32[]{:S(2)}) collective-permute-start(bf16[576,128]{1,0:T(8,128)(2,1)S(1)} %get-tuple-element.35), channel_id=1, source_target_pairs={{0,8},{4,12},{8,0},{12,4},{1,9},{5,13},{9,1},{13,5},{2,10},{6,14},... | collective-permute-start | bytes 442376 | tf_op jit(solution)/shard_map/ppermute | solution.py:89
  35.5 7.9 %collective-permute-start.7 = (bf16[576,128]{1,0:T(8,128)(2,1)S(1)}, bf16[576,128]{1,0:T(8,128)(2,1)S(1)}, u32[]{:S(2)}, u32[]{:S(2)}) collective-permute-start(bf16[576,128]{1,0:T(8,128)(2,1)S(1)} %get-tuple-element.36), channel_id=1, source_target_pairs={{0,4},{4,0},{8,12},{12,8},{1,5},{5,1},{9,13},{13,9},{2,6},{6,2},{1... | collective-permute-start | bytes 442376 | tf_op jit(solution)/shard_map/ppermute | solution.py:89
  43.5 5.9 %collective-permute-start.10 = (bf16[144,128]{1,0:T(8,128)(2,1)S(1)}, bf16[144,128]{1,0:T(8,128)(2,1)S(1)}, u32[]{:S(2)}, u32[]{:S(2)}) collective-permute-start(bf16[144,128]{1,0:T(8,128)(2,1)S(1)} %get-tuple-element.61), channel_id=1, source_target_pairs={{0,3},{1,2},{2,1},{3,0},{4,7},{5,6},{6,5},{7,4},{8,11},{9,10},{10,... | collective-permute-start | bytes 110600 | tf_op jit(solution)/shard_map/ppermute | solution.py:151
  46.0 6.5 %collective-permute-start.9 = (bf16[144,128]{1,0:T(8,128)(2,1)S(1)}, bf16[144,128]{1,0:T(8,128)(2,1)S(1)}, u32[]{:S(2)}, u32[]{:S(2)}) collective-permute-start(bf16[144,128]{1,0:T(8,128)(2,1)S(1)} %get-tuple-element.62), channel_id=1, source_target_pairs={{0,2},{1,3},{2,0},{3,1},{4,6},{5,7},{6,4},{7,5},{8,10},{9,11},{10,... | collective-permute-start | bytes 110600 | tf_op jit(solution)/shard_map/ppermute | solution.py:151
  49.4 4.0 %collective-permute-start.8 = (bf16[144,128]{1,0:T(8,128)(2,1)S(1)}, bf16[144,128]{1,0:T(8,128)(2,1)S(1)}, u32[]{:S(2)}, u32[]{:S(2)}) collective-permute-start(bf16[144,128]{1,0:T(8,128)(2,1)S(1)} %get-tuple-element.60), channel_id=1, source_target_pairs={{0,1},{1,0},{2,3},{3,2},{4,5},{5,4},{6,7},{7,6},{8,9},{9,8},{10,11... | collective-permute-start | bytes 110600 | tf_op jit(solution)/shard_map/ppermute | solution.py:151
  53.4 5.8 %collective-permute-start.11 = (bf16[144,128]{1,0:T(8,128)(2,1)S(1)}, bf16[144,128]{1,0:T(8,128)(2,1)S(1)}, u32[]{:S(2)}, u32[]{:S(2)}) collective-permute-start(bf16[144,128]{1,0:T(8,128)(2,1)S(1)} %get-tuple-element.55), channel_id=1, source_target_pairs={{0,3},{1,2},{2,1},{3,0},{4,7},{5,6},{6,5},{7,4},{8,11},{9,10},{10,... | collective-permute-start | bytes 110600 | tf_op jit(solution)/shard_map/ppermute | solution.py:102
  54.6 5.6 %collective-permute-start.12 = (bf16[144,128]{1,0:T(8,128)(2,1)S(1)}, bf16[144,128]{1,0:T(8,128)(2,1)S(1)}, u32[]{:S(2)}, u32[]{:S(2)}) collective-permute-start(bf16[144,128]{1,0:T(8,128)(2,1)S(1)} %get-tuple-element.55), channel_id=1, source_target_pairs={{0,2},{1,3},{2,0},{3,1},{4,6},{5,7},{6,4},{7,5},{8,10},{9,11},{10,... | collective-permute-start | bytes 110600 | tf_op jit(solution)/shard_map/ppermute | solution.py:102
  55.4 4.8 %collective-permute-start.13 = (bf16[144,128]{1,0:T(8,128)(2,1)S(1)}, bf16[144,128]{1,0:T(8,128)(2,1)S(1)}, u32[]{:S(2)}, u32[]{:S(2)}) collective-permute-start(bf16[144,128]{1,0:T(8,128)(2,1)S(1)} %get-tuple-element.55), channel_id=1, source_target_pairs={{0,1},{1,0},{2,3},{3,2},{4,5},{5,4},{6,7},{7,6},{8,9},{9,8},{10,11... | collective-permute-start | bytes 110600 | tf_op jit(solution)/shard_map/ppermute | solution.py:102
  60.2 6.2 %collective-permute-start.14 = (bf16[576,128]{1,0:T(8,128)(2,1)S(1)}, bf16[576,128]{1,0:T(8,128)(2,1)S(1)}, u32[]{:S(2)}, u32[]{:S(2)}) collective-permute-start(bf16[576,128]{1,0:T(8,128)(2,1)S(1)} %constant_dynamic-update-slice_fusion.4), channel_id=1, source_target_pairs={{0,12},{4,8},{8,4},{12,0},{1,13},{5,9},{9,5},{13,1},{2,14},{6,10},... | collective-permute-start | bytes 442376 | tf_op jit(solution)/shard_map/ppermute | solution.py:102
  61.7 6.2 %collective-permute-start.15 = (bf16[576,128]{1,0:T(8,128)(2,1)S(1)}, bf16[576,128]{1,0:T(8,128)(2,1)S(1)}, u32[]{:S(2)}, u32[]{:S(2)}) collective-permute-start(bf16[576,128]{1,0:T(8,128)(2,1)S(1)} %constant_dynamic-update-slice_fusion.4), channel_id=1, source_target_pairs={{0,8},{4,12},{8,0},{12,4},{1,9},{5,13},{9,1},{13,5},{2,10},{6,14},... | collective-permute-start | bytes 442376 | tf_op jit(solution)/shard_map/ppermute | solution.py:102
  62.3 5.6 %collective-permute-start.16 = (bf16[576,128]{1,0:T(8,128)(2,1)S(1)}, bf16[576,128]{1,0:T(8,128)(2,1)S(1)}, u32[]{:S(2)}, u32[]{:S(2)}) collective-permute-start(bf16[576,128]{1,0:T(8,128)(2,1)S(1)} %constant_dynamic-update-slice_fusion.4), channel_id=1, source_target_pairs={{0,4},{4,0},{8,12},{12,8},{1,5},{5,1},{9,13},{13,9},{2,6},{6,2},{1... | collective-permute-start | bytes 442376 | tf_op jit(solution)/shard_map/ppermute | solution.py:102
  67.9 2.1 %collective-permute-start.17 = (bf16[2304,128]{1,0:T(8,128)(2,1)S(1)}, bf16[2304,128]{1,0:T(8,128)(2,1)S(1)}, u32[]{:S(2)}, u32[]{:S(2)}) collective-permute-start(bf16[2304,128]{1,0:T(8,128)(2,1)S(1)} %constant_dynamic-update-slice_fusion.half), channel_id=1, source_target_pairs={{0,16},{16,0},{1,17},{17,1},{2,18},{18,2},{3,19},{19,3},{4,20},{20... | collective-permute-start | bytes 1769480 | tf_op jit(solution)/shard_map/ppermute | solution.py:154
